TPU v7x, 512 devices: a whole 4x4x16 slice. The times are simulated.
512 devices in a mesh: tm: 128 (over y, x_hi, z), col: 4 (over x_lo, core).
Axes of the slice: x: 4 (x_hi: 2, x_lo: 2; x = x_hi * 2 + x_lo), y: 4, z: 16, core: 2. Of those that a mesh axis runs over, the one named last changes fastest.
Arguments:
- frames: bfloat16 [384, 2, 96, 384], P('tm', None, 'col'), may hold values from -6 to 6
- up_kernel: bfloat16 [10368, 256], P(None, 'tm'), may hold values from -0.109375 to 0.109375
- mix_kernel: bfloat16 [6912, 256], P(None, 'tm'), may hold values from -0.078125 to 0.078125
- cotangent: bfloat16 [768, 2, 96, 256], P('tm', None, 'col'), may hold values from -6 to 6
Outputs:
- decoded: bfloat16 [768, 2, 96, 256], P('tm', None, 'col')
- frames_grad: bfloat16 [384, 2, 96, 384], P('tm', None, 'col')
All inputs are finite; a program needn't handle non-finite values.
Results may differ from a plain program's by a relative error of at most 0.005.
Values may be sent and summed in bfloat16 or wider, within the bound.
No kernel may reach another device: no remote copies, remote signals or barrier semaphores. Data moves between devices by JAX's collectives and lax.ppermute only.
A program may use at most 64 MiB of HBM per device.

v0:
```python
import functools

import jax
import jax.numpy as jnp
from jax import lax
from jax.experimental import pallas as pl
from jax.experimental.pallas import tpu as pltpu
from jax.sharding import Mesh, PartitionSpec as P

PLANES = ("y", "xh", "z")
COLS = ("xl", "core")
RING = ("xh", "xl")
LANES = 128
PAD = 32


def shift(array, axis, by):
    devices = lax.axis_size(axis)
    pairs = [(i, i + by) for i in range(devices) if 0 <= i + by < devices]
    return lax.ppermute(array, axis, pairs)


def swap(array):
    return lax.ppermute(array, "core", [(0, 1), (1, 0)])


def spread(array, axis):
    count = lax.axis_size(axis)
    return lax.all_to_all(
        jnp.broadcast_to(array, (count, *array.shape)), axis, 0, 0, tiled=True
    )


def later(rows, by):
    if by == 0:
        return rows
    return pltpu.roll(rows, rows.shape[0] - by, 0)


def call(kernel, outs, scratch, flops, *operands):
    space = pl.BlockSpec(memory_space=pltpu.VMEM)
    return pl.pallas_call(
        kernel,
        out_shape=outs,
        in_specs=[space] * len(operands),
        out_specs=jax.tree.map(lambda _: space, outs),
        scratch_shapes=scratch,
        compiler_params=pltpu.CompilerParams(vmem_limit_bytes=48 * 2**20),
        cost_estimate=pl.CostEstimate(flops=flops, bytes_accessed=8 * 2**20, transcendentals=0),
    )(*operands)


def unfold_kernel(sizes, inputs, frame_rows, cot_rows):
    blocks, base = inputs.shape[0], 0
    for out, (times, splits) in zip((frame_rows, cot_rows), sizes, strict=True):

        def step(at, _, out=out, splits=splits, base=base):
            time, block = at // blocks, at % blocks
            target = pl.ds(pl.multiple_of(at * PAD, PAD), PAD)
            for row in range(2):
                for split in range(splits):
                    first = base + ((time * 2 + row) * splits + split) * PAD
                    source = pl.ds(pl.multiple_of(first, PAD), PAD)
                    chunk = inputs[block, source, :].astype(jnp.float32)
                    for tap in range(3):
                        lane = ((row * 3 + tap) * splits + split) * LANES
                        moved = later(chunk, tap).astype(jnp.bfloat16)
                        out[target, lane : lane + LANES] = moved
            return 0

        lax.fori_loop(0, times * blocks, step, 0)
        base += times * 2 * splits * PAD


def readers(layout, first, own, other):
    nz, up_half, up_count, up_size = layout
    lead = first[0] == 0

    def low(start, count):
        rows = slice(start, start + count)
        return jnp.where(lead, own[:, rows], other[:, rows])

    def high(start, count):
        rows = slice(start, start + count)
        return jnp.where(lead, other[:, rows], own[:, rows])

    def up_tile(kt, kh, kw, split, splits):
        tile = ((kt * 3 + kh) * 3 + kw) * splits + split
        if tile < up_half:
            value = low(tile * nz, nz)
        else:
            value = high((tile - (up_count - up_half)) * nz, nz)
        return value.reshape(-1, LANES)

    def mix_tile(kt, kw, pair):
        start = up_size + ((kt * 3 + kw) * 2 + pair) * 2 * nz
        return jnp.stack((low(start, 2 * nz), high(start, 2 * nz)), axis=1).reshape(-1, LANES)

    return up_tile, mix_tile


def forward_kernel(
    layout, first, rows, own, other, mask, decoded, slope, up_w, ups, hidden, mix_w, total
):
    up_tile, mix_tile = readers(layout, first, own, other)
    splits = rows.shape[1] // (6 * LANES)
    part, unit = up_w.shape[0] // 6, mask.shape[0]
    for kt in range(3):
        for out_row in range(2):
            for row in range(2):
                for kw in range(3):
                    for split in range(splits):
                        at = kt * 2 * part + out_row * part
                        lane = ((row * 3 + kw) * splits + split) * LANES
                        up_w[at : at + part, lane : lane + LANES] = up_tile(
                            kt, row - out_row + 1, kw, split, splits
                        )
    step = 2 * LANES
    ups[...] = jnp.zeros_like(ups)

    def product(k, _):
        lanes = pl.ds(pl.multiple_of(k * step, step), step)
        ups[...] += lax.dot_general(
            rows[:, lanes],
            up_w[:, lanes],
            (((1,), (1,)), ((), ())),
            preferred_element_type=jnp.float32,
        )
        return 0

    lax.fori_loop(0, rows.shape[1] // step, product, 0)
    inside = mask[...] > 0
    times = 2 * (rows.shape[0] // unit - 1) - 1
    for time in range(times):
        at = time // 2 * unit
        if time % 2 == 0:
            before = ups[at + unit : at + 2 * unit, :LANES] + ups[at : at + unit, 2 * LANES :]
        else:
            before = ups[at + unit : at + 2 * unit, LANES : 2 * LANES]
        sigma = jax.nn.sigmoid(before)
        if time < times - 1:
            value = jnp.where(inside, before * sigma, 0.0)
            for kw in range(3):
                hidden[time * unit : (time + 1) * unit, kw * LANES : (kw + 1) * LANES] = later(
                    value, kw
                ).astype(jnp.bfloat16)
        if time >= 2:
            slope[(time - 2) * unit : (time - 1) * unit, :] = jnp.where(
                inside, sigma * (1.0 + before * (1.0 - sigma)), 0.0
            )
    channels = mix_w.shape[0] // 2
    for kt in range(3):
        for out_row in range(2):
            for kw in range(3):
                mix_w[
                    out_row * channels : (out_row + 1) * channels,
                    (kt * 3 + kw) * LANES : (kt * 3 + kw + 1) * LANES,
                ] = mix_tile(kt, kw, out_row)
    total[...] = jnp.zeros_like(total)
    for kt in range(3):
        total[...] += lax.dot_general(
            hidden[kt * unit : kt * unit + total.shape[0], :],
            mix_w[:, kt * 3 * LANES : (kt + 1) * 3 * LANES],
            (((1,), (1,)), ((), ())),
            preferred_element_type=jnp.float32,
        )
    store(decoded, total, channels)


def store(out, total, channels):
    blocks, times, _, width, _ = out.shape
    for block in range(blocks):
        for time in range(times):
            at = (time * blocks + block) * PAD
            for out_row in range(2):
                lanes = slice(out_row * channels, (out_row + 1) * channels)
                value = total[at : at + PAD, lanes].astype(jnp.bfloat16)
                out[block, time, out_row] = value[:width]


def backward_kernel(
    layout, first, rows, own, other, slope, grads, mix_w, partial, evens, odds, up_w, total
):
    up_tile, mix_tile = readers(layout, first, own, other)
    channels = rows.shape[1] // 6
    unit = evens.shape[0] - total.shape[0]
    splits = up_w.shape[1] // (2 * LANES)
    part = LANES // 2
    for kt in range(3):
        for row in range(2):
            for shift_w in range(3):
                at = (row * 3 + shift_w) * channels
                mix_w[at : at + channels, kt * LANES : (kt + 1) * LANES] = mix_tile(
                    kt, 2 - shift_w, row
                )
    step = 2 * LANES
    partial[...] = jnp.zeros_like(partial)

    def product(k, _):
        lanes = pl.ds(pl.multiple_of(k * step, step), step)
        partial[...] += jnp.dot(
            rows[:, lanes], mix_w[lanes, :], preferred_element_type=jnp.float32
        )
        return 0

    lax.fori_loop(0, rows.shape[1] // step, product, 0)
    times = rows.shape[0] // unit - 2
    for time in range(times):
        at = time * unit
        hidden_grad = (
            partial[at + 2 * unit : at + 3 * unit, :LANES]
            + partial[at + unit : at + 2 * unit, LANES : 2 * LANES]
            + partial[at : at + unit, 2 * LANES :]
        )
        value = hidden_grad * slope[at : at + unit, :]
        target = evens if time % 2 == 0 else odds
        place = time // 2 * unit
        for shift_w in range(3):
            target[place : place + unit, shift_w * LANES : (shift_w + 1) * LANES] = later(
                value, shift_w
            ).astype(jnp.bfloat16)
    for kt in range(3):
        for shift_w in range(3):
            for row in range(2):
                for out_row in range(2):
                    for split in range(splits):
                        at = (kt * 3 + shift_w) * LANES + row * part
                        lane = (out_row * splits + split) * LANES
                        up_w[at : at + part, lane : lane + LANES] = up_tile(
                            kt, out_row + 1 - row, 2 - shift_w, split, splits
                        )
    count = total.shape[0]
    lhs = (evens[:count, :], odds[:count, :], evens[unit : unit + count, :])
    total[...] = jnp.zeros_like(total)
    for kt in range(3):
        total[...] += jnp.dot(
            lhs[kt],
            up_w[kt * 3 * LANES : (kt + 1) * 3 * LANES, :],
            preferred_element_type=jnp.float32,
        )
    store(grads, total, splits * LANES)


def unfold(inputs, frame_times, cot_times, frame_splits, cot_splits):
    unit = inputs.shape[0] * PAD
    sizes = ((frame_times, frame_splits), (cot_times, cot_splits))
    outs = tuple(
        jax.ShapeDtypeStruct((times * unit, 6 * splits * LANES), jnp.bfloat16)
        for times, splits in sizes
    )
    return call(functools.partial(unfold_kernel, sizes), outs, [], 10**6, inputs)


def forward(layout, first, rows, own, other, mask, width, channels):
    blocks = mask.shape[0] // PAD
    unit = mask.shape[0]
    times = 2 * (rows.shape[0] // unit - 3)
    outs = (
        jax.ShapeDtypeStruct((blocks, times, 2, width, channels), jnp.bfloat16),
        jax.ShapeDtypeStruct(((times + 1) * unit, LANES), jnp.float32),
    )
    scratch = [
        pltpu.VMEM((3 * LANES, rows.shape[1]), jnp.bfloat16),
        pltpu.VMEM((rows.shape[0], 3 * LANES), jnp.float32),
        pltpu.VMEM(((times + 2) * unit, 3 * LANES), jnp.bfloat16),
        pltpu.VMEM((2 * channels, 9 * LANES), jnp.bfloat16),
        pltpu.VMEM((times * unit, 2 * channels), jnp.float32),
    ]
    kernel = functools.partial(forward_kernel, layout)
    return call_scalar(kernel, outs, scratch, 2 * 10**9, first, rows, own, other, mask)


def backward(layout, first, rows, own, other, slope, unit, width, in_channels):
    times = slope.shape[0] // unit
    out = jax.ShapeDtypeStruct((unit // PAD, times // 2, 2, width, in_channels), jnp.bfloat16)
    scratch = [
        pltpu.VMEM((rows.shape[1], 3 * LANES), jnp.bfloat16),
        pltpu.VMEM((rows.shape[0], 3 * LANES), jnp.float32),
        pltpu.VMEM(((times + 1) // 2 * unit, 3 * LANES), jnp.bfloat16),
        pltpu.VMEM((times // 2 * unit, 3 * LANES), jnp.bfloat16),
        pltpu.VMEM((9 * LANES, 2 * in_channels), jnp.bfloat16),
        pltpu.VMEM((times // 2 * unit, 2 * in_channels), jnp.float32),
    ]
    kernel = functools.partial(backward_kernel, layout)
    return call_scalar(kernel, out, scratch, 2 * 10**9, first, rows, own, other, slope)


def call_scalar(kernel, outs, scratch, flops, first, *operands):
    space = pl.BlockSpec(memory_space=pltpu.VMEM)
    return pl.pallas_call(
        kernel,
        out_shape=outs,
        in_specs=[pl.BlockSpec(memory_space=pltpu.SMEM)] + [space] * len(operands),
        out_specs=jax.tree.map(lambda _: space, outs),
        scratch_shapes=scratch,
        compiler_params=pltpu.CompilerParams(vmem_limit_bytes=48 * 2**20),
        cost_estimate=pl.CostEstimate(flops=flops, bytes_accessed=8 * 2**20, transcendentals=0),
    )(first, *operands)


def with_columns(field):
    width = field.shape[2]
    low = shift(field[:, :, width - 2 :], COLS, 1)
    high = shift(field[:, :, :2], COLS, -1)
    return jnp.concatenate((low, field, high), axis=2)


def flat(field):
    padded = jnp.pad(field, ((0, 0), (0, 0), (0, PAD - field.shape[2]), (0, 0)))
    tiles = padded.reshape(*padded.shape[:3], -1, LANES)
    return tiles.transpose(0, 1, 3, 2, 4).reshape(-1, LANES)


def tiles_of(kernel):
    return kernel.T.reshape(2, -1, LANES).transpose(1, 0, 2)


def shards(frames, up_kernel, mix_kernel, cotangent):
    frame_count, height, width, in_channels = frames.shape
    out_channels = mix_kernel.shape[0] // 27
    xh, xl, core = lax.axis_index("xh"), lax.axis_index("xl"), lax.axis_index("core")
    ny, nz, nx = lax.axis_size("y"), lax.axis_size("z"), lax.axis_size(RING)
    part = out_channels // nx

    raw_mix = tiles_of(mix_kernel)
    mix_other = lax.ppermute(raw_mix, RING, [(0, 3), (3, 0), (1, 2), (2, 1)])
    up_column = lax.dynamic_index_in_dim(up_kernel.T, xl, 0, keepdims=False)
    up_tiles = up_column.reshape(-1, LANES)
    up_count = up_tiles.shape[0]
    up_half = (up_count + 1) // 2
    up_part = lax.dynamic_slice_in_dim(up_tiles, core * (up_count - up_half), up_half, 0)
    up_pairs = (up_half + 1) // 2
    up_part = jnp.pad(up_part, ((0, 2 * up_pairs - up_half), (0, 0))).reshape(-1, 2, LANES)

    mix_tiles = jnp.where(xh == core, raw_mix, mix_other)
    splits = out_channels // LANES
    pick_shape = (3, out_channels, 4 * part)
    tap = lax.broadcasted_iota(jnp.int32, pick_shape, 0)
    source = lax.broadcasted_iota(jnp.int32, pick_shape, 1)
    target = lax.broadcasted_iota(jnp.int32, pick_shape, 2)
    pair, side, place = target // (2 * part), target // part % 2, target % part
    wanted = (place // nz) * (4 * nz) + xh * (2 * nz) + (place % nz) * 2 + xl
    pick = (source == wanted) & (tap == side + 1 - pair)
    mix_part = jnp.einsum(
        "thwsjl,hslm->twjm",
        mix_tiles.reshape(3, 3, 3, splits, 2, LANES),
        pick.astype(jnp.bfloat16).reshape(3, splits, LANES, 4 * part),
        preferred_element_type=jnp.float32,
    ).astype(jnp.bfloat16)
    mix_part = mix_part.reshape(9, 2, 2, 2 * part).transpose(0, 2, 1, 3).reshape(-1, 2, LANES)

    planes = spread(jnp.concatenate((up_part, mix_part), axis=0), "z")
    wide_frames, wide_cot = with_columns(frames), with_columns(cotangent)
    fields = jnp.concatenate(
        (shift(wide_frames[-2:], PLANES, 1), wide_frames, shift(wide_frames[:1], PLANES, -1)),
        axis=0,
    )
    cots = jnp.concatenate((wide_cot, shift(wide_cot[:3], PLANES, -1)), axis=0)
    planes, fields, cots = lax.optimization_barrier((planes, fields, cots))
    inputs = jnp.concatenate((flat(fields), flat(cots)), axis=0)
    inputs = lax.all_gather(inputs, RING, axis=0)

    up_rows = planes[:, :up_pairs].transpose(1, 2, 0, 3).reshape(-1, LANES)
    mix_rows = planes[:, up_pairs:].transpose(1, 0, 2, 3).reshape(-1, LANES)
    own = spread(jnp.concatenate((up_rows, mix_rows), axis=0), "y")
    other = swap(own)
    layout = (nz, up_half, up_count, up_rows.shape[0])

    frame_rows, cot_rows = unfold(
        inputs, fields.shape[0], cots.shape[0], in_channels // LANES, splits
    )
    columns = lax.axis_size(COLS) * width
    firsts = (2 * (jnp.arange(nx) % 2) + core) * width - 1
    at = firsts[:, None] + jnp.arange(PAD)
    inside = ((at >= 0) & (at < columns)).astype(jnp.float32).reshape(-1, 1)
    mask = jnp.broadcast_to(inside, (nx * PAD, LANES))
    first = core.reshape(1)

    decoded_parts, slope = forward(
        layout, first, frame_rows, own, other, mask, width, out_channels
    )
    decoded_parts = lax.all_to_all(decoded_parts, RING, 0, 0, tiled=True)
    grad_parts = backward(
        layout, first, cot_rows, own, other, slope, nx * PAD, width, in_channels
    )
    grad_parts = lax.all_to_all(grad_parts, RING, 0, 0, tiled=True)
    decoded = jnp.sum(decoded_parts.astype(jnp.float32), axis=0)
    frames_grad = jnp.sum(grad_parts.astype(jnp.float32), axis=0)
    return decoded.astype(jnp.bfloat16), frames_grad.astype(jnp.bfloat16)


def solution(mesh):
    planes, columns = mesh.devices.shape
    shape = (4, 2, planes // 8, 2, columns // 2)
    fine = Mesh(mesh.devices.reshape(shape), (*PLANES, *COLS))
    placed = P(PLANES, None, COLS, None)
    weights = P(None, PLANES)
    return jax.shard_map(
        shards,
        mesh=fine,
        in_specs=(placed, weights, weights, placed),
        out_specs=(placed, placed),
        check_vma=False,
    )
```

profile of v0, /device:TPU:1, one launch (start us, length us, event | category | flops | bytes accessed | tf_op | source)
XLA Modules:
  0.0 151.6 jit_solution(13546170506301319183)
XLA Ops:
  7.2 0.0 copy-start
  7.2 0.8 reshape.91
  8.0 5.2 %collective-permute-start = (bf16[54,2,128]{2,0,1:T(8,128)(2,1)S(1)}, bf16[54,2,128]{2,0,1:T(8,128)(2,1)S(1)}, u32[]{:S(2)}, u32[]{:S(2)}) collective-permute-start(bf16[54,2,128]{2,0,1:T(8,128)(2,1)S(1)} %bitcast.44), channel_id=1, source_target_pairs={{0,66},{66,0},{2,64},{64,2},{1,67},{67,1},{3,65},{65,3},{4,70},{70... | collective-permute-start | bytes 82952 | tf_op jit(solution)/shard_map/ppermute | solution.py:326
  13.3 0.1 dynamic-slice_reduce_fusion
  13.5 0.9 collective-permute-done
  14.5 0.0 copy-start.3
  14.5 0.0 copy-start.4
  14.5 0.3 fusion
  14.9 0.9 broadcast_in_dim.6
  15.8 15.1 %all-to-all-start = ((bf16[16,39,2,128]{3,2,1,0:T(2,128)(2,1)}), bf16[16,39,2,128]{3,2,1,0:T(2,128)(2,1)S(1)}, u32[]{:S(2)}, u32[]{:S(2)}) async-start(bf16[16,39,2,128]{3,2,1,0:T(2,128)(2,1)} %broadcast_in_dim.6), calls=%async_computation | async-start | bytes 638976 | tf_op jit(solution)/shard_map/all_to_all | solution.py:29
  30.9 0.0 all-gather.3.cloned.1.call-start
  31.0 3.9 %collective-permute-start.1 = (bf16[3,2,2,384]{3,2,1,0:T(2,128)(2,1)S(1)}, bf16[3,2,2,384]{3,2,1,0:T(2,128)(2,1)S(1)}, u32[]{:S(2)}, u32[]{:S(2)}) collective-permute-start(bf16[3,2,2,384]{3,2,1,0:T(2,128)(2,1)S(1)} %get-tuple-element.18), channel_id=1, source_target_pairs={{0,1},{1,2},{2,3},{4,5},{5,6},{6,7},{8,9},{9,10},{10,11},{12,13},{... | collective-permute-start | bytes 27656 | tf_op jit(solution)/shard_map/ppermute | solution.py:20
  34.9 1.9 %collective-permute-start.2 = (bf16[3,2,2,384]{3,2,1,0:T(2,128)(2,1)S(1)}, bf16[3,2,2,384]{3,2,1,0:T(2,128)(2,1)S(1)}, u32[]{:S(2)}, u32[]{:S(2)}) collective-permute-start(bf16[3,2,2,384]{3,2,1,0:T(2,128)(2,1)S(1)} %get-tuple-element.19), channel_id=1, source_target_pairs={{1,0},{2,1},{3,2},{5,4},{6,5},{7,6},{9,8},{10,9},{11,10},{13,12},{... | collective-permute-start | bytes 27656 | tf_op jit(solution)/shard_map/ppermute | solution.py:20
  36.9 3.6 %collective-permute-start.5 = (bf16[6,2,2,256]{3,2,1,0:T(2,128)(2,1)S(1)}, bf16[6,2,2,256]{3,2,1,0:T(2,128)(2,1)S(1)}, u32[]{:S(2)}, u32[]{:S(2)}) collective-permute-start(bf16[6,2,2,256]{3,2,1,0:T(2,128)(2,1)S(1)} %get-tuple-element.16), channel_id=1, source_target_pairs={{0,1},{1,2},{2,3},{4,5},{5,6},{6,7},{8,9},{9,10},{10,11},{12,13},{... | collective-permute-start | bytes 36872 | tf_op jit(solution)/shard_map/ppermute | solution.py:20
  40.6 1.9 %collective-permute-start.6 = (bf16[6,2,2,256]{3,2,1,0:T(2,128)(2,1)S(1)}, bf16[6,2,2,256]{3,2,1,0:T(2,128)(2,1)S(1)}, u32[]{:S(2)}, u32[]{:S(2)}) collective-permute-start(bf16[6,2,2,256]{3,2,1,0:T(2,128)(2,1)S(1)} %get-tuple-element.17), channel_id=1, source_target_pairs={{1,0},{2,1},{3,2},{5,4},{6,5},{7,6},{9,8},{10,9},{11,10},{13,12},{... | collective-permute-start | bytes 36872 | tf_op jit(solution)/shard_map/ppermute | solution.py:20
  42.5 0.0 collective-permute-done.1
  42.5 0.1 pad_maximum_fusion.4
  42.6 3.6 %collective-permute-start.3 = (bf16[2,2,28,384]{3,2,1,0:T(8,128)(2,1)S(1)}, bf16[2,2,28,384]{3,2,1,0:T(8,128)(2,1)S(1)}, u32[]{:S(2)}, u32[]{:S(2)}) collective-permute-start(bf16[2,2,28,384]{3,2,1,0:T(8,128)(2,1)S(1)} %slice.36), channel_id=1, source_target_pairs={{0,4},{4,8},{8,12},{12,16},{16,20},{20,24},{24,28},{28,32},{32,36}... | collective-permute-start | bytes 258056 | tf_op jit(solution)/shard_map/ppermute | solution.py:20
  46.2 1.3 collective-permute-start.4
  47.5 1.3 collective-permute-start.7
  48.8 2.5 %collective-permute-done.4 = bf16[1,2,28,384]{3,2,1,0:T(8,128)(2,1)S(1)} collective-permute-done((bf16[1,2,28,384]{3,2,1,0:T(8,128)(2,1)S(1)}, bf16[1,2,28,384]{3,2,1,0:T(8,128)(2,1)S(1)}, u32[]{:S(2)}, u32[]{:S(2)}) %collective-permute-start.4) | collective-permute-done | bytes 43040 | tf_op jit(solution)/shard_map/ppermute | solution.py:20
  51.3 0.1 pad_maximum_fusion.2
  51.4 2.2 %collective-permute-done.7 = bf16[3,2,28,256]{3,2,1,0:T(8,128)(2,1)S(1)} collective-permute-done((bf16[3,2,28,256]{3,2,1,0:T(8,128)(2,1)S(1)}, bf16[3,2,28,256]{3,2,1,0:T(8,128)(2,1)S(1)}, u32[]{:S(2)}, u32[]{:S(2)}) %collective-permute-start.7) | collective-permute-done | bytes 86048 | tf_op jit(solution)/shard_map/ppermute | solution.py:20
  53.5 0.1 pad_maximum_fusion.3
  53.7 0.1 reshape.95
  53.8 0.1 copy.31
  53.8 0.1 copy_bitcast_fusion
  53.9 0.9 pad_maximum_fusion
  54.7 0.0 all-gather.3.cloned.1.call-update
  54.8 0.1 slice_bitcast_fusion
  55.0 0.1 copy.34
  55.1 0.2 broadcast_in_dim.14
  55.3 26.1 %all_to_all.20.own = bf16[4,1248,128]{2,1,0:T(8,128)(2,1)S(1)} all-to-all(bf16[4,1248,128]{2,1,0:T(8,128)(2,1)S(1)} %broadcast_in_dim.14), channel_id=1, replica_groups=mesh['y'=4,'xh'=2,'z'=16,'xl'=2,'core'=2] {'y'}, dimensions={0} | all-to-all | bytes 2555904 | tf_op jit(solution)/shard_map/all_to_all | solution.py:29
  81.4 2.9 %collective-permute-start.8 = (bf16[4,1248,128]{2,1,0:T(8,128)(2,1)S(1)}, bf16[4,1248,128]{2,1,0:T(8,128)(2,1)S(1)}, u32[]{:S(2)}, u32[]{:S(2)}) collective-permute-start(bf16[4,1248,128]{2,1,0:T(8,128)(2,1)S(1)} %all_to_all.20.own), channel_id=1, source_target_pairs={{0,1},{1,0},{2,3},{3,2},{4,5},{5,4},{6,7},{7,6},{8,9},{9,8},{10,11... | collective-permute-start | bytes 3833864 | tf_op jit(solution)/shard_map/ppermute | solution.py:24
  84.3 0.1 fusion.42
  84.4 0.1 reshape.101
  84.4 16.1 %all-gather.3.cloned.1.call-done = bf16[9216,128]{1,0:T(8,128)(2,1)} async-done(((bf16[2304,128]{1,0:T(8,128)(2,1)}), bf16[9216,128]{1,0:T(8,128)(2,1)}) %all-gather.3.cloned.1.call-update) | async-done | bytes 2359312 | tf_op jit(solution)/shard_map/all_gather | solution.py:361
  100.5 1.7 %copy-done.1 = bf16[9216,128]{1,0:T(8,128)(2,1)S(1)} copy-done((bf16[9216,128]{1,0:T(8,128)(2,1)S(1)}, bf16[9216,128]{1,0:T(8,128)(2,1)}, u32[]{:S(2)}) %copy-start.1) | copy-done | bytes 2359320
  102.2 3.7 %shard_map.59 = (bf16[768,2304]{1,0:T(8,128)(2,1)S(1)}, bf16[1152,1536]{1,0:T(8,128)(2,1)}) custom-call(bf16[4,2304,128]{2,1,0:T(8,128)(2,1)S(1)} %bitcast.38), custom_call_target="tpu_custom_call" | custom-call | flops 1000000 | bytes 8388608 | tf_op jit(solution)/shard_map/pallas_call | solution.py:42
  105.9 1.8 %copy-done.2 = bf16[768,2304]{1,0:T(8,128)(2,1)} copy-done((bf16[768,2304]{1,0:T(8,128)(2,1)}, bf16[768,2304]{1,0:T(8,128)(2,1)S(1)}, u32[]{:S(2)}) %copy-start.2) | copy-done | bytes 3538968
  107.7 0.1 broadcast_in_dim.15.mask
  107.8 8.5 %shard_map.60 = (bf16[4,6,2,24,256]{4,3,2,1,0:T(8,128)(2,1)}, f32[896,128]{1,0:T(8,128)S(1)}) custom-call(s32[1]{0:T(128)} %bitcast.first, bf16[768,2304]{1,0:T(8,128)(2,1)} %copy-done.2, bf16[4,1248,128]{2,1,0:T(8,128)(2,1)S(1)} %all_to_all.20.own, bf16[4,1248,128]{2,1,0:T(8,128)(2,1)S(1)} %collective-permute-done.8.other, f32[128,128]{1,0:T(8,128)S(1)} %broadcast_in_dim.15.mask), custom_call_target="tpu_custom_call" | custom-call | flops 2000000000 | bytes 8388608 | tf_op jit(solution)/shard_map/pallas_call | solution.py:290
  116.3 6.5 %shard_map.61 = bf16[4,3,2,24,384]{4,3,2,1,0:T(8,128)(2,1)S(1)} custom-call(s32[1]{0:T(128)} %bitcast.first, bf16[1152,1536]{1,0:T(8,128)(2,1)} %get-tuple-element.14.rows, bf16[4,1248,128]{2,1,0:T(8,128)(2,1)S(1)} %all_to_all.20.own, bf16[4,1248,128]{2,1,0:T(8,128)(2,1)S(1)} %collective-permute-done.8.other, f32[896,128]{1,0:T(8,128)S(1)} %get-tuple-element.15.slope), custom_call_target="tpu_custom_call" | custom-call | flops 2000000000 | bytes 8388608 | tf_op jit(solution)/shard_map/pallas_call | solution.py:290
  122.8 10.0 %all_to_all.21 = bf16[4,3,2,24,384]{4,3,2,1,0:T(8,128)(2,1)S(1)} all-to-all(bf16[4,3,2,24,384]{4,3,2,1,0:T(8,128)(2,1)S(1)} %shard_map.61), channel_id=1, replica_groups=mesh['y'=4,'xh'=2,'z'=16,'xl'=2,'core'=2] {'xh','xl'}, dimensions={0} | all-to-all | bytes 884736 | tf_op jit(solution)/shard_map/all_to_all | solution.py:386
  132.8 3.5 %all-to-all-start.2 = ((bf16[4,6,2,24,256]{4,3,2,1,0:T(8,128)(2,1)}), bf16[4,6,2,24,256]{4,3,2,1,0:T(8,128)(2,1)S(1)}, u32[]{:S(2)}, u32[]{:S(2)}) async-start(bf16[4,6,2,24,256]{4,3,2,1,0:T(8,128)(2,1)} %get-tuple-element.13), calls=%async_computation.2 | async-start | bytes 1179648 | tf_op jit(solution)/shard_map/all_to_all | solution.py:382
  136.3 0.7 reduce_sum.25
  137.0 7.0 %all-to-all-done.2 = bf16[4,6,2,24,256]{4,3,2,1,0:T(8,128)(2,1)S(1)} async-done(((bf16[4,6,2,24,256]{4,3,2,1,0:T(8,128)(2,1)}), bf16[4,6,2,24,256]{4,3,2,1,0:T(8,128)(2,1)S(1)}, u32[]{:S(2)}, u32[]{:S(2)}) %all-to-all-start.2) | async-done | bytes 589856 | tf_op jit(solution)/shard_map/all_to_all | solution.py:382
  144.0 0.8 reduce_sum.24
  (36 shorter events, 0.4 us)
Async XLA Ops:
  7.2 6.1 %copy-start = (bf16[10368,2]{0,1:T(2,128)(2,1)S(1)}, bf16[10368,2]{0,1:T(2,128)(2,1)}, u32[]{:S(2)}) copy-start(bf16[10368,2]{0,1:T(2,128)(2,1)} %param.5) | copy-start | bytes 124420
  8.0 6.5 %collective-permute-start = (bf16[54,2,128]{2,0,1:T(8,128)(2,1)S(1)}, bf16[54,2,128]{2,0,1:T(8,128)(2,1)S(1)}, u32[]{:S(2)}, u32[]{:S(2)}) collective-permute-start(bf16[54,2,128]{2,0,1:T(8,128)(2,1)S(1)} %bitcast.44), channel_id=1, source_target_pairs={{0,66},{66,0},{2,64},{64,2},{1,67},{67,1},{3,65},{65,3},{4,70},{70... | collective-permute-start | bytes 82952 | tf_op jit(solution)/shard_map/ppermute | solution.py:326
  14.5 16.5 %copy-start.3 = (bf16[3,2,24,384]{3,2,1,0:T(8,128)(2,1)S(1)}, bf16[3,2,24,384]{3,2,1,0:T(8,128)(2,1)}, u32[]{:S(2)}) copy-start(bf16[3,2,24,384]{3,2,1,0:T(8,128)(2,1)} %param.4) | copy-start | bytes 331780
  14.5 22.4 %copy-start.4 = (bf16[6,2,24,256]{3,2,1,0:T(8,128)(2,1)S(1)}, bf16[6,2,24,256]{3,2,1,0:T(8,128)(2,1)}, u32[]{:S(2)}) copy-start(bf16[6,2,24,256]{3,2,1,0:T(8,128)(2,1)} %param.7) | copy-start | bytes 442372
  15.8 37.8 %all-to-all-start = ((bf16[16,39,2,128]{3,2,1,0:T(2,128)(2,1)}), bf16[16,39,2,128]{3,2,1,0:T(2,128)(2,1)S(1)}, u32[]{:S(2)}, u32[]{:S(2)}) async-start(bf16[16,39,2,128]{3,2,1,0:T(2,128)(2,1)} %broadcast_in_dim.6), calls=%async_computation | async-start | bytes 638976 | tf_op jit(solution)/shard_map/all_to_all | solution.py:29
  30.9 69.6 %all-gather.3.cloned.1.call-start = ((), (), s32[]{:S(2)}) async-start(), calls=%async_computation.4 | async-start | bytes 2949120 | tf_op jit(solution)/shard_map/all_gather | solution.py:361
  31.0 11.5 %collective-permute-start.1 = (bf16[3,2,2,384]{3,2,1,0:T(2,128)(2,1)S(1)}, bf16[3,2,2,384]{3,2,1,0:T(2,128)(2,1)S(1)}, u32[]{:S(2)}, u32[]{:S(2)}) collective-permute-start(bf16[3,2,2,384]{3,2,1,0:T(2,128)(2,1)S(1)} %get-tuple-element.18), channel_id=1, source_target_pairs={{0,1},{1,2},{2,3},{4,5},{5,6},{6,7},{8,9},{9,10},{10,11},{12,13},{... | collective-permute-start | bytes 27656 | tf_op jit(solution)/shard_map/ppermute | solution.py:20
  34.9 7.6 %collective-permute-start.2 = (bf16[3,2,2,384]{3,2,1,0:T(2,128)(2,1)S(1)}, bf16[3,2,2,384]{3,2,1,0:T(2,128)(2,1)S(1)}, u32[]{:S(2)}, u32[]{:S(2)}) collective-permute-start(bf16[3,2,2,384]{3,2,1,0:T(2,128)(2,1)S(1)} %get-tuple-element.19), channel_id=1, source_target_pairs={{1,0},{2,1},{3,2},{5,4},{6,5},{7,6},{9,8},{10,9},{11,10},{13,12},{... | collective-permute-start | bytes 27656 | tf_op jit(solution)/shard_map/ppermute | solution.py:20
  36.9 10.6 %collective-permute-start.5 = (bf16[6,2,2,256]{3,2,1,0:T(2,128)(2,1)S(1)}, bf16[6,2,2,256]{3,2,1,0:T(2,128)(2,1)S(1)}, u32[]{:S(2)}, u32[]{:S(2)}) collective-permute-start(bf16[6,2,2,256]{3,2,1,0:T(2,128)(2,1)S(1)} %get-tuple-element.16), channel_id=1, source_target_pairs={{0,1},{1,2},{2,3},{4,5},{5,6},{6,7},{8,9},{9,10},{10,11},{12,13},{... | collective-permute-start | bytes 36872 | tf_op jit(solution)/shard_map/ppermute | solution.py:20
  40.6 6.9 %collective-permute-start.6 = (bf16[6,2,2,256]{3,2,1,0:T(2,128)(2,1)S(1)}, bf16[6,2,2,256]{3,2,1,0:T(2,128)(2,1)S(1)}, u32[]{:S(2)}, u32[]{:S(2)}) collective-permute-start(bf16[6,2,2,256]{3,2,1,0:T(2,128)(2,1)S(1)} %get-tuple-element.17), channel_id=1, source_target_pairs={{1,0},{2,1},{3,2},{5,4},{6,5},{7,6},{9,8},{10,9},{11,10},{13,12},{... | collective-permute-start | bytes 36872 | tf_op jit(solution)/shard_map/ppermute | solution.py:20
  42.6 8.7 %collective-permute-start.3 = (bf16[2,2,28,384]{3,2,1,0:T(8,128)(2,1)S(1)}, bf16[2,2,28,384]{3,2,1,0:T(8,128)(2,1)S(1)}, u32[]{:S(2)}, u32[]{:S(2)}) collective-permute-start(bf16[2,2,28,384]{3,2,1,0:T(8,128)(2,1)S(1)} %slice.36), channel_id=1, source_target_pairs={{0,4},{4,8},{8,12},{12,16},{16,20},{20,24},{24,28},{28,32},{32,36}... | collective-permute-start | bytes 258056 | tf_op jit(solution)/shard_map/ppermute | solution.py:20
  46.2 5.1 %collective-permute-start.4 = (bf16[1,2,28,384]{3,2,1,0:T(8,128)(2,1)S(1)}, bf16[1,2,28,384]{3,2,1,0:T(8,128)(2,1)S(1)}, u32[]{:S(2)}, u32[]{:S(2)}) collective-permute-start(bf16[1,2,28,384]{3,2,1,0:T(8,128)(2,1)S(1)} %pad_maximum_fusion.7), channel_id=1, source_target_pairs={{4,0},{8,4},{12,8},{16,12},{20,16},{24,20},{28,24},{32,28},{36,32}... | collective-permute-start | bytes 129032 | tf_op jit(solution)/shard_map/ppermute | solution.py:20
  47.5 6.0 %collective-permute-start.7 = (bf16[3,2,28,256]{3,2,1,0:T(8,128)(2,1)S(1)}, bf16[3,2,28,256]{3,2,1,0:T(8,128)(2,1)S(1)}, u32[]{:S(2)}, u32[]{:S(2)}) collective-permute-start(bf16[3,2,28,256]{3,2,1,0:T(8,128)(2,1)S(1)} %pad_maximum_fusion.5), channel_id=1, source_target_pairs={{4,0},{8,4},{12,8},{16,12},{20,16},{24,20},{28,24},{32,28},{36,32}... | collective-permute-start | bytes 258056 | tf_op jit(solution)/shard_map/ppermute | solution.py:20
  81.4 26.3 %collective-permute-start.8 = (bf16[4,1248,128]{2,1,0:T(8,128)(2,1)S(1)}, bf16[4,1248,128]{2,1,0:T(8,128)(2,1)S(1)}, u32[]{:S(2)}, u32[]{:S(2)}) collective-permute-start(bf16[4,1248,128]{2,1,0:T(8,128)(2,1)S(1)} %all_to_all.20.own), channel_id=1, source_target_pairs={{0,1},{1,0},{2,3},{3,2},{4,5},{5,4},{6,7},{7,6},{8,9},{9,8},{10,11... | collective-permute-start | bytes 3833864 | tf_op jit(solution)/shard_map/ppermute | solution.py:24
  100.5 1.7 %copy-start.1 = (bf16[9216,128]{1,0:T(8,128)(2,1)S(1)}, bf16[9216,128]{1,0:T(8,128)(2,1)}, u32[]{:S(2)}) copy-start(bf16[9216,128]{1,0:T(8,128)(2,1)} %all-gather.3.cloned.1.call-done) | copy-start | bytes 7077892
  105.9 1.8 %copy-start.2 = (bf16[768,2304]{1,0:T(8,128)(2,1)}, bf16[768,2304]{1,0:T(8,128)(2,1)S(1)}, u32[]{:S(2)}) copy-start(bf16[768,2304]{1,0:T(8,128)(2,1)S(1)} %get-tuple-element.11.rows) | copy-start | bytes 10616836
  132.8 11.2 %all-to-all-start.2 = ((bf16[4,6,2,24,256]{4,3,2,1,0:T(8,128)(2,1)}), bf16[4,6,2,24,256]{4,3,2,1,0:T(8,128)(2,1)S(1)}, u32[]{:S(2)}, u32[]{:S(2)}) async-start(bf16[4,6,2,24,256]{4,3,2,1,0:T(8,128)(2,1)} %get-tuple-element.13), calls=%async_computation.2 | async-start | bytes 1179648 | tf_op jit(solution)/shard_map/all_to_all | solution.py:382
Sparse Core Ops, SparseCore 0:
  54.9 45.5 all-gather.2
where the time goes:
time: 154 us; the launch traced here: 152 us
  starting transfers between devices  44.2 us (29%)
  blocking collectives  36.1 us (23%)
  waiting for transfers between devices  28.7 us (19%)
  Pallas kernels  18.7 us (12%)
  between operations  14.5 us (9%)
  local copies, waits for them, and re-layouts  6.31 us (4%)
  other arithmetic  2.79 us (2%)
    all_to_all x1, blocking collectives, spread(): lax.all_to_all(jnp.broadcast_to(array, (count, *array.shape)), axis, 0, 0...  26.1 us
    ppermute x7, starting transfers between devices, shift(): return lax.ppermute(array, axis, pairs)  17.5 us
    all_gather x1, waiting for transfers between devices, shards(): inputs = lax.all_gather(inputs, RING, axis=0)  16.1 us
    all_to_all x1, starting transfers between devices, spread(): lax.all_to_all(jnp.broadcast_to(array, (count, *array.shape)), axis, 0, 0...  15.1 us
    pallas_call x2, Pallas kernels, call_scalar(): pl.pallas_call(kernel, out_shape=outs, in_specs=[pl.BlockSpec(memory_spac...  15 us
    all_to_all x1, blocking collectives, shards(): grad_parts = lax.all_to_all(grad_parts, RING, 0, 0, tiled=True)  9.99 us
    all_to_all x1, waiting for transfers between devices, shards(): decoded_parts = lax.all_to_all(decoded_parts, RING, 0, 0, tiled=True)  7.01 us
    ppermute x1, starting transfers between devices, shards(): mix_other = lax.ppermute(raw_mix, RING, [(0, 3), (3, 0), (1, 2), (2, 1)])  5.22 us
  transfers between devices with their start and end apart: 12, of which 5 were waited for; matrix products, arithmetic and copies ran while one was open for 1% of the time, Pallas kernels for 2%

commit v1 on v0

--- a/solution.py
+++ b/solution.py
@@ -12,6 +12,7 @@
 RING = ("xh", "xl")
 LANES = 128
 PAD = 32
+OFFSETS = (0, 3, 1, 2)
 
 
 def shift(array, axis, by):
@@ -37,44 +38,45 @@
     return pltpu.roll(rows, rows.shape[0] - by, 0)
 
 
-def call(kernel, outs, scratch, flops, *operands):
-    space = pl.BlockSpec(memory_space=pltpu.VMEM)
-    return pl.pallas_call(
-        kernel,
-        out_shape=outs,
-        in_specs=[space] * len(operands),
-        out_specs=jax.tree.map(lambda _: space, outs),
-        scratch_shapes=scratch,
-        compiler_params=pltpu.CompilerParams(vmem_limit_bytes=48 * 2**20),
-        cost_estimate=pl.CostEstimate(flops=flops, bytes_accessed=8 * 2**20, transcendentals=0),
-    )(*operands)
-
-
-def unfold_kernel(sizes, inputs, frame_rows, cot_rows):
-    blocks, base = inputs.shape[0], 0
-    for out, (times, splits) in zip((frame_rows, cot_rows), sizes, strict=True):
-
-        def step(at, _, out=out, splits=splits, base=base):
+def unfold_kernel(sizes, place, own, other, frame_rows, cot_rows):
+    _, xl, core = place[0], place[1], place[2]
+    blocks, base = own.shape[0], 0
+    for out, (times, splits, width) in zip((frame_rows, cot_rows), sizes, strict=True):
+
+        def step(at, _, out=out, splits=splits, width=width, base=base):
             time, block = at // blocks, at % blocks
+            side = (xl + (block + 1) // 2) % 2
+            partner = jnp.where(xl == 0, (block + 2) % 4, block + 1 - 2 * (block % 2))
+            left = jnp.where(core == 1, block, partner)
+            right = jnp.where(core == 0, block, partner)
+            has_left = 2 * side + core > 0
+            has_right = 2 * side + core < 3
             target = pl.ds(pl.multiple_of(at * PAD, PAD), PAD)
             for row in range(2):
                 for split in range(splits):
-                    first = base + ((time * 2 + row) * splits + split) * PAD
-                    source = pl.ds(pl.multiple_of(first, PAD), PAD)
-                    chunk = inputs[block, source, :].astype(jnp.float32)
+                    first = base + ((time * 2 + row) * splits + split) * width
+                    rows = pl.ds(pl.multiple_of(first, 8), width)
+                    head = pl.ds(pl.multiple_of(first, 8), 8)
+                    tail = pl.ds(pl.multiple_of(first + width - 8, 8), 8)
+                    low = other[left, tail, :].astype(jnp.float32)
+                    middle = own[block, rows, :].astype(jnp.float32)
+                    high = other[right, head, :].astype(jnp.float32)
+                    low = jnp.where(has_left, low, 0.0)
+                    high = jnp.where(has_right, high, 0.0)
+                    chunk = jnp.concatenate((low, middle, high), axis=0)
                     for tap in range(3):
                         lane = ((row * 3 + tap) * splits + split) * LANES
-                        moved = later(chunk, tap).astype(jnp.bfloat16)
+                        moved = chunk[6 + tap : 6 + tap + PAD].astype(jnp.bfloat16)
                         out[target, lane : lane + LANES] = moved
             return 0
 
         lax.fori_loop(0, times * blocks, step, 0)
-        base += times * 2 * splits * PAD
-
-
-def readers(layout, first, own, other):
+        base += times * 2 * splits * width
+
+
+def readers(layout, place, own, other):
     nz, up_half, up_count, up_size = layout
-    lead = first[0] == 0
+    lead = place[2] == 0
 
     def low(start, count):
         rows = slice(start, start + count)
@@ -100,11 +102,18 @@
 
 
 def forward_kernel(
-    layout, first, rows, own, other, mask, decoded, slope, up_w, ups, hidden, mix_w, total
+    layout, place, rows, own, other, decoded, slope, up_w, ups, mask, hidden, mix_w, total
 ):
-    up_tile, mix_tile = readers(layout, first, own, other)
+    up_tile, mix_tile = readers(layout, place, own, other)
     splits = rows.shape[1] // (6 * LANES)
     part, unit = up_w.shape[0] // 6, mask.shape[0]
+    width = decoded.shape[3]
+    column = lax.broadcasted_iota(jnp.int32, (PAD, LANES), 0) - 1
+    for block in range(decoded.shape[0]):
+        side = (place[1] + (block + 1) // 2) % 2
+        at = (2 * side + place[2]) * width + column
+        inside = (at >= 0) & (at < 4 * width)
+        mask[block * PAD : (block + 1) * PAD, :] = inside.astype(jnp.float32)
     for kt in range(3):
         for out_row in range(2):
             for row in range(2):
@@ -164,24 +173,25 @@
             (((1,), (1,)), ((), ())),
             preferred_element_type=jnp.float32,
         )
-    store(decoded, total, channels)
-
-
-def store(out, total, channels):
+    store(place, decoded, total, channels)
+
+
+def store(place, out, total, channels):
     blocks, times, _, width, _ = out.shape
     for block in range(blocks):
+        member = (2 * place[0] + place[1] + OFFSETS[block]) % 4
         for time in range(times):
             at = (time * blocks + block) * PAD
             for out_row in range(2):
                 lanes = slice(out_row * channels, (out_row + 1) * channels)
                 value = total[at : at + PAD, lanes].astype(jnp.bfloat16)
-                out[block, time, out_row] = value[:width]
+                out[member, time, out_row] = value[:width]
 
 
 def backward_kernel(
-    layout, first, rows, own, other, slope, grads, mix_w, partial, evens, odds, up_w, total
+    layout, place, rows, own, other, slope, grads, mix_w, partial, evens, odds, up_w, total
 ):
-    up_tile, mix_tile = readers(layout, first, own, other)
+    up_tile, mix_tile = readers(layout, place, own, other)
     channels = rows.shape[1] // 6
     unit = evens.shape[0] - total.shape[0]
     splits = up_w.shape[1] // (2 * LANES)
@@ -214,9 +224,9 @@
         )
         value = hidden_grad * slope[at : at + unit, :]
         target = evens if time % 2 == 0 else odds
-        place = time // 2 * unit
+        spot = time // 2 * unit
         for shift_w in range(3):
-            target[place : place + unit, shift_w * LANES : (shift_w + 1) * LANES] = later(
+            target[spot : spot + unit, shift_w * LANES : (shift_w + 1) * LANES] = later(
                 value, shift_w
             ).astype(jnp.bfloat16)
     for kt in range(3):
@@ -238,22 +248,34 @@
             up_w[kt * 3 * LANES : (kt + 1) * 3 * LANES, :],
             preferred_element_type=jnp.float32,
         )
-    store(grads, total, splits * LANES)
-
-
-def unfold(inputs, frame_times, cot_times, frame_splits, cot_splits):
-    unit = inputs.shape[0] * PAD
-    sizes = ((frame_times, frame_splits), (cot_times, cot_splits))
+    store(place, grads, total, splits * LANES)
+
+
+def call(kernel, outs, scratch, flops, megabytes, place, *operands):
+    space = pl.BlockSpec(memory_space=pltpu.VMEM)
+    return pl.pallas_call(
+        kernel,
+        out_shape=outs,
+        in_specs=[pl.BlockSpec(memory_space=pltpu.SMEM)] + [space] * len(operands),
+        out_specs=jax.tree.map(lambda _: space, outs),
+        scratch_shapes=scratch,
+        compiler_params=pltpu.CompilerParams(vmem_limit_bytes=megabytes * 2**20),
+        cost_estimate=pl.CostEstimate(flops=flops, bytes_accessed=8 * 2**20, transcendentals=0),
+    )(place, *operands)
+
+
+def unfold(place, own, other, sizes):
+    unit = own.shape[0] * PAD
     outs = tuple(
         jax.ShapeDtypeStruct((times * unit, 6 * splits * LANES), jnp.bfloat16)
-        for times, splits in sizes
-    )
-    return call(functools.partial(unfold_kernel, sizes), outs, [], 10**6, inputs)
-
-
-def forward(layout, first, rows, own, other, mask, width, channels):
-    blocks = mask.shape[0] // PAD
-    unit = mask.shape[0]
+        for times, splits, _ in sizes
+    )
+    return call(functools.partial(unfold_kernel, sizes), outs, [], 10**9, 14, place, own, other)
+
+
+def forward(layout, place, rows, own, other, width, channels):
+    blocks = own.shape[0]
+    unit = blocks * PAD
     times = 2 * (rows.shape[0] // unit - 3)
     outs = (
         jax.ShapeDtypeStruct((blocks, times, 2, width, channels), jnp.bfloat16),
@@ -262,15 +284,16 @@
     scratch = [
         pltpu.VMEM((3 * LANES, rows.shape[1]), jnp.bfloat16),
         pltpu.VMEM((rows.shape[0], 3 * LANES), jnp.float32),
+        pltpu.VMEM((unit, LANES), jnp.float32),
         pltpu.VMEM(((times + 2) * unit, 3 * LANES), jnp.bfloat16),
         pltpu.VMEM((2 * channels, 9 * LANES), jnp.bfloat16),
         pltpu.VMEM((times * unit, 2 * channels), jnp.float32),
     ]
     kernel = functools.partial(forward_kernel, layout)
-    return call_scalar(kernel, outs, scratch, 2 * 10**9, first, rows, own, other, mask)
-
-
-def backward(layout, first, rows, own, other, slope, unit, width, in_channels):
+    return call(kernel, outs, scratch, 2 * 10**9, 14, place, rows, own, other)
+
+
+def backward(layout, place, rows, own, other, slope, unit, width, in_channels):
     times = slope.shape[0] // unit
     out = jax.ShapeDtypeStruct((unit // PAD, times // 2, 2, width, in_channels), jnp.bfloat16)
     scratch = [
@@ -282,32 +305,15 @@
         pltpu.VMEM((times // 2 * unit, 2 * in_channels), jnp.float32),
     ]
     kernel = functools.partial(backward_kernel, layout)
-    return call_scalar(kernel, out, scratch, 2 * 10**9, first, rows, own, other, slope)
-
-
-def call_scalar(kernel, outs, scratch, flops, first, *operands):
-    space = pl.BlockSpec(memory_space=pltpu.VMEM)
-    return pl.pallas_call(
-        kernel,
-        out_shape=outs,
-        in_specs=[pl.BlockSpec(memory_space=pltpu.SMEM)] + [space] * len(operands),
-        out_specs=jax.tree.map(lambda _: space, outs),
-        scratch_shapes=scratch,
-        compiler_params=pltpu.CompilerParams(vmem_limit_bytes=48 * 2**20),
-        cost_estimate=pl.CostEstimate(flops=flops, bytes_accessed=8 * 2**20, transcendentals=0),
-    )(first, *operands)
-
-
-def with_columns(field):
-    width = field.shape[2]
-    low = shift(field[:, :, width - 2 :], COLS, 1)
-    high = shift(field[:, :, :2], COLS, -1)
-    return jnp.concatenate((low, field, high), axis=2)
+    return call(kernel, out, scratch, 2 * 10**9, 14, place, rows, own, other, slope)
+
+
+def ring(array, by):
+    return lax.ppermute(array, RING, [(i, (i + by) % 4) for i in range(4)])
 
 
 def flat(field):
-    padded = jnp.pad(field, ((0, 0), (0, 0), (0, PAD - field.shape[2]), (0, 0)))
-    tiles = padded.reshape(*padded.shape[:3], -1, LANES)
+    tiles = field.reshape(*field.shape[:3], -1, LANES)
     return tiles.transpose(0, 1, 3, 2, 4).reshape(-1, LANES)
 
 
@@ -350,15 +356,15 @@
     mix_part = mix_part.reshape(9, 2, 2, 2 * part).transpose(0, 2, 1, 3).reshape(-1, 2, LANES)
 
     planes = spread(jnp.concatenate((up_part, mix_part), axis=0), "z")
-    wide_frames, wide_cot = with_columns(frames), with_columns(cotangent)
     fields = jnp.concatenate(
-        (shift(wide_frames[-2:], PLANES, 1), wide_frames, shift(wide_frames[:1], PLANES, -1)),
-        axis=0,
-    )
-    cots = jnp.concatenate((wide_cot, shift(wide_cot[:3], PLANES, -1)), axis=0)
-    planes, fields, cots = lax.optimization_barrier((planes, fields, cots))
-    inputs = jnp.concatenate((flat(fields), flat(cots)), axis=0)
-    inputs = lax.all_gather(inputs, RING, axis=0)
+        (shift(frames[-2:], PLANES, 1), frames, shift(frames[:1], PLANES, -1)), axis=0
+    )
+    cots = jnp.concatenate((cotangent, shift(cotangent[:3], PLANES, -1)), axis=0)
+    block = jnp.concatenate((flat(fields), flat(cots)), axis=0)
+    blocks = (block, ring(block, 1), ring(block, -1), ring(block, 2))
+    planes, block = lax.optimization_barrier((planes, block))
+    blocks = jnp.stack(blocks)
+    others = swap(blocks)
 
     up_rows = planes[:, :up_pairs].transpose(1, 2, 0, 3).reshape(-1, LANES)
     mix_rows = planes[:, up_pairs:].transpose(1, 0, 2, 3).reshape(-1, LANES)
@@ -366,23 +372,18 @@
     other = swap(own)
     layout = (nz, up_half, up_count, up_rows.shape[0])
 
-    frame_rows, cot_rows = unfold(
-        inputs, fields.shape[0], cots.shape[0], in_channels // LANES, splits
-    )
-    columns = lax.axis_size(COLS) * width
-    firsts = (2 * (jnp.arange(nx) % 2) + core) * width - 1
-    at = firsts[:, None] + jnp.arange(PAD)
-    inside = ((at >= 0) & (at < columns)).astype(jnp.float32).reshape(-1, 1)
-    mask = jnp.broadcast_to(inside, (nx * PAD, LANES))
-    first = core.reshape(1)
-
-    decoded_parts, slope = forward(
-        layout, first, frame_rows, own, other, mask, width, out_channels
-    )
+    place = jnp.stack((xh, xl, core))
+    sizes = (
+        (fields.shape[0], in_channels // LANES, width),
+        (cots.shape[0], splits, width),
+    )
+    frame_rows, cot_rows = unfold(place, blocks, others, sizes)
+    decoded_parts, slope = forward(layout, place, frame_rows, own, other, width, out_channels)
     decoded_parts = lax.all_to_all(decoded_parts, RING, 0, 0, tiled=True)
     grad_parts = backward(
-        layout, first, cot_rows, own, other, slope, nx * PAD, width, in_channels
-    )
+        layout, place, cot_rows, own, other, slope, nx * PAD, width, in_channels
+    )
+    decoded_parts, grad_parts = lax.optimization_barrier((decoded_parts, grad_parts))
     grad_parts = lax.all_to_all(grad_parts, RING, 0, 0, tiled=True)
     decoded = jnp.sum(decoded_parts.astype(jnp.float32), axis=0)
     frames_grad = jnp.sum(grad_parts.astype(jnp.float32), axis=0)

time: 154 us -> 119 us (0.77)
  blocking collectives: 36.1 us -> 0 us
  between operations: 14.5 us -> 1.03 us
  starting transfers between devices: 44.2 us -> 57.1 us
  local copies, waits for them, and re-layouts: 6.31 us -> 9.55 us
  other arithmetic: 2.79 us -> 4.36 us
    all_to_all x2 -> x0, blocking collectives: 36.1 us -> none  [the longest x1 26.1 us: spread(): lax.all_to_all(jnp.broadcast_to(array, (count, *array.shape)), axis, 0, 0...]
    all_gather x1 -> x0, waiting for transfers between devices: 16.1 us -> none  [shards(): inputs = lax.all_gather(inputs, RING, axis=0)]
    ppermute x7 -> x3, starting transfers between devices: 17.5 us -> 5.85 us  [shift(): return lax.ppermute(array, axis, pairs)]
    ppermute x0 -> x3, starting transfers between devices: none -> 9.19 us  [ring(): return lax.ppermute(array, RING, [(i, (i + by) % 4) for i in range(4)])]
    ppermute x0 -> x3, waiting for transfers between devices: none -> 8.74 us  [ring(): return lax.ppermute(array, RING, [(i, (i + by) % 4) for i in range(4)])]
    ppermute x1 -> x2, starting transfers between devices: 2.89 us -> 9.19 us  [swap(): return lax.ppermute(array, 'core', [(0, 1), (1, 0)])]
    ppermute x7 -> x3, waiting for transfers between devices: 4.63 us -> 10.7 us  [shift(): return lax.ppermute(array, axis, pairs)]
    all_to_all x1, waiting for transfers between devices: 7.01 us -> 1.19 us  [shards(): decoded_parts = lax.all_to_all(decoded_parts, RING, 0, 0, tiled=True)]
  transfers between devices with their start and end apart: 12 -> 13, of which waited for: 5 -> 6; matrix products, arithmetic and copies ran while one was open for 1% -> 5% of each run, Pallas kernels for 2% -> 10%
where the time goes in v1:
time: 119 us; the launch traced here: 118 us
  starting transfers between devices  57.1 us (48%)
  waiting for transfers between devices  27.2 us (23%)
  Pallas kernels  18.3 us (15%)
  local copies, waits for them, and re-layouts  9.55 us (8%)
  other arithmetic  4.36 us (4%)
    all_to_all x2, starting transfers between devices, spread(): lax.all_to_all(jnp.broadcast_to(array, (count, *array.shape)), axis, 0, 0...  20 us
    pallas_call x3, Pallas kernels, call(): pl.pallas_call(kernel, out_shape=outs, in_specs=[pl.BlockSpec(memory_spac...  18.3 us
    ppermute x3, waiting for transfers between devices, shift(): return lax.ppermute(array, axis, pairs)  10.7 us
    ppermute x2, starting transfers between devices, swap(): return lax.ppermute(array, 'core', [(0, 1), (1, 0)])  9.19 us
    ppermute x3, starting transfers between devices, ring(): return lax.ppermute(array, RING, [(i, (i + by) % 4) for i in range(4)])  9.19 us
    ppermute x3, waiting for transfers between devices, ring(): return lax.ppermute(array, RING, [(i, (i + by) % 4) for i in range(4)])  8.74 us
    unnamed x20, local copies, waits for them, and re-layouts  6.01 us
    ppermute x3, starting transfers between devices, shift(): return lax.ppermute(array, axis, pairs)  5.85 us
  transfers between devices with their start and end apart: 13, of which 6 were waited for; matrix products, arithmetic and copies ran while one was open for 5% of the time, Pallas kernels for 10%

profile of v1, /device:TPU:1, one launch (start us, length us, event | category | flops | bytes accessed | tf_op | source)
XLA Modules:
  0.0 117.9 jit_solution(12393740904463171243)
XLA Ops:
  0.6 0.0 copy-start
  0.6 0.8 reshape.52
  1.5 5.2 %collective-permute-start.7 = (bf16[54,2,128]{2,0,1:T(8,128)(2,1)S(1)}, bf16[54,2,128]{2,0,1:T(8,128)(2,1)S(1)}, u32[]{:S(2)}, u32[]{:S(2)}) collective-permute-start(bf16[54,2,128]{2,0,1:T(8,128)(2,1)S(1)} %bitcast.52), channel_id=1, source_target_pairs={{0,66},{66,0},{2,64},{64,2},{1,67},{67,1},{3,65},{65,3},{4,70},{70... | collective-permute-start | bytes 82952 | tf_op jit(solution)/shard_map/ppermute | solution.py:332
  6.8 0.1 dynamic-slice_reduce_fusion
  7.0 0.9 collective-permute-done.7
  8.0 0.0 copy-start.5
  8.0 0.0 copy-start.9
  8.0 0.3 fusion
  8.4 0.9 broadcast_in_dim.6
  9.3 15.1 %all-to-all-start = ((bf16[16,39,2,128]{3,2,1,0:T(2,128)(2,1)}), bf16[16,39,2,128]{3,2,1,0:T(2,128)(2,1)S(1)}, u32[]{:S(2)}, u32[]{:S(2)}) async-start(bf16[16,39,2,128]{3,2,1,0:T(2,128)(2,1)} %broadcast_in_dim.6), calls=%async_computation | async-start | bytes 638976 | tf_op jit(solution)/shard_map/all_to_all | solution.py:30
  24.4 3.3 %collective-permute-start = (bf16[2,2,24,384]{3,2,1,0:T(8,128)(2,1)S(1)}, bf16[2,2,24,384]{3,2,1,0:T(8,128)(2,1)S(1)}, u32[]{:S(2)}, u32[]{:S(2)}) collective-permute-start(bf16[2,2,24,384]{3,2,1,0:T(8,128)(2,1)S(1)} %slice.15), channel_id=1, source_target_pairs={{0,4},{4,8},{8,12},{12,16},{16,20},{20,24},{24,28},{28,32},{32,36}... | collective-permute-start | bytes 221192 | tf_op jit(solution)/shard_map/ppermute | solution.py:21
  27.7 1.3 %collective-permute-start.1 = (bf16[1,2,24,384]{3,2,1,0:T(8,128)(2,1)S(1)}, bf16[1,2,24,384]{3,2,1,0:T(8,128)(2,1)S(1)}, u32[]{:S(2)}, u32[]{:S(2)}) collective-permute-start(bf16[1,2,24,384]{3,2,1,0:T(8,128)(2,1)S(1)} %slice.16), channel_id=1, source_target_pairs={{4,0},{8,4},{12,8},{16,12},{20,16},{24,20},{28,24},{32,28},{36,32}... | collective-permute-start | bytes 110600 | tf_op jit(solution)/shard_map/ppermute | solution.py:21
  29.1 1.3 %collective-permute-start.2 = (bf16[3,2,24,256]{3,2,1,0:T(8,128)(2,1)S(1)}, bf16[3,2,24,256]{3,2,1,0:T(8,128)(2,1)S(1)}, u32[]{:S(2)}, u32[]{:S(2)}) collective-permute-start(bf16[3,2,24,256]{3,2,1,0:T(8,128)(2,1)S(1)} %slice.17), channel_id=1, source_target_pairs={{4,0},{8,4},{12,8},{16,12},{20,16},{24,20},{28,24},{32,28},{36,32}... | collective-permute-start | bytes 221192 | tf_op jit(solution)/shard_map/ppermute | solution.py:21
  30.4 7.5 %collective-permute-done.1 = bf16[1,2,24,384]{3,2,1,0:T(8,128)(2,1)S(1)} collective-permute-done((bf16[1,2,24,384]{3,2,1,0:T(8,128)(2,1)S(1)}, bf16[1,2,24,384]{3,2,1,0:T(8,128)(2,1)S(1)}, u32[]{:S(2)}, u32[]{:S(2)}) %collective-permute-start.1) | collective-permute-done | bytes 36896 | tf_op jit(solution)/shard_map/ppermute | solution.py:21
  37.9 0.0 collective-permute-done
  37.9 0.1 reshape.46
  38.0 3.2 %collective-permute-done.2 = bf16[3,2,24,256]{3,2,1,0:T(8,128)(2,1)S(1)} collective-permute-done((bf16[3,2,24,256]{3,2,1,0:T(8,128)(2,1)S(1)}, bf16[3,2,24,256]{3,2,1,0:T(8,128)(2,1)S(1)}, u32[]{:S(2)}, u32[]{:S(2)}) %collective-permute-start.2) | collective-permute-done | bytes 73760 | tf_op jit(solution)/shard_map/ppermute | solution.py:21
  41.3 0.1 fusion.51
  41.4 3.8 %collective-permute-start.5 = (bf16[1728,128]{1,0:T(8,128)(2,1)S(1)}, bf16[1728,128]{1,0:T(8,128)(2,1)S(1)}, u32[]{:S(2)}, u32[]{:S(2)}) collective-permute-start(bf16[1728,128]{1,0:T(8,128)(2,1)S(1)} %get-tuple-element.17), channel_id=1, source_target_pairs={{0,64},{2,66},{64,0},{66,2},{1,65},{3,67},{65,1},{67,3},{4,68},{6,... | collective-permute-start | bytes 1327112 | tf_op jit(solution)/shard_map/ppermute | solution.py:312
  45.2 2.9 %collective-permute-start.4 = (bf16[1728,128]{1,0:T(8,128)(2,1)S(1)}, bf16[1728,128]{1,0:T(8,128)(2,1)S(1)}, u32[]{:S(2)}, u32[]{:S(2)}) collective-permute-start(bf16[1728,128]{1,0:T(8,128)(2,1)S(1)} %get-tuple-element.17), channel_id=1, source_target_pairs={{0,66},{2,0},{64,2},{66,64},{1,67},{3,1},{65,3},{67,65},{4,70},{6,... | collective-permute-start | bytes 1327112 | tf_op jit(solution)/shard_map/ppermute | solution.py:312
  48.1 2.5 %collective-permute-start.3 = (bf16[1728,128]{1,0:T(8,128)(2,1)S(1)}, bf16[1728,128]{1,0:T(8,128)(2,1)S(1)}, u32[]{:S(2)}, u32[]{:S(2)}) collective-permute-start(bf16[1728,128]{1,0:T(8,128)(2,1)S(1)} %get-tuple-element.17), channel_id=1, source_target_pairs={{0,2},{2,64},{64,66},{66,0},{1,3},{3,65},{65,67},{67,1},{4,6},{6,6... | collective-permute-start | bytes 1327112 | tf_op jit(solution)/shard_map/ppermute | solution.py:312
  50.6 0.1 slice_bitcast_fusion
  50.7 0.1 copy.35
  50.9 1.2 %broadcast_in_dim.7 = bf16[4,1248,128]{2,1,0:T(8,128)(2,1)} broadcast(bf16[1248,128]{1,0:T(8,128)(2,1)S(1)} %pad_maximum_fusion.2), dimensions={1,2} | broadcast | bytes 1597440 | tf_op jit(solution)/shard_map/broadcast_in_dim | solution.py:31
  52.1 4.9 %all-to-all-start.1 = ((bf16[4,1248,128]{2,1,0:T(8,128)(2,1)}), bf16[4,1248,128]{2,1,0:T(8,128)(2,1)S(1)}, u32[]{:S(2)}, u32[]{:S(2)}) async-start(bf16[4,1248,128]{2,1,0:T(8,128)(2,1)} %broadcast_in_dim.7), calls=%async_computation.1 | async-start | bytes 2555904 | tf_op jit(solution)/shard_map/all_to_all | solution.py:30
  57.1 8.7 %collective-permute-done.4 = bf16[1728,128]{1,0:T(8,128)(2,1)S(1)} collective-permute-done((bf16[1728,128]{1,0:T(8,128)(2,1)S(1)}, bf16[1728,128]{1,0:T(8,128)(2,1)S(1)}, u32[]{:S(2)}, u32[]{:S(2)}) %collective-permute-start.4) | collective-permute-done | bytes 442400 | tf_op jit(solution)/shard_map/ppermute | solution.py:312
  65.8 0.0 collective-permute-done.3
  65.8 0.8 copy-done.7
  66.6 0.2 copy-done.8
  66.7 1.5 %pad_maximum_fusion.own = bf16[4,1728,128]{2,1,0:T(8,128)(2,1)S(1)} fusion(bf16[1,1728,128]{2,1,0:T(8,128)(2,1)} %bitcast.49, bf16[1,1728,128]{2,1,0:T(8,128)(2,1)} %bitcast.50, bf16[1,1728,128]{2,1,0:T(8,128)(2,1)} %bitcast.51, bf16[1,1728,128]{2,1,0:T(8,128)(2,1)S(1)} %get-tuple-element.16), kind=kLoop, calls=%fused_computation.4 | loop fusion | flops 2654208 | bytes 3538944 | tf_op jit(solution)/shard_map/stack | solution.py:366
  68.2 3.5 %collective-permute-start.6 = (bf16[4,1728,128]{2,1,0:T(8,128)(2,1)S(1)}, bf16[4,1728,128]{2,1,0:T(8,128)(2,1)}, u32[]{:S(2)}, u32[]{:S(2)}) collective-permute-start(bf16[4,1728,128]{2,1,0:T(8,128)(2,1)S(1)} %pad_maximum_fusion.own), channel_id=1, source_target_pairs={{0,1},{1,0},{2,3},{3,2},{4,5},{5,4},{6,7},{7,6},{8,9},{9,8},{10,11... | collective-permute-start | bytes 5308424 | tf_op jit(solution)/shard_map/ppermute | solution.py:25
  71.7 0.0 all-to-all-done.1.own
  71.7 5.7 %collective-permute-start.8 = (bf16[4,1248,128]{2,1,0:T(8,128)(2,1)S(1)}, bf16[4,1248,128]{2,1,0:T(8,128)(2,1)S(1)}, u32[]{:S(2)}, u32[]{:S(2)}) collective-permute-start(bf16[4,1248,128]{2,1,0:T(8,128)(2,1)S(1)} %all-to-all-done.1.own), channel_id=1, source_target_pairs={{0,1},{1,0},{2,3},{3,2},{4,5},{5,4},{6,7},{7,6},{8,9},{9,8},{10,11... | collective-permute-start | bytes 3833864 | tf_op jit(solution)/shard_map/ppermute | solution.py:25
  77.5 0.1 pad_add_fusion.place
  77.5 0.0 collective-permute-done.6.other
  77.5 5.4 %shard_map.59 = (bf16[768,2304]{1,0:T(8,128)(2,1)S(1)}, bf16[1152,1536]{1,0:T(8,128)(2,1)S(1)}) custom-call(s32[3]{0:T(128)S(1)} %pad_add_fusion.place, bf16[4,1728,128]{2,1,0:T(8,128)(2,1)S(1)} %pad_maximum_fusion.own, bf16[4,1728,128]{2,1,0:T(8,128)(2,1)} %collective-permute-done.6.other), custom_call_target="tpu_custom_call" | custom-call | flops 1000000000 | bytes 8388608 | tf_op jit(solution)/shard_map/pallas_call | solution.py:256
  82.9 1.7 %copy-done.3 = bf16[1152,1536]{1,0:T(8,128)(2,1)} copy-done((bf16[1152,1536]{1,0:T(8,128)(2,1)}, bf16[1152,1536]{1,0:T(8,128)(2,1)S(1)}, u32[]{:S(2)}) %copy-start.3) | copy-done | bytes 3538968
  84.7 0.0 collective-permute-done.8.other
  84.7 7.1 %shard_map.60 = (bf16[4,6,2,24,256]{4,3,2,1,0:T(8,128)(2,1)}, f32[896,128]{1,0:T(8,128)S(1)}) custom-call(s32[3]{0:T(128)S(1)} %pad_add_fusion.place, bf16[768,2304]{1,0:T(8,128)(2,1)S(1)} %get-tuple-element.9.rows, bf16[4,1248,128]{2,1,0:T(8,128)(2,1)S(1)} %all-to-all-done.1.own, bf16[4,1248,128]{2,1,0:T(8,128)(2,1)S(1)} %collective-permute-done.8.other), custom_call_target="tpu_custom_call" | custom-call | flops 2000000000 | bytes 8388608 | tf_op jit(solution)/shard_map/pallas_call | solution.py:256
  91.7 4.1 %all-to-all-start.2 = ((bf16[4,6,2,24,256]{4,3,2,1,0:T(8,128)(2,1)}), bf16[4,6,2,24,256]{4,3,2,1,0:T(8,128)(2,1)}, u32[]{:S(2)}, u32[]{:S(2)}) async-start(bf16[4,6,2,24,256]{4,3,2,1,0:T(8,128)(2,1)} %get-tuple-element.11), calls=%async_computation.2 | async-start | bytes 1179648 | tf_op jit(solution)/shard_map/all_to_all | solution.py:382
  95.9 1.3 %copy-done.2 = bf16[4,1248,128]{2,1,0:T(8,128)(2,1)S(1)} copy-done((bf16[4,1248,128]{2,1,0:T(8,128)(2,1)S(1)}, bf16[4,1248,128]{2,1,0:T(8,128)(2,1)}, u32[]{:S(2)}) %copy-start.2) | copy-done | bytes 1277976
  97.2 2.0 %copy-done.4 = bf16[1152,1536]{1,0:T(8,128)(2,1)S(1)} copy-done((bf16[1152,1536]{1,0:T(8,128)(2,1)S(1)}, bf16[1152,1536]{1,0:T(8,128)(2,1)}, u32[]{:S(2)}) %copy-start.4) | copy-done | bytes 3538968
  99.2 5.9 %shard_map.61 = bf16[4,3,2,24,384]{4,3,2,1,0:T(8,128)(2,1)} custom-call(s32[3]{0:T(128)S(1)} %pad_add_fusion.place, bf16[1152,1536]{1,0:T(8,128)(2,1)S(1)} %copy-done.4, bf16[4,1248,128]{2,1,0:T(8,128)(2,1)S(1)} %all-to-all-done.1.own, bf16[4,1248,128]{2,1,0:T(8,128)(2,1)S(1)} %copy-done.2, f32[896,128]{1,0:T(8,128)S(1)} %get-tuple-element.13.slope), custom_call_target="tpu_custom_call" | custom-call | flops 2000000000 | bytes 8388608 | tf_op jit(solution)/shard_map/pallas_call | solution.py:256
  105.1 1.2 %all-to-all-done.2 = bf16[4,6,2,24,256]{4,3,2,1,0:T(8,128)(2,1)} async-done(((bf16[4,6,2,24,256]{4,3,2,1,0:T(8,128)(2,1)}), bf16[4,6,2,24,256]{4,3,2,1,0:T(8,128)(2,1)}, u32[]{:S(2)}, u32[]{:S(2)}) %all-to-all-start.2) | async-done | bytes 589856 | tf_op jit(solution)/shard_map/all_to_all | solution.py:382
  106.2 3.5 %all-to-all-start.3 = ((bf16[4,3,2,24,384]{4,3,2,1,0:T(8,128)(2,1)}), bf16[4,3,2,24,384]{4,3,2,1,0:T(8,128)(2,1)S(1)}, u32[]{:S(2)}, u32[]{:S(2)}) async-start(bf16[4,3,2,24,384]{4,3,2,1,0:T(8,128)(2,1)} %shard_map.61), calls=%async_computation.3 | async-start | bytes 884736 | tf_op jit(solution)/shard_map/all_to_all | solution.py:387
  109.7 1.8 %reduce_sum.24 = bf16[6,2,24,256]{3,2,1,0:T(8,128)(2,1)} reduce(bf16[4,6,2,24,256]{4,3,2,1,0:T(8,128)(2,1)} %all-to-all-done.2, bf16[]{:T(256)} %constant.92.clone.1), dimensions={0}, to_apply=%region_0.1 | reduce | flops 221184 | bytes 737282 | tf_op jit(solution)/shard_map/reduce_sum | solution.py:388
  111.6 5.6 %all-to-all-done.3 = bf16[4,3,2,24,384]{4,3,2,1,0:T(8,128)(2,1)S(1)} async-done(((bf16[4,3,2,24,384]{4,3,2,1,0:T(8,128)(2,1)}), bf16[4,3,2,24,384]{4,3,2,1,0:T(8,128)(2,1)S(1)}, u32[]{:S(2)}, u32[]{:S(2)}) %all-to-all-start.3) | async-done | bytes 442400 | tf_op jit(solution)/shard_map/all_to_all | solution.py:387
  117.2 0.7 reduce_sum.25
  (38 shorter events, 0.4 us)
Async XLA Ops:
  0.6 6.1 %copy-start = (bf16[10368,2]{0,1:T(2,128)(2,1)S(1)}, bf16[10368,2]{0,1:T(2,128)(2,1)}, u32[]{:S(2)}) copy-start(bf16[10368,2]{0,1:T(2,128)(2,1)} %param.5) | copy-start | bytes 124420
  1.5 6.5 %collective-permute-start.7 = (bf16[54,2,128]{2,0,1:T(8,128)(2,1)S(1)}, bf16[54,2,128]{2,0,1:T(8,128)(2,1)S(1)}, u32[]{:S(2)}, u32[]{:S(2)}) collective-permute-start(bf16[54,2,128]{2,0,1:T(8,128)(2,1)S(1)} %bitcast.52), channel_id=1, source_target_pairs={{0,66},{66,0},{2,64},{64,2},{1,67},{67,1},{3,65},{65,3},{4,70},{70... | collective-permute-start | bytes 82952 | tf_op jit(solution)/shard_map/ppermute | solution.py:332
  8.0 16.5 %copy-start.5 = (bf16[3,2,24,384]{3,2,1,0:T(8,128)(2,1)S(1)}, bf16[3,2,24,384]{3,2,1,0:T(8,128)(2,1)}, u32[]{:S(2)}) copy-start(bf16[3,2,24,384]{3,2,1,0:T(8,128)(2,1)} %param.4) | copy-start | bytes 331780
  8.0 21.1 %copy-start.9 = (bf16[6,2,24,256]{3,2,1,0:T(8,128)(2,1)S(1)}, bf16[6,2,24,256]{3,2,1,0:T(8,128)(2,1)}, u32[]{:S(2)}) copy-start(bf16[6,2,24,256]{3,2,1,0:T(8,128)(2,1)} %param.7) | copy-start | bytes 442372
  9.3 41.3 %all-to-all-start = ((bf16[16,39,2,128]{3,2,1,0:T(2,128)(2,1)}), bf16[16,39,2,128]{3,2,1,0:T(2,128)(2,1)S(1)}, u32[]{:S(2)}, u32[]{:S(2)}) async-start(bf16[16,39,2,128]{3,2,1,0:T(2,128)(2,1)} %broadcast_in_dim.6), calls=%async_computation | async-start | bytes 638976 | tf_op jit(solution)/shard_map/all_to_all | solution.py:30
  24.4 13.4 %collective-permute-start = (bf16[2,2,24,384]{3,2,1,0:T(8,128)(2,1)S(1)}, bf16[2,2,24,384]{3,2,1,0:T(8,128)(2,1)S(1)}, u32[]{:S(2)}, u32[]{:S(2)}) collective-permute-start(bf16[2,2,24,384]{3,2,1,0:T(8,128)(2,1)S(1)} %slice.15), channel_id=1, source_target_pairs={{0,4},{4,8},{8,12},{12,16},{16,20},{20,24},{24,28},{28,32},{32,36}... | collective-permute-start | bytes 221192 | tf_op jit(solution)/shard_map/ppermute | solution.py:21
  27.7 10.1 %collective-permute-start.1 = (bf16[1,2,24,384]{3,2,1,0:T(8,128)(2,1)S(1)}, bf16[1,2,24,384]{3,2,1,0:T(8,128)(2,1)S(1)}, u32[]{:S(2)}, u32[]{:S(2)}) collective-permute-start(bf16[1,2,24,384]{3,2,1,0:T(8,128)(2,1)S(1)} %slice.16), channel_id=1, source_target_pairs={{4,0},{8,4},{12,8},{16,12},{20,16},{24,20},{28,24},{32,28},{36,32}... | collective-permute-start | bytes 110600 | tf_op jit(solution)/shard_map/ppermute | solution.py:21
  29.1 12.2 %collective-permute-start.2 = (bf16[3,2,24,256]{3,2,1,0:T(8,128)(2,1)S(1)}, bf16[3,2,24,256]{3,2,1,0:T(8,128)(2,1)S(1)}, u32[]{:S(2)}, u32[]{:S(2)}) collective-permute-start(bf16[3,2,24,256]{3,2,1,0:T(8,128)(2,1)S(1)} %slice.17), channel_id=1, source_target_pairs={{4,0},{8,4},{12,8},{16,12},{20,16},{24,20},{28,24},{32,28},{36,32}... | collective-permute-start | bytes 221192 | tf_op jit(solution)/shard_map/ppermute | solution.py:21
  41.4 15.7 %collective-permute-start.5 = (bf16[1728,128]{1,0:T(8,128)(2,1)S(1)}, bf16[1728,128]{1,0:T(8,128)(2,1)S(1)}, u32[]{:S(2)}, u32[]{:S(2)}) collective-permute-start(bf16[1728,128]{1,0:T(8,128)(2,1)S(1)} %get-tuple-element.17), channel_id=1, source_target_pairs={{0,64},{2,66},{64,0},{66,2},{1,65},{3,67},{65,1},{67,3},{4,68},{6,... | collective-permute-start | bytes 1327112 | tf_op jit(solution)/shard_map/ppermute | solution.py:312
  45.2 20.6 %collective-permute-start.4 = (bf16[1728,128]{1,0:T(8,128)(2,1)S(1)}, bf16[1728,128]{1,0:T(8,128)(2,1)S(1)}, u32[]{:S(2)}, u32[]{:S(2)}) collective-permute-start(bf16[1728,128]{1,0:T(8,128)(2,1)S(1)} %get-tuple-element.17), channel_id=1, source_target_pairs={{0,66},{2,0},{64,2},{66,64},{1,67},{3,1},{65,3},{67,65},{4,70},{6,... | collective-permute-start | bytes 1327112 | tf_op jit(solution)/shard_map/ppermute | solution.py:312
  48.1 17.7 %collective-permute-start.3 = (bf16[1728,128]{1,0:T(8,128)(2,1)S(1)}, bf16[1728,128]{1,0:T(8,128)(2,1)S(1)}, u32[]{:S(2)}, u32[]{:S(2)}) collective-permute-start(bf16[1728,128]{1,0:T(8,128)(2,1)S(1)} %get-tuple-element.17), channel_id=1, source_target_pairs={{0,2},{2,64},{64,66},{66,0},{1,3},{3,65},{65,67},{67,1},{4,6},{6,6... | collective-permute-start | bytes 1327112 | tf_op jit(solution)/shard_map/ppermute | solution.py:312
  52.1 19.6 %all-to-all-start.1 = ((bf16[4,1248,128]{2,1,0:T(8,128)(2,1)}), bf16[4,1248,128]{2,1,0:T(8,128)(2,1)S(1)}, u32[]{:S(2)}, u32[]{:S(2)}) async-start(bf16[4,1248,128]{2,1,0:T(8,128)(2,1)} %broadcast_in_dim.7), calls=%async_computation.1 | async-start | bytes 2555904 | tf_op jit(solution)/shard_map/all_to_all | solution.py:30
  57.0 8.8 %copy-start.6 = (bf16[1728,128]{1,0:T(8,128)(2,1)}, bf16[1728,128]{1,0:T(8,128)(2,1)S(1)}, u32[]{:S(2)}) copy-start(bf16[1728,128]{1,0:T(8,128)(2,1)S(1)} %collective-permute-done.5) | copy-start | bytes 1327108
  65.8 0.8 copy-start.7
  65.8 0.9 copy-start.8
  68.2 9.3 %collective-permute-start.6 = (bf16[4,1728,128]{2,1,0:T(8,128)(2,1)S(1)}, bf16[4,1728,128]{2,1,0:T(8,128)(2,1)}, u32[]{:S(2)}, u32[]{:S(2)}) collective-permute-start(bf16[4,1728,128]{2,1,0:T(8,128)(2,1)S(1)} %pad_maximum_fusion.own), channel_id=1, source_target_pairs={{0,1},{1,0},{2,3},{3,2},{4,5},{5,4},{6,7},{7,6},{8,9},{9,8},{10,11... | collective-permute-start | bytes 5308424 | tf_op jit(solution)/shard_map/ppermute | solution.py:25
  71.7 12.9 %collective-permute-start.8 = (bf16[4,1248,128]{2,1,0:T(8,128)(2,1)S(1)}, bf16[4,1248,128]{2,1,0:T(8,128)(2,1)S(1)}, u32[]{:S(2)}, u32[]{:S(2)}) collective-permute-start(bf16[4,1248,128]{2,1,0:T(8,128)(2,1)S(1)} %all-to-all-done.1.own), channel_id=1, source_target_pairs={{0,1},{1,0},{2,3},{3,2},{4,5},{5,4},{6,7},{7,6},{8,9},{9,8},{10,11... | collective-permute-start | bytes 3833864 | tf_op jit(solution)/shard_map/ppermute | solution.py:25
  82.9 1.8 %copy-start.3 = (bf16[1152,1536]{1,0:T(8,128)(2,1)}, bf16[1152,1536]{1,0:T(8,128)(2,1)S(1)}, u32[]{:S(2)}) copy-start(bf16[1152,1536]{1,0:T(8,128)(2,1)S(1)} %get-tuple-element.12.rows) | copy-start | bytes 10616836
  84.7 7.1 %copy-start.1 = (bf16[4,1248,128]{2,1,0:T(8,128)(2,1)}, bf16[4,1248,128]{2,1,0:T(8,128)(2,1)S(1)}, u32[]{:S(2)}) copy-start(bf16[4,1248,128]{2,1,0:T(8,128)(2,1)S(1)} %collective-permute-done.8.other) | copy-start | bytes 3833860
  91.7 14.5 %all-to-all-start.2 = ((bf16[4,6,2,24,256]{4,3,2,1,0:T(8,128)(2,1)}), bf16[4,6,2,24,256]{4,3,2,1,0:T(8,128)(2,1)}, u32[]{:S(2)}, u32[]{:S(2)}) async-start(bf16[4,6,2,24,256]{4,3,2,1,0:T(8,128)(2,1)} %get-tuple-element.11), calls=%async_computation.2 | async-start | bytes 1179648 | tf_op jit(solution)/shard_map/all_to_all | solution.py:382
  95.9 1.3 %copy-start.2 = (bf16[4,1248,128]{2,1,0:T(8,128)(2,1)S(1)}, bf16[4,1248,128]{2,1,0:T(8,128)(2,1)}, u32[]{:S(2)}) copy-start(bf16[4,1248,128]{2,1,0:T(8,128)(2,1)} %copy-done.1) | copy-start | bytes 3833860
  97.2 2.0 %copy-start.4 = (bf16[1152,1536]{1,0:T(8,128)(2,1)S(1)}, bf16[1152,1536]{1,0:T(8,128)(2,1)}, u32[]{:S(2)}) copy-start(bf16[1152,1536]{1,0:T(8,128)(2,1)} %copy-done.3) | copy-start | bytes 10616836
  106.2 10.9 %all-to-all-start.3 = ((bf16[4,3,2,24,384]{4,3,2,1,0:T(8,128)(2,1)}), bf16[4,3,2,24,384]{4,3,2,1,0:T(8,128)(2,1)S(1)}, u32[]{:S(2)}, u32[]{:S(2)}) async-start(bf16[4,3,2,24,384]{4,3,2,1,0:T(8,128)(2,1)} %shard_map.61), calls=%async_computation.3 | async-start | bytes 884736 | tf_op jit(solution)/shard_map/all_to_all | solution.py:387

commit v2 on v1

--- a/solution.py
+++ b/solution.py
@@ -102,14 +102,13 @@
 
 
 def forward_kernel(
-    layout, place, rows, own, other, decoded, slope, up_w, ups, mask, hidden, mix_w, total
+    layout, width, place, rows, own, other, out, slope, up_w, ups, mask, hidden, mix_w, total
 ):
     up_tile, mix_tile = readers(layout, place, own, other)
     splits = rows.shape[1] // (6 * LANES)
     part, unit = up_w.shape[0] // 6, mask.shape[0]
-    width = decoded.shape[3]
     column = lax.broadcasted_iota(jnp.int32, (PAD, LANES), 0) - 1
-    for block in range(decoded.shape[0]):
+    for block in range(out.shape[0]):
         side = (place[1] + (block + 1) // 2) % 2
         at = (2 * side + place[2]) * width + column
         inside = (at >= 0) & (at < 4 * width)
@@ -173,23 +172,38 @@
             (((1,), (1,)), ((), ())),
             preferred_element_type=jnp.float32,
         )
-    store(place, decoded, total, channels)
-
-
-def store(place, out, total, channels):
-    blocks, times, _, width, _ = out.shape
-    for block in range(blocks):
+    store(place, out, total, 0, total.shape[0] // unit, channels, width)
+
+
+def store(place, out, total, base, times, channels, width):
+    splits = channels // LANES
+    for block in range(out.shape[0]):
         member = (2 * place[0] + place[1] + OFFSETS[block]) % 4
         for time in range(times):
-            at = (time * blocks + block) * PAD
-            for out_row in range(2):
-                lanes = slice(out_row * channels, (out_row + 1) * channels)
-                value = total[at : at + PAD, lanes].astype(jnp.bfloat16)
-                out[member, time, out_row] = value[:width]
+            at = (time * out.shape[0] + block) * PAD
+            for tile in range(2 * splits):
+                first = base + (time * 2 * splits + tile) * width
+                value = total[at : at + width, tile * LANES : (tile + 1) * LANES]
+                out[member, first : first + width, :] = value.astype(jnp.bfloat16)
+
+
+def add_kernel(sizes, parts, *outs):
+    first = 0
+    for out, (times, splits, width) in zip(outs, sizes, strict=True):
+        for time in range(times):
+            for row in range(2):
+                for split in range(splits):
+                    rows = slice(first, first + width)
+                    total = parts[0, rows, :].astype(jnp.float32)
+                    for member in range(1, parts.shape[0]):
+                        total = total + parts[member, rows, :].astype(jnp.float32)
+                    lanes = slice(split * LANES, (split + 1) * LANES)
+                    out[time, row, :, lanes] = total.astype(jnp.bfloat16)
+                    first += width
 
 
 def backward_kernel(
-    layout, place, rows, own, other, slope, grads, mix_w, partial, evens, odds, up_w, total
+    layout, width, place, rows, own, other, out, base, slope, mix_w, partial, evens, odds, up_w, total
 ):
     up_tile, mix_tile = readers(layout, place, own, other)
     channels = rows.shape[1] // 6
@@ -248,7 +262,14 @@
             up_w[kt * 3 * LANES : (kt + 1) * 3 * LANES, :],
             preferred_element_type=jnp.float32,
         )
-    store(place, grads, total, splits * LANES)
+    store(place, out, total, base, count // unit, splits * LANES, width)
+
+
+def compute_kernel(
+    layout, width, base, place, frame_rows, cot_rows, own, other, out, slope, *scratch
+):
+    forward_kernel(layout, width, place, frame_rows, own, other, out, slope, *scratch[:6])
+    backward_kernel(layout, width, place, cot_rows, own, other, out, base, slope, *scratch[6:])
 
 
 def call(kernel, outs, scratch, flops, megabytes, place, *operands):
@@ -273,39 +294,44 @@
     return call(functools.partial(unfold_kernel, sizes), outs, [], 10**9, 14, place, own, other)
 
 
-def forward(layout, place, rows, own, other, width, channels):
+def compute(layout, place, frame_rows, cot_rows, own, other, width, channels, in_channels):
     blocks = own.shape[0]
     unit = blocks * PAD
-    times = 2 * (rows.shape[0] // unit - 3)
-    outs = (
-        jax.ShapeDtypeStruct((blocks, times, 2, width, channels), jnp.bfloat16),
-        jax.ShapeDtypeStruct(((times + 1) * unit, LANES), jnp.float32),
-    )
+    times = 2 * (frame_rows.shape[0] // unit - 3)
+    base = times * 2 * (channels // LANES) * width
+    rows = base + times * (in_channels // LANES) * width
     scratch = [
-        pltpu.VMEM((3 * LANES, rows.shape[1]), jnp.bfloat16),
-        pltpu.VMEM((rows.shape[0], 3 * LANES), jnp.float32),
+        pltpu.VMEM(((times + 1) * unit, LANES), jnp.float32),
+        pltpu.VMEM((3 * LANES, frame_rows.shape[1]), jnp.bfloat16),
+        pltpu.VMEM((frame_rows.shape[0], 3 * LANES), jnp.float32),
         pltpu.VMEM((unit, LANES), jnp.float32),
         pltpu.VMEM(((times + 2) * unit, 3 * LANES), jnp.bfloat16),
         pltpu.VMEM((2 * channels, 9 * LANES), jnp.bfloat16),
         pltpu.VMEM((times * unit, 2 * channels), jnp.float32),
-    ]
-    kernel = functools.partial(forward_kernel, layout)
-    return call(kernel, outs, scratch, 2 * 10**9, 14, place, rows, own, other)
-
-
-def backward(layout, place, rows, own, other, slope, unit, width, in_channels):
-    times = slope.shape[0] // unit
-    out = jax.ShapeDtypeStruct((unit // PAD, times // 2, 2, width, in_channels), jnp.bfloat16)
-    scratch = [
-        pltpu.VMEM((rows.shape[1], 3 * LANES), jnp.bfloat16),
-        pltpu.VMEM((rows.shape[0], 3 * LANES), jnp.float32),
-        pltpu.VMEM(((times + 1) // 2 * unit, 3 * LANES), jnp.bfloat16),
+        pltpu.VMEM((cot_rows.shape[1], 3 * LANES), jnp.bfloat16),
+        pltpu.VMEM((cot_rows.shape[0], 3 * LANES), jnp.float32),
+        pltpu.VMEM((times // 2 * unit + unit, 3 * LANES), jnp.bfloat16),
         pltpu.VMEM((times // 2 * unit, 3 * LANES), jnp.bfloat16),
         pltpu.VMEM((9 * LANES, 2 * in_channels), jnp.bfloat16),
         pltpu.VMEM((times // 2 * unit, 2 * in_channels), jnp.float32),
     ]
-    kernel = functools.partial(backward_kernel, layout)
-    return call(kernel, out, scratch, 2 * 10**9, 14, place, rows, own, other, slope)
+    kernel = functools.partial(compute_kernel, layout, width, base)
+    out = jax.ShapeDtypeStruct((blocks, rows, LANES), jnp.bfloat16)
+    return call(kernel, out, scratch, 4 * 10**9, 32, place, frame_rows, cot_rows, own, other)
+
+
+def add_parts(parts, sizes):
+    space = pl.BlockSpec(memory_space=pltpu.VMEM)
+    return pl.pallas_call(
+        functools.partial(add_kernel, sizes),
+        out_shape=tuple(
+            jax.ShapeDtypeStruct((times, 2, width, splits * LANES), jnp.bfloat16)
+            for times, splits, width in sizes
+        ),
+        in_specs=[space],
+        out_specs=(space, space),
+        compiler_params=pltpu.CompilerParams(vmem_limit_bytes=8 * 2**20),
+    )(parts)
 
 
 def ring(array, by):
@@ -355,11 +381,17 @@
     ).astype(jnp.bfloat16)
     mix_part = mix_part.reshape(9, 2, 2, 2 * part).transpose(0, 2, 1, 3).reshape(-1, 2, LANES)
 
-    planes = spread(jnp.concatenate((up_part, mix_part), axis=0), "z")
-    fields = jnp.concatenate(
-        (shift(frames[-2:], PLANES, 1), frames, shift(frames[:1], PLANES, -1)), axis=0
-    )
-    cots = jnp.concatenate((cotangent, shift(cotangent[:3], PLANES, -1)), axis=0)
+    payload, *halos = lax.optimization_barrier(
+        (
+            jnp.concatenate((up_part, mix_part), axis=0),
+            shift(frames[-2:], PLANES, 1),
+            shift(frames[:1], PLANES, -1),
+            shift(cotangent[:3], PLANES, -1),
+        )
+    )
+    planes = spread(payload, "z")
+    fields = jnp.concatenate((halos[0], frames, halos[1]), axis=0)
+    cots = jnp.concatenate((cotangent, halos[2]), axis=0)
     block = jnp.concatenate((flat(fields), flat(cots)), axis=0)
     blocks = (block, ring(block, 1), ring(block, -1), ring(block, 2))
     planes, block = lax.optimization_barrier((planes, block))
@@ -378,16 +410,12 @@
         (cots.shape[0], splits, width),
     )
     frame_rows, cot_rows = unfold(place, blocks, others, sizes)
-    decoded_parts, slope = forward(layout, place, frame_rows, own, other, width, out_channels)
-    decoded_parts = lax.all_to_all(decoded_parts, RING, 0, 0, tiled=True)
-    grad_parts = backward(
-        layout, place, cot_rows, own, other, slope, nx * PAD, width, in_channels
-    )
-    decoded_parts, grad_parts = lax.optimization_barrier((decoded_parts, grad_parts))
-    grad_parts = lax.all_to_all(grad_parts, RING, 0, 0, tiled=True)
-    decoded = jnp.sum(decoded_parts.astype(jnp.float32), axis=0)
-    frames_grad = jnp.sum(grad_parts.astype(jnp.float32), axis=0)
-    return decoded.astype(jnp.bfloat16), frames_grad.astype(jnp.bfloat16)
+    parts = compute(
+        layout, place, frame_rows, cot_rows, own, other, width, out_channels, in_channels
+    )
+    parts = lax.all_to_all(parts, RING, 0, 0, tiled=True)
+    outs = ((2 * frame_count, splits, width), (frame_count, in_channels // LANES, width))
+    return add_parts(parts, outs)
 
 
 def solution(mesh):

time: 119 us -> 114 us (0.958)
  the two profiles are of different devices: /device:TPU:1 before, /device:TPU:32 now
where the time goes in v2:
time: 114 us
  starting transfers between devices  46.1 us (40%)
  waiting for transfers between devices  22.1 us (19%)
  blocking collectives  18.3 us (16%)
  Pallas kernels  16.8 us (15%)
  local copies, waits for them, and re-layouts  7.15 us (6%)
  other arithmetic  1.8 us (2%)
    all_to_all x2, starting transfers between devices, spread(): lax.all_to_all(jnp.broadcast_to(array, (count, *array.shape)), axis, 0, 0...  20.8 us
    all_to_all x2, waiting for transfers between devices, spread(): lax.all_to_all(jnp.broadcast_to(array, (count, *array.shape)), axis, 0, 0...  19 us
    all_to_all x1, blocking collectives, shards(): parts = lax.all_to_all(parts, RING, 0, 0, tiled=True)  18.3 us
    pallas_call x2, Pallas kernels, call(): pl.pallas_call(kernel, out_shape=outs, in_specs=[pl.BlockSpec(memory_spac...  16.1 us
    ppermute x3, starting transfers between devices, ring(): return lax.ppermute(array, RING, [(i, (i + by) % 4) for i in range(4)])  8.97 us
    ppermute x3, starting transfers between devices, shift(): return lax.ppermute(array, axis, pairs)  7.82 us
    ppermute x1, starting transfers between devices, shards(): mix_other = lax.ppermute(raw_mix, RING, [(0, 3), (3, 0), (1, 2), (2, 1)])  4.67 us
    ppermute x2, starting transfers between devices, swap(): return lax.ppermute(array, 'core', [(0, 1), (1, 0)])  3.83 us
  transfers between devices with their start and end apart: 11, of which 3 were waited for; matrix products, arithmetic and copies ran while one was open for 6% of the time, Pallas kernels for 5%

profile of v2, /device:TPU:32, one launch (start us, length us, event | category | flops | bytes accessed | tf_op | source)
XLA Modules:
  0.0 113.6 jit_solution(12474501351443902714)
XLA Ops:
  0.6 0.0 copy-start
  0.6 0.8 reshape.48
  1.5 4.7 %collective-permute-start = (bf16[54,2,128]{2,0,1:T(8,128)(2,1)S(1)}, bf16[54,2,128]{2,0,1:T(8,128)(2,1)S(1)}, u32[]{:S(2)}, u32[]{:S(2)}) collective-permute-start(bf16[54,2,128]{2,0,1:T(8,128)(2,1)S(1)} %bitcast.52), channel_id=1, source_target_pairs={{0,66},{66,0},{2,64},{64,2},{1,67},{67,1},{3,65},{65,3},{4,70},{70... | collective-permute-start | bytes 82952 | tf_op jit(solution)/shard_map/ppermute | solution.py:358
  6.1 0.9 slice.15
  7.0 3.8 %collective-permute-start.1 = (bf16[2,2,24,384]{3,2,1,0:T(8,128)(2,1)S(1)}, bf16[2,2,24,384]{3,2,1,0:T(8,128)(2,1)S(1)}, u32[]{:S(2)}, u32[]{:S(2)}) collective-permute-start(bf16[2,2,24,384]{3,2,1,0:T(8,128)(2,1)S(1)} %slice.15), channel_id=1, source_target_pairs={{0,4},{4,8},{8,12},{12,16},{16,20},{20,24},{24,28},{28,32},{32,36}... | collective-permute-start | bytes 221192 | tf_op jit(solution)/shard_map/ppermute | solution.py:21
  10.8 0.9 slice.17
  11.7 2.1 %collective-permute-start.3 = (bf16[3,2,24,256]{3,2,1,0:T(8,128)(2,1)S(1)}, bf16[3,2,24,256]{3,2,1,0:T(8,128)(2,1)S(1)}, u32[]{:S(2)}, u32[]{:S(2)}) collective-permute-start(bf16[3,2,24,256]{3,2,1,0:T(8,128)(2,1)S(1)} %slice.17), channel_id=1, source_target_pairs={{4,0},{8,4},{12,8},{16,12},{20,16},{24,20},{28,24},{32,28},{36,32}... | collective-permute-start | bytes 221192 | tf_op jit(solution)/shard_map/ppermute | solution.py:21
  13.8 0.8 slice.16
  14.6 1.9 %collective-permute-start.2 = (bf16[1,2,24,384]{3,2,1,0:T(8,128)(2,1)S(1)}, bf16[1,2,24,384]{3,2,1,0:T(8,128)(2,1)S(1)}, u32[]{:S(2)}, u32[]{:S(2)}) collective-permute-start(bf16[1,2,24,384]{3,2,1,0:T(8,128)(2,1)S(1)} %slice.16), channel_id=1, source_target_pairs={{4,0},{8,4},{12,8},{16,12},{20,16},{24,20},{28,24},{32,28},{36,32}... | collective-permute-start | bytes 110600 | tf_op jit(solution)/shard_map/ppermute | solution.py:21
  16.6 0.0 copy-done
  16.6 0.1 dynamic-slice_reduce_fusion
  16.8 0.0 collective-permute-done
  16.9 0.0 copy-start.1
  16.9 0.3 fusion
  17.2 0.0 copy-start.5
  17.4 3.1 %collective-permute-done.2 = bf16[1,2,24,384]{3,2,1,0:T(8,128)(2,1)S(1)} collective-permute-done((bf16[1,2,24,384]{3,2,1,0:T(8,128)(2,1)S(1)}, bf16[1,2,24,384]{3,2,1,0:T(8,128)(2,1)S(1)}, u32[]{:S(2)}, u32[]{:S(2)}) %collective-permute-start.2) | collective-permute-done | bytes 36896 | tf_op jit(solution)/shard_map/ppermute | solution.py:21
  20.5 0.0 collective-permute-done.1
  20.5 0.0 collective-permute-done.3
  20.5 0.9 broadcast_in_dim.6
  21.4 16.3 %all-to-all-start = ((bf16[16,39,2,128]{3,2,1,0:T(2,128)(2,1)}), bf16[16,39,2,128]{3,2,1,0:T(2,128)(2,1)S(1)}, u32[]{:S(2)}, u32[]{:S(2)}) async-start(bf16[16,39,2,128]{3,2,1,0:T(2,128)(2,1)} %broadcast_in_dim.6), calls=%async_computation | async-start | bytes 638976 | tf_op jit(solution)/shard_map/all_to_all | solution.py:30
  37.7 0.1 reshape.52
  37.8 0.0 copy-done.5
  37.9 0.1 fusion.51
  38.0 2.1 %collective-permute-start.4 = (bf16[1728,128]{1,0:T(8,128)(2,1)S(1)}, bf16[1728,128]{1,0:T(8,128)(2,1)S(1)}, u32[]{:S(2)}, u32[]{:S(2)}) collective-permute-start(bf16[1728,128]{1,0:T(8,128)(2,1)S(1)} %get-tuple-element.17), channel_id=1, source_target_pairs={{0,2},{2,64},{64,66},{66,0},{1,3},{3,65},{65,67},{67,1},{4,6},{6,6... | collective-permute-start | bytes 1327112 | tf_op jit(solution)/shard_map/ppermute | solution.py:338
  40.1 4.9 %collective-permute-start.5 = (bf16[1728,128]{1,0:T(8,128)(2,1)S(1)}, bf16[1728,128]{1,0:T(8,128)(2,1)S(1)}, u32[]{:S(2)}, u32[]{:S(2)}) collective-permute-start(bf16[1728,128]{1,0:T(8,128)(2,1)S(1)} %get-tuple-element.17), channel_id=1, source_target_pairs={{0,66},{2,0},{64,2},{66,64},{1,67},{3,1},{65,3},{67,65},{4,70},{6,... | collective-permute-start | bytes 1327112 | tf_op jit(solution)/shard_map/ppermute | solution.py:338
  45.0 1.9 %collective-permute-start.6 = (bf16[1728,128]{1,0:T(8,128)(2,1)S(1)}, bf16[1728,128]{1,0:T(8,128)(2,1)S(1)}, u32[]{:S(2)}, u32[]{:S(2)}) collective-permute-start(bf16[1728,128]{1,0:T(8,128)(2,1)S(1)} %get-tuple-element.17), channel_id=1, source_target_pairs={{0,64},{2,66},{64,0},{66,2},{1,65},{3,67},{65,1},{67,3},{4,68},{6,... | collective-permute-start | bytes 1327112 | tf_op jit(solution)/shard_map/ppermute | solution.py:338
  47.0 8.5 %all-to-all-done = bf16[16,39,2,128]{3,2,1,0:T(2,128)(2,1)S(1)} async-done(((bf16[16,39,2,128]{3,2,1,0:T(2,128)(2,1)}), bf16[16,39,2,128]{3,2,1,0:T(2,128)(2,1)S(1)}, u32[]{:S(2)}, u32[]{:S(2)}) %all-to-all-start) | async-done | bytes 319520 | tf_op jit(solution)/shard_map/all_to_all | solution.py:30
  55.4 0.1 slice_bitcast_fusion
  55.6 0.1 copy.35
  55.7 1.2 %broadcast_in_dim.7 = bf16[4,1248,128]{2,1,0:T(8,128)(2,1)} broadcast(bf16[1248,128]{1,0:T(8,128)(2,1)S(1)} %pad_maximum_fusion.2), dimensions={1,2} | broadcast | bytes 1597440 | tf_op jit(solution)/shard_map/broadcast_in_dim | solution.py:31
  57.0 4.5 %all-to-all-start.1 = ((bf16[4,1248,128]{2,1,0:T(8,128)(2,1)}), bf16[4,1248,128]{2,1,0:T(8,128)(2,1)S(1)}, u32[]{:S(2)}, u32[]{:S(2)}) async-start(bf16[4,1248,128]{2,1,0:T(8,128)(2,1)} %broadcast_in_dim.7), calls=%async_computation.1 | async-start | bytes 2555904 | tf_op jit(solution)/shard_map/all_to_all | solution.py:30
  61.4 0.0 collective-permute-done.4
  61.4 0.0 collective-permute-done.5
  61.5 0.0 collective-permute-done.6
  61.5 0.7 copy-done.2
  62.2 0.1 copy-done.3
  62.3 0.1 copy-done.4
  62.5 1.5 %pad_maximum_fusion.own = bf16[4,1728,128]{2,1,0:T(8,128)(2,1)S(1)} fusion(bf16[1,1728,128]{2,1,0:T(8,128)(2,1)} %bitcast.51, bf16[1,1728,128]{2,1,0:T(8,128)(2,1)} %bitcast.50, bf16[1,1728,128]{2,1,0:T(8,128)(2,1)} %bitcast.49, bf16[1,1728,128]{2,1,0:T(8,128)(2,1)S(1)} %get-tuple-element.16), kind=kLoop, calls=%fused_computation.4 | loop fusion | flops 2654208 | bytes 3538944 | tf_op jit(solution)/shard_map/stack | solution.py:398
  64.0 1.9 %collective-permute-start.7 = (bf16[4,1728,128]{2,1,0:T(8,128)(2,1)S(1)}, bf16[4,1728,128]{2,1,0:T(8,128)(2,1)}, u32[]{:S(2)}, u32[]{:S(2)}) collective-permute-start(bf16[4,1728,128]{2,1,0:T(8,128)(2,1)S(1)} %pad_maximum_fusion.own), channel_id=1, source_target_pairs={{0,1},{1,0},{2,3},{3,2},{4,5},{5,4},{6,7},{7,6},{8,9},{9,8},{10,11... | collective-permute-start | bytes 5308424 | tf_op jit(solution)/shard_map/ppermute | solution.py:25
  65.9 10.5 %all-to-all-done.1.own = bf16[4,1248,128]{2,1,0:T(8,128)(2,1)S(1)} async-done(((bf16[4,1248,128]{2,1,0:T(8,128)(2,1)}), bf16[4,1248,128]{2,1,0:T(8,128)(2,1)S(1)}, u32[]{:S(2)}, u32[]{:S(2)}) %all-to-all-start.1) | async-done | bytes 1277984 | tf_op jit(solution)/shard_map/all_to_all | solution.py:30
  76.4 1.9 %collective-permute-start.8 = (bf16[4,1248,128]{2,1,0:T(8,128)(2,1)S(1)}, bf16[4,1248,128]{2,1,0:T(8,128)(2,1)S(1)}, u32[]{:S(2)}, u32[]{:S(2)}) collective-permute-start(bf16[4,1248,128]{2,1,0:T(8,128)(2,1)S(1)} %all-to-all-done.1.own), channel_id=1, source_target_pairs={{0,1},{1,0},{2,3},{3,2},{4,5},{5,4},{6,7},{7,6},{8,9},{9,8},{10,11... | collective-permute-start | bytes 3833864 | tf_op jit(solution)/shard_map/ppermute | solution.py:25
  78.4 0.1 pad_add_fusion.place
  78.4 0.0 collective-permute-done.7.other
  78.4 5.4 %shard_map.59 = (bf16[768,2304]{1,0:T(8,128)(2,1)S(1)}, bf16[1152,1536]{1,0:T(8,128)(2,1)S(1)}) custom-call(s32[3]{0:T(128)S(1)} %pad_add_fusion.place, bf16[4,1728,128]{2,1,0:T(8,128)(2,1)S(1)} %pad_maximum_fusion.own, bf16[4,1728,128]{2,1,0:T(8,128)(2,1)} %collective-permute-done.7.other), custom_call_target="tpu_custom_call" | custom-call | flops 1000000000 | bytes 8388608 | tf_op jit(solution)/shard_map/pallas_call | solution.py:277
  83.8 0.0 collective-permute-done.8.other
  83.8 10.7 %shard_map.60 = bf16[4,1008,128]{2,1,0:T(8,128)(2,1)S(1)} custom-call(s32[3]{0:T(128)S(1)} %pad_add_fusion.place, bf16[768,2304]{1,0:T(8,128)(2,1)S(1)} %get-tuple-element.12.frame_rows, bf16[1152,1536]{1,0:T(8,128)(2,1)S(1)} %get-tuple-element.13.cot_rows, bf16[4,1248,128]{2,1,0:T(8,128)(2,1)S(1)} %all-to-all-done.1.own, ...), custom_call_target="tpu_custom_call" | custom-call | flops 4000000000 | bytes 8388608 | tf_op jit(solution)/shard_map/pallas_call | solution.py:277
  94.5 18.3 %all_to_all.15.parts = bf16[4,1008,128]{2,1,0:T(8,128)(2,1)S(1)} all-to-all(bf16[4,1008,128]{2,1,0:T(8,128)(2,1)S(1)} %shard_map.60), channel_id=1, replica_groups=mesh['y'=4,'xh'=2,'z'=16,'xl'=2,'core'=2] {'xh','xl'}, dimensions={0} | all-to-all | bytes 2064384 | tf_op jit(solution)/shard_map/all_to_all | solution.py:416
  112.8 0.8 shard_map.61
  (25 shorter events, 0.4 us)
Async XLA Ops:
  0.6 16.0 %copy-start = (bf16[10368,2]{0,1:T(2,128)(2,1)S(1)}, bf16[10368,2]{0,1:T(2,128)(2,1)}, u32[]{:S(2)}) copy-start(bf16[10368,2]{0,1:T(2,128)(2,1)} %param.5) | copy-start | bytes 124420
  1.5 15.4 %collective-permute-start = (bf16[54,2,128]{2,0,1:T(8,128)(2,1)S(1)}, bf16[54,2,128]{2,0,1:T(8,128)(2,1)S(1)}, u32[]{:S(2)}, u32[]{:S(2)}) collective-permute-start(bf16[54,2,128]{2,0,1:T(8,128)(2,1)S(1)} %bitcast.52), channel_id=1, source_target_pairs={{0,66},{66,0},{2,64},{64,2},{1,67},{67,1},{3,65},{65,3},{4,70},{70... | collective-permute-start | bytes 82952 | tf_op jit(solution)/shard_map/ppermute | solution.py:358
  7.0 13.4 %collective-permute-start.1 = (bf16[2,2,24,384]{3,2,1,0:T(8,128)(2,1)S(1)}, bf16[2,2,24,384]{3,2,1,0:T(8,128)(2,1)S(1)}, u32[]{:S(2)}, u32[]{:S(2)}) collective-permute-start(bf16[2,2,24,384]{3,2,1,0:T(8,128)(2,1)S(1)} %slice.15), channel_id=1, source_target_pairs={{0,4},{4,8},{8,12},{12,16},{16,20},{20,24},{24,28},{28,32},{32,36}... | collective-permute-start | bytes 221192 | tf_op jit(solution)/shard_map/ppermute | solution.py:21
  11.7 8.7 %collective-permute-start.3 = (bf16[3,2,24,256]{3,2,1,0:T(8,128)(2,1)S(1)}, bf16[3,2,24,256]{3,2,1,0:T(8,128)(2,1)S(1)}, u32[]{:S(2)}, u32[]{:S(2)}) collective-permute-start(bf16[3,2,24,256]{3,2,1,0:T(8,128)(2,1)S(1)} %slice.17), channel_id=1, source_target_pairs={{4,0},{8,4},{12,8},{16,12},{20,16},{24,20},{28,24},{32,28},{36,32}... | collective-permute-start | bytes 221192 | tf_op jit(solution)/shard_map/ppermute | solution.py:21
  14.6 5.8 %collective-permute-start.2 = (bf16[1,2,24,384]{3,2,1,0:T(8,128)(2,1)S(1)}, bf16[1,2,24,384]{3,2,1,0:T(8,128)(2,1)S(1)}, u32[]{:S(2)}, u32[]{:S(2)}) collective-permute-start(bf16[1,2,24,384]{3,2,1,0:T(8,128)(2,1)S(1)} %slice.16), channel_id=1, source_target_pairs={{4,0},{8,4},{12,8},{16,12},{20,16},{24,20},{28,24},{32,28},{36,32}... | collective-permute-start | bytes 110600 | tf_op jit(solution)/shard_map/ppermute | solution.py:21
  16.9 20.8 %copy-start.1 = (bf16[3,2,24,384]{3,2,1,0:T(8,128)(2,1)S(1)}, bf16[3,2,24,384]{3,2,1,0:T(8,128)(2,1)}, u32[]{:S(2)}) copy-start(bf16[3,2,24,384]{3,2,1,0:T(8,128)(2,1)} %param.4) | copy-start | bytes 331780
  17.2 20.6 %copy-start.5 = (bf16[6,2,24,256]{3,2,1,0:T(8,128)(2,1)S(1)}, bf16[6,2,24,256]{3,2,1,0:T(8,128)(2,1)}, u32[]{:S(2)}) copy-start(bf16[6,2,24,256]{3,2,1,0:T(8,128)(2,1)} %param.7) | copy-start | bytes 442372
  21.4 34.1 %all-to-all-start = ((bf16[16,39,2,128]{3,2,1,0:T(2,128)(2,1)}), bf16[16,39,2,128]{3,2,1,0:T(2,128)(2,1)S(1)}, u32[]{:S(2)}, u32[]{:S(2)}) async-start(bf16[16,39,2,128]{3,2,1,0:T(2,128)(2,1)} %broadcast_in_dim.6), calls=%async_computation | async-start | bytes 638976 | tf_op jit(solution)/shard_map/all_to_all | solution.py:30
  38.0 23.5 %collective-permute-start.4 = (bf16[1728,128]{1,0:T(8,128)(2,1)S(1)}, bf16[1728,128]{1,0:T(8,128)(2,1)S(1)}, u32[]{:S(2)}, u32[]{:S(2)}) collective-permute-start(bf16[1728,128]{1,0:T(8,128)(2,1)S(1)} %get-tuple-element.17), channel_id=1, source_target_pairs={{0,2},{2,64},{64,66},{66,0},{1,3},{3,65},{65,67},{67,1},{4,6},{6,6... | collective-permute-start | bytes 1327112 | tf_op jit(solution)/shard_map/ppermute | solution.py:338
  40.1 21.3 %collective-permute-start.5 = (bf16[1728,128]{1,0:T(8,128)(2,1)S(1)}, bf16[1728,128]{1,0:T(8,128)(2,1)S(1)}, u32[]{:S(2)}, u32[]{:S(2)}) collective-permute-start(bf16[1728,128]{1,0:T(8,128)(2,1)S(1)} %get-tuple-element.17), channel_id=1, source_target_pairs={{0,66},{2,0},{64,2},{66,64},{1,67},{3,1},{65,3},{67,65},{4,70},{6,... | collective-permute-start | bytes 1327112 | tf_op jit(solution)/shard_map/ppermute | solution.py:338
  45.0 16.4 %collective-permute-start.6 = (bf16[1728,128]{1,0:T(8,128)(2,1)S(1)}, bf16[1728,128]{1,0:T(8,128)(2,1)S(1)}, u32[]{:S(2)}, u32[]{:S(2)}) collective-permute-start(bf16[1728,128]{1,0:T(8,128)(2,1)S(1)} %get-tuple-element.17), channel_id=1, source_target_pairs={{0,64},{2,66},{64,0},{66,2},{1,65},{3,67},{65,1},{67,3},{4,68},{6,... | collective-permute-start | bytes 1327112 | tf_op jit(solution)/shard_map/ppermute | solution.py:338
  57.0 19.5 %all-to-all-start.1 = ((bf16[4,1248,128]{2,1,0:T(8,128)(2,1)}), bf16[4,1248,128]{2,1,0:T(8,128)(2,1)S(1)}, u32[]{:S(2)}, u32[]{:S(2)}) async-start(bf16[4,1248,128]{2,1,0:T(8,128)(2,1)} %broadcast_in_dim.7), calls=%async_computation.1 | async-start | bytes 2555904 | tf_op jit(solution)/shard_map/all_to_all | solution.py:30
  61.4 0.8 copy-start.2
  61.4 0.9 copy-start.3
  61.5 1.0 copy-start.4
  64.0 14.4 %collective-permute-start.7 = (bf16[4,1728,128]{2,1,0:T(8,128)(2,1)S(1)}, bf16[4,1728,128]{2,1,0:T(8,128)(2,1)}, u32[]{:S(2)}, u32[]{:S(2)}) collective-permute-start(bf16[4,1728,128]{2,1,0:T(8,128)(2,1)S(1)} %pad_maximum_fusion.own), channel_id=1, source_target_pairs={{0,1},{1,0},{2,3},{3,2},{4,5},{5,4},{6,7},{7,6},{8,9},{9,8},{10,11... | collective-permute-start | bytes 5308424 | tf_op jit(solution)/shard_map/ppermute | solution.py:25
  76.4 7.4 %collective-permute-start.8 = (bf16[4,1248,128]{2,1,0:T(8,128)(2,1)S(1)}, bf16[4,1248,128]{2,1,0:T(8,128)(2,1)S(1)}, u32[]{:S(2)}, u32[]{:S(2)}) collective-permute-start(bf16[4,1248,128]{2,1,0:T(8,128)(2,1)S(1)} %all-to-all-done.1.own), channel_id=1, source_target_pairs={{0,1},{1,0},{2,3},{3,2},{4,5},{5,4},{6,7},{7,6},{8,9},{9,8},{10,11... | collective-permute-start | bytes 3833864 | tf_op jit(solution)/shard_map/ppermute | solution.py:25

commit v3 on v2

--- a/solution.py
+++ b/solution.py
@@ -2,6 +2,7 @@
 
 import jax
 import jax.numpy as jnp
+import numpy as np
 from jax import lax
 from jax.experimental import pallas as pl
 from jax.experimental.pallas import tpu as pltpu
@@ -38,29 +39,26 @@
     return pltpu.roll(rows, rows.shape[0] - by, 0)
 
 
-def unfold_kernel(sizes, place, own, other, frame_rows, cot_rows):
-    _, xl, core = place[0], place[1], place[2]
-    blocks, base = own.shape[0], 0
-    for out, (times, splits, width) in zip((frame_rows, cot_rows), sizes, strict=True):
-
-        def step(at, _, out=out, splits=splits, width=width, base=base):
-            time, block = at // blocks, at % blocks
-            side = (xl + (block + 1) // 2) % 2
-            partner = jnp.where(xl == 0, (block + 2) % 4, block + 1 - 2 * (block % 2))
-            left = jnp.where(core == 1, block, partner)
-            right = jnp.where(core == 0, block, partner)
-            has_left = 2 * side + core > 0
-            has_right = 2 * side + core < 3
-            target = pl.ds(pl.multiple_of(at * PAD, PAD), PAD)
-            for row in range(2):
-                for split in range(splits):
-                    first = base + ((time * 2 + row) * splits + split) * width
-                    rows = pl.ds(pl.multiple_of(first, 8), width)
-                    head = pl.ds(pl.multiple_of(first, 8), 8)
-                    tail = pl.ds(pl.multiple_of(first + width - 8, 8), 8)
-                    low = other[left, tail, :].astype(jnp.float32)
-                    middle = own[block, rows, :].astype(jnp.float32)
-                    high = other[right, head, :].astype(jnp.float32)
+def unfold_kernel(sizes, width, place, own, other, frame_rows, cot_rows):
+    xl, core = place[1], place[2]
+    blocks = own.shape[0]
+
+    def step(block, _):
+        side = (xl + (block + 1) // 2) % 2
+        partner = jnp.where(xl == 0, (block + 2) % 4, block + 1 - 2 * (block % 2))
+        left = jnp.where(core == 1, block, partner)
+        right = jnp.where(core == 0, block, partner)
+        has_left = 2 * side + core > 0
+        has_right = 2 * side + core < 3
+        for out, (starts, splits) in zip((frame_rows, cot_rows), sizes, strict=True):
+            for time, start in enumerate(starts):
+                target = pl.ds(pl.multiple_of((time * blocks + block) * PAD, PAD), PAD)
+                for tile in range(2 * splits):
+                    row, split = tile // splits, tile % splits
+                    first = start + tile * width
+                    low = other[left, first + width - 8 : first + width, :].astype(jnp.float32)
+                    middle = own[block, first : first + width, :].astype(jnp.float32)
+                    high = other[right, first : first + 8, :].astype(jnp.float32)
                     low = jnp.where(has_left, low, 0.0)
                     high = jnp.where(has_right, high, 0.0)
                     chunk = jnp.concatenate((low, middle, high), axis=0)
@@ -68,10 +66,9 @@
                         lane = ((row * 3 + tap) * splits + split) * LANES
                         moved = chunk[6 + tap : 6 + tap + PAD].astype(jnp.bfloat16)
                         out[target, lane : lane + LANES] = moved
-            return 0
-
-        lax.fori_loop(0, times * blocks, step, 0)
-        base += times * 2 * splits * width
+        return 0
+
+    lax.fori_loop(0, blocks, step, 0)
 
 
 def readers(layout, place, own, other):
@@ -285,13 +282,35 @@
     )(place, *operands)
 
 
-def unfold(place, own, other, sizes):
+def unfold(place, own, other, sizes, width):
     unit = own.shape[0] * PAD
     outs = tuple(
-        jax.ShapeDtypeStruct((times * unit, 6 * splits * LANES), jnp.bfloat16)
-        for times, splits, _ in sizes
+        jax.ShapeDtypeStruct((len(starts) * unit, 6 * splits * LANES), jnp.bfloat16)
+        for starts, splits in sizes
     )
-    return call(functools.partial(unfold_kernel, sizes), outs, [], 10**9, 14, place, own, other)
+    kernel = functools.partial(unfold_kernel, sizes, width)
+    return call(kernel, outs, [], 10**9, 14, place, own, other)
+
+
+def beside(blocks, xh, z, by):
+    axes = ("y", "xh", "z", "xl")
+    dims = tuple(lax.axis_size(axis) for axis in axes)
+    edge = dims[2] - 1 if by > 0 else 0
+    near, wrap = [], []
+    for target in np.ndindex(*dims):
+        ty, tx, tz, tl = target
+        to = int(np.ravel_multi_index(target, dims))
+        if tz != edge:
+            near.append((int(np.ravel_multi_index((ty, tx, tz + by, tl), dims)), to))
+            continue
+        far = dims[2] - 1 - edge
+        near.append((int(np.ravel_multi_index((ty, 1 - tx, far, tl), dims)), to))
+        if 0 <= ty + by < dims[0]:
+            wrap.append((int(np.ravel_multi_index((ty + by, 1 - tx, far, tl), dims)), to))
+    beyond = lax.ppermute(blocks, axes, wrap)
+    side = (xh * 2 + lax.axis_index("xl") + jnp.array(OFFSETS)) % 4 // 2
+    turned = (z == edge) & (side == (1 if by > 0 else 0))
+    return jnp.where(turned[:, None, None], beyond, lax.ppermute(blocks, axes, near))
 
 
 def compute(layout, place, frame_rows, cot_rows, own, other, width, channels, in_channels):
@@ -381,22 +400,33 @@
     ).astype(jnp.bfloat16)
     mix_part = mix_part.reshape(9, 2, 2, 2 * part).transpose(0, 2, 1, 3).reshape(-1, 2, LANES)
 
-    payload, *halos = lax.optimization_barrier(
+    frame_size, cot_size = 2 * (in_channels // LANES) * width, 2 * splits * width
+    count = 2 * frame_count
+    block = jnp.concatenate((flat(cotangent[3:]), flat(cotangent[:3]), flat(frames)), axis=0)
+    payload, *rest = lax.optimization_barrier(
         (
             jnp.concatenate((up_part, mix_part), axis=0),
-            shift(frames[-2:], PLANES, 1),
-            shift(frames[:1], PLANES, -1),
-            shift(cotangent[:3], PLANES, -1),
+            ring(block, 1),
+            ring(block, -1),
+            ring(block, 2),
         )
     )
     planes = spread(payload, "z")
-    fields = jnp.concatenate((halos[0], frames, halos[1]), axis=0)
-    cots = jnp.concatenate((cotangent, halos[2]), axis=0)
-    block = jnp.concatenate((flat(fields), flat(cots)), axis=0)
-    blocks = (block, ring(block, 1), ring(block, -1), ring(block, 2))
-    planes, block = lax.optimization_barrier((planes, block))
-    blocks = jnp.stack(blocks)
+    blocks = jnp.stack((block, *rest))
+    z = lax.axis_index("z")
+    early = (count - 3) * cot_size
+    following = beside(blocks[:, early : count * cot_size + frame_size], xh, z, 1)
+    previous = beside(blocks[:, block.shape[0] - 2 * frame_size :], xh, z, -1)
+    blocks = jnp.concatenate((blocks, following, previous), axis=1)
     others = swap(blocks)
+    first = block.shape[0]
+    last = first + 3 * cot_size + frame_size
+    cot_starts = [early + time * cot_size for time in range(3)]
+    cot_starts += [time * cot_size for time in range(count - 3)]
+    cot_starts += [first + time * cot_size for time in range(3)]
+    frame_starts = [last + time * frame_size for time in range(2)]
+    frame_starts += [count * cot_size + time * frame_size for time in range(frame_count)]
+    frame_starts += [first + 3 * cot_size]
 
     up_rows = planes[:, :up_pairs].transpose(1, 2, 0, 3).reshape(-1, LANES)
     mix_rows = planes[:, up_pairs:].transpose(1, 0, 2, 3).reshape(-1, LANES)
@@ -405,16 +435,13 @@
     layout = (nz, up_half, up_count, up_rows.shape[0])
 
     place = jnp.stack((xh, xl, core))
-    sizes = (
-        (fields.shape[0], in_channels // LANES, width),
-        (cots.shape[0], splits, width),
-    )
-    frame_rows, cot_rows = unfold(place, blocks, others, sizes)
+    sizes = ((tuple(frame_starts), in_channels // LANES), (tuple(cot_starts), splits))
+    frame_rows, cot_rows = unfold(place, blocks, others, sizes, width)
     parts = compute(
         layout, place, frame_rows, cot_rows, own, other, width, out_channels, in_channels
     )
     parts = lax.all_to_all(parts, RING, 0, 0, tiled=True)
-    outs = ((2 * frame_count, splits, width), (frame_count, in_channels // LANES, width))
+    outs = ((count, splits, width), (frame_count, in_channels // LANES, width))
     return add_parts(parts, outs)
 
 

time: 114 us -> 130 us (1.14)
  the two profiles are of different devices: /device:TPU:32 before, /device:TPU:1 now
where the time goes in v3:
time: 130 us
  starting transfers between devices  55.1 us (42%)
  waiting for transfers between devices  31.6 us (24%)
  blocking collectives  18.2 us (14%)
  Pallas kernels  15.2 us (12%)
  local copies, waits for them, and re-layouts  5.52 us (4%)
  other arithmetic  2.58 us (2%)
    all_to_all x2, starting transfers between devices, spread(): lax.all_to_all(jnp.broadcast_to(array, (count, *array.shape)), axis, 0, 0...  20.3 us
    all_to_all x1, blocking collectives, shards(): parts = lax.all_to_all(parts, RING, 0, 0, tiled=True)  18.2 us
    ppermute x2, waiting for transfers between devices, beside(): lax.ppermute(blocks, axes, near)  17.5 us
    pallas_call x2, Pallas kernels, call(): pl.pallas_call(kernel, out_shape=outs, in_specs=[pl.BlockSpec(memory_spac...  14.4 us
    ppermute x2, starting transfers between devices, beside(): lax.ppermute(blocks, axes, near)  11.8 us
    ppermute x3, starting transfers between devices, ring(): return lax.ppermute(array, RING, [(i, (i + by) % 4) for i in range(4)])  10.8 us
    all_to_all x2, waiting for transfers between devices, spread(): lax.all_to_all(jnp.broadcast_to(array, (count, *array.shape)), axis, 0, 0...  10.7 us
    ppermute x2, starting transfers between devices, swap(): return lax.ppermute(array, 'core', [(0, 1), (1, 0)])  8.21 us
  transfers between devices with their start and end apart: 12, of which 3 were waited for; matrix products, arithmetic and copies ran while one was open for 4% of the time, Pallas kernels for 3%

profile of v3, /device:TPU:1, one launch (start us, length us, event | category | flops | bytes accessed | tf_op | source)
XLA Modules:
  0.0 129.6 jit_solution(8667280640552366018)
XLA Ops:
  0.6 0.0 copy-start
  0.6 0.9 slice_bitcast_fusion.2
  1.6 0.9 reshape.58
  2.6 3.9 %collective-permute-start.1 = (bf16[1008,128]{1,0:T(8,128)(2,1)S(1)}, bf16[1008,128]{1,0:T(8,128)(2,1)S(1)}, u32[]{:S(2)}, u32[]{:S(2)}) collective-permute-start(bf16[1008,128]{1,0:T(8,128)(2,1)S(1)} %get-tuple-element.17), channel_id=1, source_target_pairs={{0,2},{2,64},{64,66},{66,0},{1,3},{3,65},{65,67},{67,1},{4,6},{6,6... | collective-permute-start | bytes 774152 | tf_op jit(solution)/shard_map/ppermute | solution.py:357
  6.6 3.2 %collective-permute-start.2 = (bf16[1008,128]{1,0:T(8,128)(2,1)S(1)}, bf16[1008,128]{1,0:T(8,128)(2,1)S(1)}, u32[]{:S(2)}, u32[]{:S(2)}) collective-permute-start(bf16[1008,128]{1,0:T(8,128)(2,1)S(1)} %get-tuple-element.17), channel_id=1, source_target_pairs={{0,66},{2,0},{64,2},{66,64},{1,67},{3,1},{65,3},{67,65},{4,70},{6,... | collective-permute-start | bytes 774152 | tf_op jit(solution)/shard_map/ppermute | solution.py:357
  9.8 3.6 %collective-permute-start.3 = (bf16[1008,128]{1,0:T(8,128)(2,1)S(1)}, bf16[1008,128]{1,0:T(8,128)(2,1)S(1)}, u32[]{:S(2)}, u32[]{:S(2)}) collective-permute-start(bf16[1008,128]{1,0:T(8,128)(2,1)S(1)} %get-tuple-element.17), channel_id=1, source_target_pairs={{0,64},{2,66},{64,0},{66,2},{1,65},{3,67},{65,1},{67,3},{4,68},{6,... | collective-permute-start | bytes 774152 | tf_op jit(solution)/shard_map/ppermute | solution.py:357
  13.4 0.8 reshape.62
  14.2 2.8 %collective-permute-start = (bf16[54,2,128]{2,0,1:T(8,128)(2,1)S(1)}, bf16[54,2,128]{2,0,1:T(8,128)(2,1)S(1)}, u32[]{:S(2)}, u32[]{:S(2)}) collective-permute-start(bf16[54,2,128]{2,0,1:T(8,128)(2,1)S(1)} %bitcast.65), channel_id=1, source_target_pairs={{0,66},{66,0},{2,64},{64,2},{1,67},{67,1},{3,65},{65,3},{4,70},{70... | collective-permute-start | bytes 82952 | tf_op jit(solution)/shard_map/ppermute | solution.py:377
  17.1 0.0 copy-done
  17.1 0.1 dynamic-slice_reduce_fusion
  17.3 3.4 %collective-permute-done = bf16[54,2,128]{2,0,1:T(8,128)(2,1)S(1)} collective-permute-done((bf16[54,2,128]{2,0,1:T(8,128)(2,1)S(1)}, bf16[54,2,128]{2,0,1:T(8,128)(2,1)S(1)}, u32[]{:S(2)}, u32[]{:S(2)}) %collective-permute-start) | collective-permute-done | bytes 27680 | tf_op jit(solution)/shard_map/ppermute | solution.py:377
  20.7 0.0 copy-start.4
  20.8 0.3 fusion
  21.2 0.0 collective-permute-done.1
  21.2 0.0 copy-start.1
  21.2 0.0 collective-permute-done.2
  21.2 0.0 copy-start.2
  21.2 0.0 collective-permute-done.3
  21.2 0.0 copy-start.3
  21.2 0.9 broadcast_in_dim.26
  22.2 16.1 %all-to-all-start = ((bf16[16,39,2,128]{3,2,1,0:T(2,128)(2,1)}), bf16[16,39,2,128]{3,2,1,0:T(2,128)(2,1)S(1)}, u32[]{:S(2)}, u32[]{:S(2)}) async-start(bf16[16,39,2,128]{3,2,1,0:T(2,128)(2,1)} %broadcast_in_dim.26), calls=%async_computation | async-start | bytes 638976 | tf_op jit(solution)/shard_map/all_to_all | solution.py:31
  38.4 0.7 collective-permute-start.6
  39.0 3.3 %collective-permute-start.7 = (bf16[4,288,128]{2,1,0:T(8,128)(2,1)S(1)}, bf16[4,288,128]{2,1,0:T(8,128)(2,1)S(1)}, u32[]{:S(2)}, u32[]{:S(2)}) collective-permute-start(bf16[4,288,128]{2,1,0:T(8,128)(2,1)S(1)} %pad_maximum_fusion.3), channel_id=1, source_target_pairs={{124,0},{126,2},{0,4},{2,6},{4,8},{6,10},{8,12},{10,14},{12,16},{1... | collective-permute-start | bytes 884744 | tf_op jit(solution)/shard_map/ppermute | solution.py:313
  42.4 0.7 collective-permute-start.4
  43.1 8.5 %collective-permute-start.5 = (bf16[4,432,128]{2,1,0:T(8,128)(2,1)S(1)}, bf16[4,432,128]{2,1,0:T(8,128)(2,1)S(1)}, u32[]{:S(2)}, u32[]{:S(2)}) collective-permute-start(bf16[4,432,128]{2,1,0:T(8,128)(2,1)S(1)} %pad_maximum_fusion.1), channel_id=1, source_target_pairs={{4,0},{6,2},{8,4},{10,6},{12,8},{14,10},{16,12},{18,14},{20,16},{2... | collective-permute-start | bytes 1327112 | tf_op jit(solution)/shard_map/ppermute | solution.py:313
  51.6 0.0 collective-permute-done.6
  51.6 17.5 %collective-permute-done.7 = bf16[4,288,128]{2,1,0:T(8,128)(2,1)S(1)} collective-permute-done((bf16[4,288,128]{2,1,0:T(8,128)(2,1)S(1)}, bf16[4,288,128]{2,1,0:T(8,128)(2,1)S(1)}, u32[]{:S(2)}, u32[]{:S(2)}) %collective-permute-start.7) | collective-permute-done | bytes 294944 | tf_op jit(solution)/shard_map/ppermute | solution.py:313
  69.1 0.8 broadcast_select_fusion.1
  69.9 0.0 all-to-all-done
  69.9 0.1 slice.24
  70.1 0.1 slice_bitcast_fusion
  70.2 0.1 copy.42
  70.3 1.2 broadcast_in_dim.27
  71.5 4.2 %all-to-all-start.1 = ((bf16[4,1248,128]{2,1,0:T(8,128)(2,1)}), bf16[4,1248,128]{2,1,0:T(8,128)(2,1)S(1)}, u32[]{:S(2)}, u32[]{:S(2)}) async-start(bf16[4,1248,128]{2,1,0:T(8,128)(2,1)} %broadcast_in_dim.27), calls=%async_computation.1 | async-start | bytes 2555904 | tf_op jit(solution)/shard_map/all_to_all | solution.py:31
  75.7 0.0 collective-permute-done.4
  75.7 0.0 collective-permute-done.5
  75.7 0.1 broadcast_select_fusion
  75.8 1.4 %pad_maximum_fusion.own = bf16[4,1728,128]{2,1,0:T(8,128)(2,1)S(1)} fusion(bf16[4,288,128]{2,1,0:T(8,128)(2,1)} %broadcast_select_fusion.1, bf16[4,432,128]{2,1,0:T(8,128)(2,1)S(1)} %broadcast_select_fusion, bf16[1,1008,128]{2,1,0:T(8,128)(2,1)} %bitcast.58, bf16[1,1008,128]{2,1,0:T(8,128)(2,1)} %bitcast.55, bf16[1,1008,128]{2,1,0:T(8,128)(2,1)} %bitcast.52, ...), kind=kLoop, calls=%fused_computation.4 | loop fusion | flops 10616832 | bytes 3538944 | tf_op jit(solution)/shard_map/concatenate | solution.py:420
  77.2 3.6 %collective-permute-start.8 = (bf16[4,1728,128]{2,1,0:T(8,128)(2,1)S(1)}, bf16[4,1728,128]{2,1,0:T(8,128)(2,1)}, u32[]{:S(2)}, u32[]{:S(2)}) collective-permute-start(bf16[4,1728,128]{2,1,0:T(8,128)(2,1)S(1)} %pad_maximum_fusion.own), channel_id=1, source_target_pairs={{0,1},{1,0},{2,3},{3,2},{4,5},{5,4},{6,7},{7,6},{8,9},{9,8},{10,11... | collective-permute-start | bytes 5308424 | tf_op jit(solution)/shard_map/ppermute | solution.py:26
  80.9 10.7 %all-to-all-done.1.own = bf16[4,1248,128]{2,1,0:T(8,128)(2,1)S(1)} async-done(((bf16[4,1248,128]{2,1,0:T(8,128)(2,1)}), bf16[4,1248,128]{2,1,0:T(8,128)(2,1)S(1)}, u32[]{:S(2)}, u32[]{:S(2)}) %all-to-all-start.1) | async-done | bytes 1277984 | tf_op jit(solution)/shard_map/all_to_all | solution.py:31
  91.6 4.6 %collective-permute-start.9 = (bf16[4,1248,128]{2,1,0:T(8,128)(2,1)S(1)}, bf16[4,1248,128]{2,1,0:T(8,128)(2,1)S(1)}, u32[]{:S(2)}, u32[]{:S(2)}) collective-permute-start(bf16[4,1248,128]{2,1,0:T(8,128)(2,1)S(1)} %all-to-all-done.1.own), channel_id=1, source_target_pairs={{0,1},{1,0},{2,3},{3,2},{4,5},{5,4},{6,7},{7,6},{8,9},{9,8},{10,11... | collective-permute-start | bytes 3833864 | tf_op jit(solution)/shard_map/ppermute | solution.py:26
  96.1 0.1 pad_add_fusion.place
  96.2 0.0 collective-permute-done.8.other
  96.2 3.6 %shard_map.77 = (bf16[768,2304]{1,0:T(8,128)(2,1)S(1)}, bf16[1152,1536]{1,0:T(8,128)(2,1)S(1)}) custom-call(s32[3]{0:T(128)S(1)} %pad_add_fusion.place, bf16[4,1728,128]{2,1,0:T(8,128)(2,1)S(1)} %pad_maximum_fusion.own, bf16[4,1728,128]{2,1,0:T(8,128)(2,1)} %collective-permute-done.8.other), custom_call_target="tpu_custom_call" | custom-call | flops 1000000000 | bytes 8388608 | tf_op jit(solution)/shard_map/pallas_call | solution.py:274
  99.9 0.0 collective-permute-done.9.other
  99.9 10.7 %shard_map.78 = bf16[4,1008,128]{2,1,0:T(8,128)(2,1)S(1)} custom-call(s32[3]{0:T(128)S(1)} %pad_add_fusion.place, bf16[768,2304]{1,0:T(8,128)(2,1)S(1)} %get-tuple-element.11.frame_rows, bf16[1152,1536]{1,0:T(8,128)(2,1)S(1)} %get-tuple-element.12.cot_rows, bf16[4,1248,128]{2,1,0:T(8,128)(2,1)S(1)} %all-to-all-done.1.own, ...), custom_call_target="tpu_custom_call" | custom-call | flops 4000000000 | bytes 8388608 | tf_op jit(solution)/shard_map/pallas_call | solution.py:274
  110.6 18.2 %all_to_all.15.parts = bf16[4,1008,128]{2,1,0:T(8,128)(2,1)S(1)} all-to-all(bf16[4,1008,128]{2,1,0:T(8,128)(2,1)S(1)} %shard_map.78), channel_id=1, replica_groups=mesh['y'=4,'xh'=2,'z'=16,'xl'=2,'core'=2] {'xh','xl'}, dimensions={0} | all-to-all | bytes 2064384 | tf_op jit(solution)/shard_map/all_to_all | solution.py:443
  128.8 0.8 shard_map.79
  (28 shorter events, 0.4 us)
Async XLA Ops:
  0.6 16.4 %copy-start = (bf16[10368,2]{0,1:T(2,128)(2,1)S(1)}, bf16[10368,2]{0,1:T(2,128)(2,1)}, u32[]{:S(2)}) copy-start(bf16[10368,2]{0,1:T(2,128)(2,1)} %param.7) | copy-start | bytes 124420
  2.6 18.6 %collective-permute-start.1 = (bf16[1008,128]{1,0:T(8,128)(2,1)S(1)}, bf16[1008,128]{1,0:T(8,128)(2,1)S(1)}, u32[]{:S(2)}, u32[]{:S(2)}) collective-permute-start(bf16[1008,128]{1,0:T(8,128)(2,1)S(1)} %get-tuple-element.17), channel_id=1, source_target_pairs={{0,2},{2,64},{64,66},{66,0},{1,3},{3,65},{65,67},{67,1},{4,6},{6,6... | collective-permute-start | bytes 774152 | tf_op jit(solution)/shard_map/ppermute | solution.py:357
  6.6 14.6 %collective-permute-start.2 = (bf16[1008,128]{1,0:T(8,128)(2,1)S(1)}, bf16[1008,128]{1,0:T(8,128)(2,1)S(1)}, u32[]{:S(2)}, u32[]{:S(2)}) collective-permute-start(bf16[1008,128]{1,0:T(8,128)(2,1)S(1)} %get-tuple-element.17), channel_id=1, source_target_pairs={{0,66},{2,0},{64,2},{66,64},{1,67},{3,1},{65,3},{67,65},{4,70},{6,... | collective-permute-start | bytes 774152 | tf_op jit(solution)/shard_map/ppermute | solution.py:357
  9.8 11.4 %collective-permute-start.3 = (bf16[1008,128]{1,0:T(8,128)(2,1)S(1)}, bf16[1008,128]{1,0:T(8,128)(2,1)S(1)}, u32[]{:S(2)}, u32[]{:S(2)}) collective-permute-start(bf16[1008,128]{1,0:T(8,128)(2,1)S(1)} %get-tuple-element.17), channel_id=1, source_target_pairs={{0,64},{2,66},{64,0},{66,2},{1,65},{3,67},{65,1},{67,3},{4,68},{6,... | collective-permute-start | bytes 774152 | tf_op jit(solution)/shard_map/ppermute | solution.py:357
  14.2 6.5 %collective-permute-start = (bf16[54,2,128]{2,0,1:T(8,128)(2,1)S(1)}, bf16[54,2,128]{2,0,1:T(8,128)(2,1)S(1)}, u32[]{:S(2)}, u32[]{:S(2)}) collective-permute-start(bf16[54,2,128]{2,0,1:T(8,128)(2,1)S(1)} %bitcast.65), channel_id=1, source_target_pairs={{0,66},{66,0},{2,64},{64,2},{1,67},{67,1},{3,65},{65,3},{4,70},{70... | collective-permute-start | bytes 82952 | tf_op jit(solution)/shard_map/ppermute | solution.py:377
  20.7 17.6 %copy-start.4 = (s32[4]{0:T(128)S(1)}, s32[4]{0:T(128)}, u32[]{:S(2)}) copy-start(s32[4]{0:T(128)} %constant.148.clone) | copy-start | bytes 52
  21.2 50.3 %copy-start.1 = (bf16[1008,128]{1,0:T(8,128)(2,1)}, bf16[1008,128]{1,0:T(8,128)(2,1)S(1)}, u32[]{:S(2)}) copy-start(bf16[1008,128]{1,0:T(8,128)(2,1)S(1)} %collective-permute-done.1) | copy-start | bytes 774148
  21.2 50.3 %copy-start.2 = (bf16[1008,128]{1,0:T(8,128)(2,1)}, bf16[1008,128]{1,0:T(8,128)(2,1)S(1)}, u32[]{:S(2)}) copy-start(bf16[1008,128]{1,0:T(8,128)(2,1)S(1)} %collective-permute-done.2) | copy-start | bytes 774148
  21.2 50.3 %copy-start.3 = (bf16[1008,128]{1,0:T(8,128)(2,1)}, bf16[1008,128]{1,0:T(8,128)(2,1)S(1)}, u32[]{:S(2)}) copy-start(bf16[1008,128]{1,0:T(8,128)(2,1)S(1)} %collective-permute-done.3) | copy-start | bytes 774148
  22.2 47.7 %all-to-all-start = ((bf16[16,39,2,128]{3,2,1,0:T(2,128)(2,1)}), bf16[16,39,2,128]{3,2,1,0:T(2,128)(2,1)S(1)}, u32[]{:S(2)}, u32[]{:S(2)}) async-start(bf16[16,39,2,128]{3,2,1,0:T(2,128)(2,1)} %broadcast_in_dim.26), calls=%async_computation | async-start | bytes 638976 | tf_op jit(solution)/shard_map/all_to_all | solution.py:31
  38.4 13.2 %collective-permute-start.6 = (bf16[4,288,128]{2,1,0:T(8,128)(2,1)S(1)}, bf16[4,288,128]{2,1,0:T(8,128)(2,1)S(1)}, u32[]{:S(2)}, u32[]{:S(2)}) collective-permute-start(bf16[4,288,128]{2,1,0:T(8,128)(2,1)S(1)} %pad_maximum_fusion.3), channel_id=1, source_target_pairs={{124,128},{126,130},{60,192},{62,194},{252,256},{254,258},{188,320... | collective-permute-start | bytes 884744 | tf_op jit(solution)/shard_map/ppermute | solution.py:310
  39.0 30.0 %collective-permute-start.7 = (bf16[4,288,128]{2,1,0:T(8,128)(2,1)S(1)}, bf16[4,288,128]{2,1,0:T(8,128)(2,1)S(1)}, u32[]{:S(2)}, u32[]{:S(2)}) collective-permute-start(bf16[4,288,128]{2,1,0:T(8,128)(2,1)S(1)} %pad_maximum_fusion.3), channel_id=1, source_target_pairs={{124,0},{126,2},{0,4},{2,6},{4,8},{6,10},{8,12},{10,14},{12,16},{1... | collective-permute-start | bytes 884744 | tf_op jit(solution)/shard_map/ppermute | solution.py:313
  42.4 33.4 %collective-permute-start.4 = (bf16[4,432,128]{2,1,0:T(8,128)(2,1)S(1)}, bf16[4,432,128]{2,1,0:T(8,128)(2,1)S(1)}, u32[]{:S(2)}, u32[]{:S(2)}) collective-permute-start(bf16[4,432,128]{2,1,0:T(8,128)(2,1)S(1)} %pad_maximum_fusion.1), channel_id=1, source_target_pairs={{192,60},{194,62},{128,124},{130,126},{320,188},{322,190},{256,252... | collective-permute-start | bytes 1327112 | tf_op jit(solution)/shard_map/ppermute | solution.py:310
  43.1 32.7 %collective-permute-start.5 = (bf16[4,432,128]{2,1,0:T(8,128)(2,1)S(1)}, bf16[4,432,128]{2,1,0:T(8,128)(2,1)S(1)}, u32[]{:S(2)}, u32[]{:S(2)}) collective-permute-start(bf16[4,432,128]{2,1,0:T(8,128)(2,1)S(1)} %pad_maximum_fusion.1), channel_id=1, source_target_pairs={{4,0},{6,2},{8,4},{10,6},{12,8},{14,10},{16,12},{18,14},{20,16},{2... | collective-permute-start | bytes 1327112 | tf_op jit(solution)/shard_map/ppermute | solution.py:313
  71.5 20.0 %all-to-all-start.1 = ((bf16[4,1248,128]{2,1,0:T(8,128)(2,1)}), bf16[4,1248,128]{2,1,0:T(8,128)(2,1)S(1)}, u32[]{:S(2)}, u32[]{:S(2)}) async-start(bf16[4,1248,128]{2,1,0:T(8,128)(2,1)} %broadcast_in_dim.27), calls=%async_computation.1 | async-start | bytes 2555904 | tf_op jit(solution)/shard_map/all_to_all | solution.py:31
  77.2 19.0 %collective-permute-start.8 = (bf16[4,1728,128]{2,1,0:T(8,128)(2,1)S(1)}, bf16[4,1728,128]{2,1,0:T(8,128)(2,1)}, u32[]{:S(2)}, u32[]{:S(2)}) collective-permute-start(bf16[4,1728,128]{2,1,0:T(8,128)(2,1)S(1)} %pad_maximum_fusion.own), channel_id=1, source_target_pairs={{0,1},{1,0},{2,3},{3,2},{4,5},{5,4},{6,7},{7,6},{8,9},{9,8},{10,11... | collective-permute-start | bytes 5308424 | tf_op jit(solution)/shard_map/ppermute | solution.py:26
  91.6 8.3 %collective-permute-start.9 = (bf16[4,1248,128]{2,1,0:T(8,128)(2,1)S(1)}, bf16[4,1248,128]{2,1,0:T(8,128)(2,1)S(1)}, u32[]{:S(2)}, u32[]{:S(2)}) collective-permute-start(bf16[4,1248,128]{2,1,0:T(8,128)(2,1)S(1)} %all-to-all-done.1.own), channel_id=1, source_target_pairs={{0,1},{1,0},{2,3},{3,2},{4,5},{5,4},{6,7},{7,6},{8,9},{9,8},{10,11... | collective-permute-start | bytes 3833864 | tf_op jit(solution)/shard_map/ppermute | solution.py:26

commit v4 on v3

--- a/solution.py
+++ b/solution.py
@@ -2,7 +2,6 @@
 
 import jax
 import jax.numpy as jnp
-import numpy as np
 from jax import lax
 from jax.experimental import pallas as pl
 from jax.experimental.pallas import tpu as pltpu
@@ -292,27 +291,6 @@
     return call(kernel, outs, [], 10**9, 14, place, own, other)
 
 
-def beside(blocks, xh, z, by):
-    axes = ("y", "xh", "z", "xl")
-    dims = tuple(lax.axis_size(axis) for axis in axes)
-    edge = dims[2] - 1 if by > 0 else 0
-    near, wrap = [], []
-    for target in np.ndindex(*dims):
-        ty, tx, tz, tl = target
-        to = int(np.ravel_multi_index(target, dims))
-        if tz != edge:
-            near.append((int(np.ravel_multi_index((ty, tx, tz + by, tl), dims)), to))
-            continue
-        far = dims[2] - 1 - edge
-        near.append((int(np.ravel_multi_index((ty, 1 - tx, far, tl), dims)), to))
-        if 0 <= ty + by < dims[0]:
-            wrap.append((int(np.ravel_multi_index((ty + by, 1 - tx, far, tl), dims)), to))
-    beyond = lax.ppermute(blocks, axes, wrap)
-    side = (xh * 2 + lax.axis_index("xl") + jnp.array(OFFSETS)) % 4 // 2
-    turned = (z == edge) & (side == (1 if by > 0 else 0))
-    return jnp.where(turned[:, None, None], beyond, lax.ppermute(blocks, axes, near))
-
-
 def compute(layout, place, frame_rows, cot_rows, own, other, width, channels, in_channels):
     blocks = own.shape[0]
     unit = blocks * PAD
@@ -403,23 +381,16 @@
     frame_size, cot_size = 2 * (in_channels // LANES) * width, 2 * splits * width
     count = 2 * frame_count
     block = jnp.concatenate((flat(cotangent[3:]), flat(cotangent[:3]), flat(frames)), axis=0)
-    payload, *rest = lax.optimization_barrier(
-        (
-            jnp.concatenate((up_part, mix_part), axis=0),
-            ring(block, 1),
-            ring(block, -1),
-            ring(block, 2),
-        )
-    )
-    planes = spread(payload, "z")
-    blocks = jnp.stack((block, *rest))
-    z = lax.axis_index("z")
+    planes = spread(jnp.concatenate((up_part, mix_part), axis=0), "z")
     early = (count - 3) * cot_size
-    following = beside(blocks[:, early : count * cot_size + frame_size], xh, z, 1)
-    previous = beside(blocks[:, block.shape[0] - 2 * frame_size :], xh, z, -1)
-    blocks = jnp.concatenate((blocks, following, previous), axis=1)
+    first = block.shape[0]
+    following = shift(block[early : count * cot_size + frame_size], PLANES, -1)
+    previous = shift(block[first - 2 * frame_size :], PLANES, 1)
+    block = jnp.concatenate((block, following, previous), axis=0)
+    blocks = (block, ring(block, 1), ring(block, -1), ring(block, 2))
+    planes, block = lax.optimization_barrier((planes, block))
+    blocks = jnp.stack(blocks)
     others = swap(blocks)
-    first = block.shape[0]
     last = first + 3 * cot_size + frame_size
     cot_starts = [early + time * cot_size for time in range(3)]
     cot_starts += [time * cot_size for time in range(count - 3)]

time: 130 us -> 112 us (0.86)
  waiting for transfers between devices: 31.6 us -> 18.6 us
  starting transfers between devices: 55.1 us -> 51.7 us
    all_to_all x2, waiting for transfers between devices: 10.7 us -> 0.1 us  [spread(): lax.all_to_all(jnp.broadcast_to(array, (count, *array.shape)), axis, 0, 0...]
    ppermute x4 -> x2, starting transfers between devices: 13.1 us -> 5.28 us  [shift(): return lax.ppermute(array, axis, pairs)]
    ppermute x3, waiting for transfers between devices: 0.01 us -> 6.69 us  [ring(): return lax.ppermute(array, RING, [(i, (i + by) % 4) for i in range(4)])]
    ppermute x4 -> x2, waiting for transfers between devices: 17.5 us -> 10.8 us  [shift(): return lax.ppermute(array, axis, pairs)]
    ppermute x2, starting transfers between devices: 8.21 us -> 11.3 us  [swap(): return lax.ppermute(array, 'core', [(0, 1), (1, 0)])]
    ppermute x1, waiting for transfers between devices: 3.41 us -> 0.94 us  [shards(): mix_other = lax.ppermute(raw_mix, RING, [(0, 3), (3, 0), (1, 2), (2, 1)])]
    ppermute x1, starting transfers between devices: 2.77 us -> 5.22 us  [shards(): mix_other = lax.ppermute(raw_mix, RING, [(0, 3), (3, 0), (1, 2), (2, 1)])]
    another operation x2 -> x1, other arithmetic: 0.06 us -> 1.5 us  [shards(): blocks = jnp.stack(blocks)]
  transfers between devices with their start and end apart: 12 -> 10, of which waited for: 3 -> 4; matrix products, arithmetic and copies ran while one was open for 4% -> 3% of each run, Pallas kernels for 3% -> 3%
where the time goes in v4:
time: 112 us; the launch traced here: 111 us
  starting transfers between devices  51.7 us (46%)
  waiting for transfers between devices  18.6 us (17%)
  blocking collectives  18.2 us (16%)
  Pallas kernels  15.1 us (13%)
  local copies, waits for them, and re-layouts  4.43 us (4%)
  other arithmetic  1.69 us (2%)
    all_to_all x2, starting transfers between devices, spread(): lax.all_to_all(jnp.broadcast_to(array, (count, *array.shape)), axis, 0, 0...  19.4 us
    all_to_all x1, blocking collectives, shards(): parts = lax.all_to_all(parts, RING, 0, 0, tiled=True)  18.2 us
    pallas_call x2, Pallas kernels, call(): pl.pallas_call(kernel, out_shape=outs, in_specs=[pl.BlockSpec(memory_spac...  14.3 us
    ppermute x2, starting transfers between devices, swap(): return lax.ppermute(array, 'core', [(0, 1), (1, 0)])  11.3 us
    ppermute x2, waiting for transfers between devices, shift(): return lax.ppermute(array, axis, pairs)  10.8 us
    ppermute x3, starting transfers between devices, ring(): return lax.ppermute(array, RING, [(i, (i + by) % 4) for i in range(4)])  10.5 us
    ppermute x3, waiting for transfers between devices, ring(): return lax.ppermute(array, RING, [(i, (i + by) % 4) for i in range(4)])  6.69 us
    ppermute x2, starting transfers between devices, shift(): return lax.ppermute(array, axis, pairs)  5.28 us
  transfers between devices with their start and end apart: 10, of which 4 were waited for; matrix products, arithmetic and copies ran while one was open for 3% of the time, Pallas kernels for 3%

profile of v4, /device:TPU:1, one launch (start us, length us, event | category | flops | bytes accessed | tf_op | source)
XLA Modules:
  0.0 111.0 jit_solution(14647033631662431801)
XLA Ops:
  0.6 0.0 copy-start
  0.6 0.8 reshape.61
  1.5 5.2 %collective-permute-start.6 = (bf16[54,2,128]{2,0,1:T(8,128)(2,1)S(1)}, bf16[54,2,128]{2,0,1:T(8,128)(2,1)S(1)}, u32[]{:S(2)}, u32[]{:S(2)}) collective-permute-start(bf16[54,2,128]{2,0,1:T(8,128)(2,1)S(1)} %bitcast.62), channel_id=1, source_target_pairs={{0,66},{66,0},{2,64},{64,2},{1,67},{67,1},{3,65},{65,3},{4,70},{70... | collective-permute-start | bytes 82952 | tf_op jit(solution)/shard_map/ppermute | solution.py:355
  6.7 0.0 copy-done
  6.8 0.1 dynamic-slice_reduce_fusion
  7.0 0.9 collective-permute-done.6
  8.0 0.0 copy-start.5
  8.0 0.0 copy-start.4
  8.0 0.3 fusion
  8.4 0.9 broadcast_in_dim.6
  9.3 15.1 %all-to-all-start = ((bf16[16,39,2,128]{3,2,1,0:T(2,128)(2,1)}), bf16[16,39,2,128]{3,2,1,0:T(2,128)(2,1)S(1)}, u32[]{:S(2)}, u32[]{:S(2)}) async-start(bf16[16,39,2,128]{3,2,1,0:T(2,128)(2,1)} %broadcast_in_dim.6), calls=%async_computation | async-start | bytes 638976 | tf_op jit(solution)/shard_map/all_to_all | solution.py:30
  24.4 0.0 copy-done.5
  24.5 0.0 copy-done.4
  24.6 1.3 %collective-permute-start = (bf16[432,128]{1,0:T(8,128)(2,1)S(1)}, bf16[432,128]{1,0:T(8,128)(2,1)S(1)}, u32[]{:S(2)}, u32[]{:S(2)}) collective-permute-start(bf16[432,128]{1,0:T(8,128)(2,1)S(1)} %get-tuple-element.10), channel_id=1, source_target_pairs={{4,0},{8,4},{12,8},{16,12},{20,16},{24,20},{28,24},{32,28},{36,32}... | collective-permute-start | bytes 331784 | tf_op jit(solution)/shard_map/ppermute | solution.py:21
  26.0 4.0 %collective-permute-start.1 = (bf16[288,128]{1,0:T(8,128)(2,1)S(1)}, bf16[288,128]{1,0:T(8,128)(2,1)S(1)}, u32[]{:S(2)}, u32[]{:S(2)}) collective-permute-start(bf16[288,128]{1,0:T(8,128)(2,1)S(1)} %bitcast.63), channel_id=1, source_target_pairs={{0,4},{4,8},{8,12},{12,16},{16,20},{20,24},{24,28},{28,32},{32,36}... | collective-permute-start | bytes 221192 | tf_op jit(solution)/shard_map/ppermute | solution.py:21
  30.0 10.8 %collective-permute-done = bf16[432,128]{1,0:T(8,128)(2,1)S(1)} collective-permute-done((bf16[432,128]{1,0:T(8,128)(2,1)S(1)}, bf16[432,128]{1,0:T(8,128)(2,1)S(1)}, u32[]{:S(2)}, u32[]{:S(2)}) %collective-permute-start) | collective-permute-done | bytes 110624 | tf_op jit(solution)/shard_map/ppermute | solution.py:21
  40.8 0.0 collective-permute-done.1
  40.9 1.9 %collective-permute-start.2 = (bf16[1728,128]{1,0:T(8,128)(2,1)S(1)}, bf16[1728,128]{1,0:T(8,128)(2,1)S(1)}, u32[]{:S(2)}, u32[]{:S(2)}) collective-permute-start(bf16[1728,128]{1,0:T(8,128)(2,1)S(1)} %constant_dynamic-update-slice_fusion), channel_id=1, source_target_pairs={{0,2},{2,64},{64,66},{66,0},{1,3},{3,65},{65,67},{67,1},{4,6},{6,6... | collective-permute-start | bytes 1327112 | tf_op jit(solution)/shard_map/ppermute | solution.py:335
  42.8 4.6 %collective-permute-start.3 = (bf16[1728,128]{1,0:T(8,128)(2,1)S(1)}, bf16[1728,128]{1,0:T(8,128)(2,1)S(1)}, u32[]{:S(2)}, u32[]{:S(2)}) collective-permute-start(bf16[1728,128]{1,0:T(8,128)(2,1)S(1)} %constant_dynamic-update-slice_fusion), channel_id=1, source_target_pairs={{0,66},{2,0},{64,2},{66,64},{1,67},{3,1},{65,3},{67,65},{4,70},{6,... | collective-permute-start | bytes 1327112 | tf_op jit(solution)/shard_map/ppermute | solution.py:335
  47.4 3.9 %collective-permute-start.4 = (bf16[1728,128]{1,0:T(8,128)(2,1)S(1)}, bf16[1728,128]{1,0:T(8,128)(2,1)S(1)}, u32[]{:S(2)}, u32[]{:S(2)}) collective-permute-start(bf16[1728,128]{1,0:T(8,128)(2,1)S(1)} %constant_dynamic-update-slice_fusion), channel_id=1, source_target_pairs={{0,64},{2,66},{64,0},{66,2},{1,65},{3,67},{65,1},{67,3},{4,68},{6,... | collective-permute-start | bytes 1327112 | tf_op jit(solution)/shard_map/ppermute | solution.py:335
  51.4 0.0 all-to-all-done
  51.4 0.1 slice_bitcast_fusion
  51.6 0.1 copy.44
  51.7 1.2 %broadcast_in_dim.7 = bf16[4,1248,128]{2,1,0:T(8,128)(2,1)} broadcast(bf16[1248,128]{1,0:T(8,128)(2,1)S(1)} %pad_maximum_fusion.1), dimensions={1,2} | broadcast | bytes 1597440 | tf_op jit(solution)/shard_map/broadcast_in_dim | solution.py:31
  52.9 4.3 %all-to-all-start.1 = ((bf16[4,1248,128]{2,1,0:T(8,128)(2,1)}), bf16[4,1248,128]{2,1,0:T(8,128)(2,1)S(1)}, u32[]{:S(2)}, u32[]{:S(2)}) async-start(bf16[4,1248,128]{2,1,0:T(8,128)(2,1)} %broadcast_in_dim.7), calls=%async_computation.1 | async-start | bytes 2555904 | tf_op jit(solution)/shard_map/all_to_all | solution.py:30
  57.2 0.0 collective-permute-done.2
  57.2 0.0 copy-start.1
  57.2 0.0 collective-permute-done.3
  57.2 0.0 copy-start.2
  57.3 6.7 %collective-permute-done.4 = bf16[1728,128]{1,0:T(8,128)(2,1)S(1)} collective-permute-done((bf16[1728,128]{1,0:T(8,128)(2,1)S(1)}, bf16[1728,128]{1,0:T(8,128)(2,1)S(1)}, u32[]{:S(2)}, u32[]{:S(2)}) %collective-permute-start.4) | collective-permute-done | bytes 442400 | tf_op jit(solution)/shard_map/ppermute | solution.py:335
  63.9 0.0 copy-start.3
  63.9 0.0 copy-done.1
  63.9 0.0 copy-done.2
  63.9 0.8 copy-done.3
  64.7 1.5 %pad_maximum_fusion.own = bf16[4,1728,128]{2,1,0:T(8,128)(2,1)S(1)} fusion(bf16[1,1728,128]{2,1,0:T(8,128)(2,1)} %bitcast.59, bf16[1,1728,128]{2,1,0:T(8,128)(2,1)} %bitcast.58, bf16[1,1728,128]{2,1,0:T(8,128)(2,1)} %bitcast.57, bf16[1,1728,128]{2,1,0:T(8,128)(2,1)S(1)} %bitcast.55), kind=kLoop, calls=%fused_computation.4 | loop fusion | flops 2654208 | bytes 3538944 | tf_op jit(solution)/shard_map/stack | solution.py:392
  66.2 5.2 %collective-permute-start.5 = (bf16[4,1728,128]{2,1,0:T(8,128)(2,1)S(1)}, bf16[4,1728,128]{2,1,0:T(8,128)(2,1)}, u32[]{:S(2)}, u32[]{:S(2)}) collective-permute-start(bf16[4,1728,128]{2,1,0:T(8,128)(2,1)S(1)} %pad_maximum_fusion.own), channel_id=1, source_target_pairs={{0,1},{1,0},{2,3},{3,2},{4,5},{5,4},{6,7},{7,6},{8,9},{9,8},{10,11... | collective-permute-start | bytes 5308424 | tf_op jit(solution)/shard_map/ppermute | solution.py:25
  71.5 0.1 all-to-all-done.1.own
  71.6 6.1 %collective-permute-start.7 = (bf16[4,1248,128]{2,1,0:T(8,128)(2,1)S(1)}, bf16[4,1248,128]{2,1,0:T(8,128)(2,1)S(1)}, u32[]{:S(2)}, u32[]{:S(2)}) collective-permute-start(bf16[4,1248,128]{2,1,0:T(8,128)(2,1)S(1)} %all-to-all-done.1.own), channel_id=1, source_target_pairs={{0,1},{1,0},{2,3},{3,2},{4,5},{5,4},{6,7},{7,6},{8,9},{9,8},{10,11... | collective-permute-start | bytes 3833864 | tf_op jit(solution)/shard_map/ppermute | solution.py:25
  77.6 0.1 pad_add_fusion.place
  77.7 0.0 collective-permute-done.5.other
  77.7 3.6 %shard_map.59 = (bf16[768,2304]{1,0:T(8,128)(2,1)S(1)}, bf16[1152,1536]{1,0:T(8,128)(2,1)S(1)}) custom-call(s32[3]{0:T(128)S(1)} %pad_add_fusion.place, bf16[4,1728,128]{2,1,0:T(8,128)(2,1)S(1)} %pad_maximum_fusion.own, bf16[4,1728,128]{2,1,0:T(8,128)(2,1)} %collective-permute-done.5.other), custom_call_target="tpu_custom_call" | custom-call | flops 1000000000 | bytes 8388608 | tf_op jit(solution)/shard_map/pallas_call | solution.py:273
  81.4 0.0 collective-permute-done.7.other
  81.4 10.7 %shard_map.60 = bf16[4,1008,128]{2,1,0:T(8,128)(2,1)S(1)} custom-call(s32[3]{0:T(128)S(1)} %pad_add_fusion.place, bf16[768,2304]{1,0:T(8,128)(2,1)S(1)} %get-tuple-element.5.frame_rows, bf16[1152,1536]{1,0:T(8,128)(2,1)S(1)} %get-tuple-element.6.cot_rows, bf16[4,1248,128]{2,1,0:T(8,128)(2,1)S(1)} %all-to-all-done.1.own, ...), custom_call_target="tpu_custom_call" | custom-call | flops 4000000000 | bytes 8388608 | tf_op jit(solution)/shard_map/pallas_call | solution.py:273
  92.1 18.2 %all_to_all.15.parts = bf16[4,1008,128]{2,1,0:T(8,128)(2,1)S(1)} all-to-all(bf16[4,1008,128]{2,1,0:T(8,128)(2,1)S(1)} %shard_map.60), channel_id=1, replica_groups=mesh['y'=4,'xh'=2,'z'=16,'xl'=2,'core'=2] {'xh','xl'}, dimensions={0} | all-to-all | bytes 2064384 | tf_op jit(solution)/shard_map/all_to_all | solution.py:414
  110.3 0.8 shard_map.61
  (29 shorter events, 0.5 us)
Async XLA Ops:
  0.6 6.1 %copy-start = (bf16[10368,2]{0,1:T(2,128)(2,1)S(1)}, bf16[10368,2]{0,1:T(2,128)(2,1)}, u32[]{:S(2)}) copy-start(bf16[10368,2]{0,1:T(2,128)(2,1)} %param.5) | copy-start | bytes 124420
  1.5 6.5 %collective-permute-start.6 = (bf16[54,2,128]{2,0,1:T(8,128)(2,1)S(1)}, bf16[54,2,128]{2,0,1:T(8,128)(2,1)S(1)}, u32[]{:S(2)}, u32[]{:S(2)}) collective-permute-start(bf16[54,2,128]{2,0,1:T(8,128)(2,1)S(1)} %bitcast.62), channel_id=1, source_target_pairs={{0,66},{66,0},{2,64},{64,2},{1,67},{67,1},{3,65},{65,3},{4,70},{70... | collective-permute-start | bytes 82952 | tf_op jit(solution)/shard_map/ppermute | solution.py:355
  8.0 16.4 %copy-start.5 = (bf16[3,2,24,384]{3,2,1,0:T(8,128)(2,1)S(1)}, bf16[3,2,24,384]{3,2,1,0:T(8,128)(2,1)}, u32[]{:S(2)}) copy-start(bf16[3,2,24,384]{3,2,1,0:T(8,128)(2,1)} %param.4) | copy-start | bytes 331780
  8.0 16.5 %copy-start.4 = (bf16[6,2,24,256]{3,2,1,0:T(8,128)(2,1)S(1)}, bf16[6,2,24,256]{3,2,1,0:T(8,128)(2,1)}, u32[]{:S(2)}) copy-start(bf16[6,2,24,256]{3,2,1,0:T(8,128)(2,1)} %param.7) | copy-start | bytes 442372
  9.3 42.1 %all-to-all-start = ((bf16[16,39,2,128]{3,2,1,0:T(2,128)(2,1)}), bf16[16,39,2,128]{3,2,1,0:T(2,128)(2,1)S(1)}, u32[]{:S(2)}, u32[]{:S(2)}) async-start(bf16[16,39,2,128]{3,2,1,0:T(2,128)(2,1)} %broadcast_in_dim.6), calls=%async_computation | async-start | bytes 638976 | tf_op jit(solution)/shard_map/all_to_all | solution.py:30
  24.6 16.2 %collective-permute-start = (bf16[432,128]{1,0:T(8,128)(2,1)S(1)}, bf16[432,128]{1,0:T(8,128)(2,1)S(1)}, u32[]{:S(2)}, u32[]{:S(2)}) collective-permute-start(bf16[432,128]{1,0:T(8,128)(2,1)S(1)} %get-tuple-element.10), channel_id=1, source_target_pairs={{4,0},{8,4},{12,8},{16,12},{20,16},{24,20},{28,24},{32,28},{36,32}... | collective-permute-start | bytes 331784 | tf_op jit(solution)/shard_map/ppermute | solution.py:21
  26.0 14.8 %collective-permute-start.1 = (bf16[288,128]{1,0:T(8,128)(2,1)S(1)}, bf16[288,128]{1,0:T(8,128)(2,1)S(1)}, u32[]{:S(2)}, u32[]{:S(2)}) collective-permute-start(bf16[288,128]{1,0:T(8,128)(2,1)S(1)} %bitcast.63), channel_id=1, source_target_pairs={{0,4},{4,8},{8,12},{12,16},{16,20},{20,24},{24,28},{28,32},{32,36}... | collective-permute-start | bytes 221192 | tf_op jit(solution)/shard_map/ppermute | solution.py:21
  40.9 16.4 %collective-permute-start.2 = (bf16[1728,128]{1,0:T(8,128)(2,1)S(1)}, bf16[1728,128]{1,0:T(8,128)(2,1)S(1)}, u32[]{:S(2)}, u32[]{:S(2)}) collective-permute-start(bf16[1728,128]{1,0:T(8,128)(2,1)S(1)} %constant_dynamic-update-slice_fusion), channel_id=1, source_target_pairs={{0,2},{2,64},{64,66},{66,0},{1,3},{3,65},{65,67},{67,1},{4,6},{6,6... | collective-permute-start | bytes 1327112 | tf_op jit(solution)/shard_map/ppermute | solution.py:335
  42.8 14.5 %collective-permute-start.3 = (bf16[1728,128]{1,0:T(8,128)(2,1)S(1)}, bf16[1728,128]{1,0:T(8,128)(2,1)S(1)}, u32[]{:S(2)}, u32[]{:S(2)}) collective-permute-start(bf16[1728,128]{1,0:T(8,128)(2,1)S(1)} %constant_dynamic-update-slice_fusion), channel_id=1, source_target_pairs={{0,66},{2,0},{64,2},{66,64},{1,67},{3,1},{65,3},{67,65},{4,70},{6,... | collective-permute-start | bytes 1327112 | tf_op jit(solution)/shard_map/ppermute | solution.py:335
  47.4 16.5 %collective-permute-start.4 = (bf16[1728,128]{1,0:T(8,128)(2,1)S(1)}, bf16[1728,128]{1,0:T(8,128)(2,1)S(1)}, u32[]{:S(2)}, u32[]{:S(2)}) collective-permute-start(bf16[1728,128]{1,0:T(8,128)(2,1)S(1)} %constant_dynamic-update-slice_fusion), channel_id=1, source_target_pairs={{0,64},{2,66},{64,0},{66,2},{1,65},{3,67},{65,1},{67,3},{4,68},{6,... | collective-permute-start | bytes 1327112 | tf_op jit(solution)/shard_map/ppermute | solution.py:335
  52.9 18.6 %all-to-all-start.1 = ((bf16[4,1248,128]{2,1,0:T(8,128)(2,1)}), bf16[4,1248,128]{2,1,0:T(8,128)(2,1)S(1)}, u32[]{:S(2)}, u32[]{:S(2)}) async-start(bf16[4,1248,128]{2,1,0:T(8,128)(2,1)} %broadcast_in_dim.7), calls=%async_computation.1 | async-start | bytes 2555904 | tf_op jit(solution)/shard_map/all_to_all | solution.py:30
  57.2 6.7 %copy-start.1 = (bf16[1728,128]{1,0:T(8,128)(2,1)}, bf16[1728,128]{1,0:T(8,128)(2,1)S(1)}, u32[]{:S(2)}) copy-start(bf16[1728,128]{1,0:T(8,128)(2,1)S(1)} %collective-permute-done.2) | copy-start | bytes 1327108
  57.2 6.7 %copy-start.2 = (bf16[1728,128]{1,0:T(8,128)(2,1)}, bf16[1728,128]{1,0:T(8,128)(2,1)S(1)}, u32[]{:S(2)}) copy-start(bf16[1728,128]{1,0:T(8,128)(2,1)S(1)} %collective-permute-done.3) | copy-start | bytes 1327108
  63.9 0.8 copy-start.3
  66.2 11.5 %collective-permute-start.5 = (bf16[4,1728,128]{2,1,0:T(8,128)(2,1)S(1)}, bf16[4,1728,128]{2,1,0:T(8,128)(2,1)}, u32[]{:S(2)}, u32[]{:S(2)}) collective-permute-start(bf16[4,1728,128]{2,1,0:T(8,128)(2,1)S(1)} %pad_maximum_fusion.own), channel_id=1, source_target_pairs={{0,1},{1,0},{2,3},{3,2},{4,5},{5,4},{6,7},{7,6},{8,9},{9,8},{10,11... | collective-permute-start | bytes 5308424 | tf_op jit(solution)/shard_map/ppermute | solution.py:25
  71.6 9.8 %collective-permute-start.7 = (bf16[4,1248,128]{2,1,0:T(8,128)(2,1)S(1)}, bf16[4,1248,128]{2,1,0:T(8,128)(2,1)S(1)}, u32[]{:S(2)}, u32[]{:S(2)}) collective-permute-start(bf16[4,1248,128]{2,1,0:T(8,128)(2,1)S(1)} %all-to-all-done.1.own), channel_id=1, source_target_pairs={{0,1},{1,0},{2,3},{3,2},{4,5},{5,4},{6,7},{7,6},{8,9},{9,8},{10,11... | collective-permute-start | bytes 3833864 | tf_op jit(solution)/shard_map/ppermute | solution.py:25

commit v5 on v4

--- a/solution.py
+++ b/solution.py
@@ -119,20 +119,16 @@
                         up_w[at : at + part, lane : lane + LANES] = up_tile(
                             kt, row - out_row + 1, kw, split, splits
                         )
-    step = 2 * LANES
-    ups[...] = jnp.zeros_like(ups)
+    step = 3 * unit
 
     def product(k, _):
-        lanes = pl.ds(pl.multiple_of(k * step, step), step)
-        ups[...] += lax.dot_general(
-            rows[:, lanes],
-            up_w[:, lanes],
-            (((1,), (1,)), ((), ())),
-            preferred_element_type=jnp.float32,
+        at = pl.ds(pl.multiple_of(k * step, step), step)
+        ups[at, :] = lax.dot_general(
+            rows[at, :], up_w[...], (((1,), (1,)), ((), ())), preferred_element_type=jnp.float32
         )
         return 0
 
-    lax.fori_loop(0, rows.shape[1] // step, product, 0)
+    lax.fori_loop(0, rows.shape[0] // step, product, 0)
     inside = mask[...] > 0
     times = 2 * (rows.shape[0] // unit - 1) - 1
     for time in range(times):
@@ -213,17 +209,14 @@
                 mix_w[at : at + channels, kt * LANES : (kt + 1) * LANES] = mix_tile(
                     kt, 2 - shift_w, row
                 )
-    step = 2 * LANES
-    partial[...] = jnp.zeros_like(partial)
+    step = 3 * unit
 
     def product(k, _):
-        lanes = pl.ds(pl.multiple_of(k * step, step), step)
-        partial[...] += jnp.dot(
-            rows[:, lanes], mix_w[lanes, :], preferred_element_type=jnp.float32
-        )
+        at = pl.ds(pl.multiple_of(k * step, step), step)
+        partial[at, :] = jnp.dot(rows[at, :], mix_w[...], preferred_element_type=jnp.float32)
         return 0
 
-    lax.fori_loop(0, rows.shape[1] // step, product, 0)
+    lax.fori_loop(0, rows.shape[0] // step, product, 0)
     times = rows.shape[0] // unit - 2
     for time in range(times):
         at = time * unit
@@ -381,11 +374,16 @@
     frame_size, cot_size = 2 * (in_channels // LANES) * width, 2 * splits * width
     count = 2 * frame_count
     block = jnp.concatenate((flat(cotangent[3:]), flat(cotangent[:3]), flat(frames)), axis=0)
-    planes = spread(jnp.concatenate((up_part, mix_part), axis=0), "z")
     early = (count - 3) * cot_size
     first = block.shape[0]
-    following = shift(block[early : count * cot_size + frame_size], PLANES, -1)
-    previous = shift(block[first - 2 * frame_size :], PLANES, 1)
+    payload, following, previous = lax.optimization_barrier(
+        (
+            jnp.concatenate((up_part, mix_part), axis=0),
+            shift(block[early : count * cot_size + frame_size], PLANES, -1),
+            shift(block[first - 2 * frame_size :], PLANES, 1),
+        )
+    )
+    planes = spread(payload, "z")
     block = jnp.concatenate((block, following, previous), axis=0)
     blocks = (block, ring(block, 1), ring(block, -1), ring(block, 2))
     planes, block = lax.optimization_barrier((planes, block))

time: 112 us -> 109 us (0.973)
  the two profiles are of different devices: /device:TPU:1 before, /device:TPU:32 now
where the time goes in v5:
time: 109 us; the launch traced here: 108 us
  starting transfers between devices  46.5 us (43%)
  waiting for transfers between devices  20.7 us (19%)
  blocking collectives  18.5 us (17%)
  Pallas kernels  13.1 us (12%)
  local copies, waits for them, and re-layouts  6.51 us (6%)
  other arithmetic  1.69 us (2%)
    all_to_all x2, starting transfers between devices, spread(): lax.all_to_all(jnp.broadcast_to(array, (count, *array.shape)), axis, 0, 0...  20.7 us
    all_to_all x1, blocking collectives, shards(): parts = lax.all_to_all(parts, RING, 0, 0, tiled=True)  18.5 us
    all_to_all x2, waiting for transfers between devices, spread(): lax.all_to_all(jnp.broadcast_to(array, (count, *array.shape)), axis, 0, 0...  17.1 us
    pallas_call x2, Pallas kernels, call(): pl.pallas_call(kernel, out_shape=outs, in_specs=[pl.BlockSpec(memory_spac...  12.3 us
    ppermute x3, starting transfers between devices, ring(): return lax.ppermute(array, RING, [(i, (i + by) % 4) for i in range(4)])  10.7 us
    ppermute x2, starting transfers between devices, shift(): return lax.ppermute(array, axis, pairs)  6.56 us
    ppermute x1, starting transfers between devices, shards(): mix_other = lax.ppermute(raw_mix, RING, [(0, 3), (3, 0), (1, 2), (2, 1)])  4.67 us
    ppermute x2, starting transfers between devices, swap(): return lax.ppermute(array, 'core', [(0, 1), (1, 0)])  3.83 us
  transfers between devices with their start and end apart: 10, of which 3 were waited for; matrix products, arithmetic and copies ran while one was open for 5% of the time, Pallas kernels for 3%

profile of v5, /device:TPU:32, one launch (start us, length us, event | category | flops | bytes accessed | tf_op | source)
XLA Modules:
  0.0 108.2 jit_solution(16394350699083915476)
XLA Ops:
  0.6 0.0 copy-start
  0.6 0.8 reshape.61
  1.5 4.7 %collective-permute-start = (bf16[54,2,128]{2,0,1:T(8,128)(2,1)S(1)}, bf16[54,2,128]{2,0,1:T(8,128)(2,1)S(1)}, u32[]{:S(2)}, u32[]{:S(2)}) collective-permute-start(bf16[54,2,128]{2,0,1:T(8,128)(2,1)S(1)} %bitcast.62), channel_id=1, source_target_pairs={{0,66},{66,0},{2,64},{64,2},{1,67},{67,1},{3,65},{65,3},{4,70},{70... | collective-permute-start | bytes 82952 | tf_op jit(solution)/shard_map/ppermute | solution.py:348
  6.1 0.9 reshape.57
  7.1 0.9 slice_bitcast_fusion.1
  8.1 4.6 %collective-permute-start.1 = (bf16[432,128]{1,0:T(8,128)(2,1)S(1)}, bf16[432,128]{1,0:T(8,128)(2,1)S(1)}, u32[]{:S(2)}, u32[]{:S(2)}) collective-permute-start(bf16[432,128]{1,0:T(8,128)(2,1)S(1)} %get-tuple-element.16), channel_id=1, source_target_pairs={{4,0},{8,4},{12,8},{16,12},{20,16},{24,20},{28,24},{32,28},{36,32}... | collective-permute-start | bytes 331784 | tf_op jit(solution)/shard_map/ppermute | solution.py:21
  12.8 1.9 %collective-permute-start.2 = (bf16[288,128]{1,0:T(8,128)(2,1)S(1)}, bf16[288,128]{1,0:T(8,128)(2,1)S(1)}, u32[]{:S(2)}, u32[]{:S(2)}) collective-permute-start(bf16[288,128]{1,0:T(8,128)(2,1)S(1)} %bitcast.63), channel_id=1, source_target_pairs={{0,4},{4,8},{8,12},{12,16},{16,20},{20,24},{24,28},{28,32},{32,36}... | collective-permute-start | bytes 221192 | tf_op jit(solution)/shard_map/ppermute | solution.py:21
  14.8 0.0 copy-done
  14.9 0.1 dynamic-slice_reduce_fusion
  15.1 0.0 collective-permute-done
  15.1 0.3 fusion
  15.6 3.5 %collective-permute-done.2 = bf16[288,128]{1,0:T(8,128)(2,1)S(1)} collective-permute-done((bf16[288,128]{1,0:T(8,128)(2,1)S(1)}, bf16[288,128]{1,0:T(8,128)(2,1)S(1)}, u32[]{:S(2)}, u32[]{:S(2)}) %collective-permute-start.2) | collective-permute-done | bytes 73760 | tf_op jit(solution)/shard_map/ppermute | solution.py:21
  19.1 0.0 collective-permute-done.1
  19.1 0.9 broadcast_in_dim.6
  20.0 13.8 %all-to-all-start = ((bf16[16,39,2,128]{3,2,1,0:T(2,128)(2,1)}), bf16[16,39,2,128]{3,2,1,0:T(2,128)(2,1)S(1)}, u32[]{:S(2)}, u32[]{:S(2)}) async-start(bf16[16,39,2,128]{3,2,1,0:T(2,128)(2,1)} %broadcast_in_dim.6), calls=%async_computation | async-start | bytes 638976 | tf_op jit(solution)/shard_map/all_to_all | solution.py:30
  33.8 4.9 %collective-permute-start.5 = (bf16[1728,128]{1,0:T(8,128)(2,1)S(1)}, bf16[1728,128]{1,0:T(8,128)(2,1)S(1)}, u32[]{:S(2)}, u32[]{:S(2)}) collective-permute-start(bf16[1728,128]{1,0:T(8,128)(2,1)S(1)} %constant_dynamic-update-slice_fusion), channel_id=1, source_target_pairs={{0,64},{2,66},{64,0},{66,2},{1,65},{3,67},{65,1},{67,3},{4,68},{6,... | collective-permute-start | bytes 1327112 | tf_op jit(solution)/shard_map/ppermute | solution.py:328
  38.7 1.9 %collective-permute-start.4 = (bf16[1728,128]{1,0:T(8,128)(2,1)S(1)}, bf16[1728,128]{1,0:T(8,128)(2,1)S(1)}, u32[]{:S(2)}, u32[]{:S(2)}) collective-permute-start(bf16[1728,128]{1,0:T(8,128)(2,1)S(1)} %constant_dynamic-update-slice_fusion), channel_id=1, source_target_pairs={{0,66},{2,0},{64,2},{66,64},{1,67},{3,1},{65,3},{67,65},{4,70},{6,... | collective-permute-start | bytes 1327112 | tf_op jit(solution)/shard_map/ppermute | solution.py:328
  40.7 3.9 %collective-permute-start.3 = (bf16[1728,128]{1,0:T(8,128)(2,1)S(1)}, bf16[1728,128]{1,0:T(8,128)(2,1)S(1)}, u32[]{:S(2)}, u32[]{:S(2)}) collective-permute-start(bf16[1728,128]{1,0:T(8,128)(2,1)S(1)} %constant_dynamic-update-slice_fusion), channel_id=1, source_target_pairs={{0,2},{2,64},{64,66},{66,0},{1,3},{3,65},{65,67},{67,1},{4,6},{6,6... | collective-permute-start | bytes 1327112 | tf_op jit(solution)/shard_map/ppermute | solution.py:328
  44.6 7.7 %all-to-all-done = bf16[16,39,2,128]{3,2,1,0:T(2,128)(2,1)S(1)} async-done(((bf16[16,39,2,128]{3,2,1,0:T(2,128)(2,1)}), bf16[16,39,2,128]{3,2,1,0:T(2,128)(2,1)S(1)}, u32[]{:S(2)}, u32[]{:S(2)}) %all-to-all-start) | async-done | bytes 319520 | tf_op jit(solution)/shard_map/all_to_all | solution.py:30
  52.3 0.1 slice_bitcast_fusion
  52.5 0.1 copy.44
  52.7 1.2 %broadcast_in_dim.7 = bf16[4,1248,128]{2,1,0:T(8,128)(2,1)} broadcast(bf16[1248,128]{1,0:T(8,128)(2,1)S(1)} %pad_maximum_fusion.1), dimensions={1,2} | broadcast | bytes 1597440 | tf_op jit(solution)/shard_map/broadcast_in_dim | solution.py:31
  53.9 6.9 %all-to-all-start.1 = ((bf16[4,1248,128]{2,1,0:T(8,128)(2,1)}), bf16[4,1248,128]{2,1,0:T(8,128)(2,1)S(1)}, u32[]{:S(2)}, u32[]{:S(2)}) async-start(bf16[4,1248,128]{2,1,0:T(8,128)(2,1)} %broadcast_in_dim.7), calls=%async_computation.1 | async-start | bytes 2555904 | tf_op jit(solution)/shard_map/all_to_all | solution.py:30
  60.7 0.0 collective-permute-done.5
  60.7 0.0 copy-start.1
  60.7 0.0 collective-permute-done.4
  60.7 0.0 copy-start.2
  60.8 0.0 collective-permute-done.3
  60.8 0.0 copy-start.3
  60.8 0.7 copy-done.1
  61.5 0.1 copy-done.2
  61.6 0.2 copy-done.3
  61.8 1.5 %pad_maximum_fusion.own = bf16[4,1728,128]{2,1,0:T(8,128)(2,1)S(1)} fusion(bf16[1,1728,128]{2,1,0:T(8,128)(2,1)} %bitcast.57, bf16[1,1728,128]{2,1,0:T(8,128)(2,1)} %bitcast.58, bf16[1,1728,128]{2,1,0:T(8,128)(2,1)} %bitcast.59, bf16[1,1728,128]{2,1,0:T(8,128)(2,1)S(1)} %bitcast.55), kind=kLoop, calls=%fused_computation.4 | loop fusion | flops 2654208 | bytes 3538944 | tf_op jit(solution)/shard_map/stack | solution.py:390
  63.3 1.9 %collective-permute-start.6 = (bf16[4,1728,128]{2,1,0:T(8,128)(2,1)S(1)}, bf16[4,1728,128]{2,1,0:T(8,128)(2,1)}, u32[]{:S(2)}, u32[]{:S(2)}) collective-permute-start(bf16[4,1728,128]{2,1,0:T(8,128)(2,1)S(1)} %pad_maximum_fusion.own), channel_id=1, source_target_pairs={{0,1},{1,0},{2,3},{3,2},{4,5},{5,4},{6,7},{7,6},{8,9},{9,8},{10,11... | collective-permute-start | bytes 5308424 | tf_op jit(solution)/shard_map/ppermute | solution.py:25
  65.2 9.4 %all-to-all-done.1.own = bf16[4,1248,128]{2,1,0:T(8,128)(2,1)S(1)} async-done(((bf16[4,1248,128]{2,1,0:T(8,128)(2,1)}), bf16[4,1248,128]{2,1,0:T(8,128)(2,1)S(1)}, u32[]{:S(2)}, u32[]{:S(2)}) %all-to-all-start.1) | async-done | bytes 1277984 | tf_op jit(solution)/shard_map/all_to_all | solution.py:30
  74.6 1.9 %collective-permute-start.7 = (bf16[4,1248,128]{2,1,0:T(8,128)(2,1)S(1)}, bf16[4,1248,128]{2,1,0:T(8,128)(2,1)S(1)}, u32[]{:S(2)}, u32[]{:S(2)}) collective-permute-start(bf16[4,1248,128]{2,1,0:T(8,128)(2,1)S(1)} %all-to-all-done.1.own), channel_id=1, source_target_pairs={{0,1},{1,0},{2,3},{3,2},{4,5},{5,4},{6,7},{7,6},{8,9},{9,8},{10,11... | collective-permute-start | bytes 3833864 | tf_op jit(solution)/shard_map/ppermute | solution.py:25
  76.5 0.1 pad_add_fusion.place
  76.6 0.0 collective-permute-done.6.other
  76.6 3.6 %shard_map.59 = (bf16[768,2304]{1,0:T(8,128)(2,1)S(1)}, bf16[1152,1536]{1,0:T(8,128)(2,1)S(1)}) custom-call(s32[3]{0:T(128)S(1)} %pad_add_fusion.place, bf16[4,1728,128]{2,1,0:T(8,128)(2,1)S(1)} %pad_maximum_fusion.own, bf16[4,1728,128]{2,1,0:T(8,128)(2,1)} %collective-permute-done.6.other), custom_call_target="tpu_custom_call" | custom-call | flops 1000000000 | bytes 8388608 | tf_op jit(solution)/shard_map/pallas_call | solution.py:266
  80.3 0.0 collective-permute-done.7.other
  80.3 8.7 %shard_map.60 = bf16[4,1008,128]{2,1,0:T(8,128)(2,1)S(1)} custom-call(s32[3]{0:T(128)S(1)} %pad_add_fusion.place, bf16[768,2304]{1,0:T(8,128)(2,1)S(1)} %get-tuple-element.10.frame_rows, bf16[1152,1536]{1,0:T(8,128)(2,1)S(1)} %get-tuple-element.11.cot_rows, bf16[4,1248,128]{2,1,0:T(8,128)(2,1)S(1)} %all-to-all-done.1.own, ...), custom_call_target="tpu_custom_call" | custom-call | flops 4000000000 | bytes 8388608 | tf_op jit(solution)/shard_map/pallas_call | solution.py:266
  88.9 18.5 %all_to_all.15.parts = bf16[4,1008,128]{2,1,0:T(8,128)(2,1)S(1)} all-to-all(bf16[4,1008,128]{2,1,0:T(8,128)(2,1)S(1)} %shard_map.60), channel_id=1, replica_groups=mesh['y'=4,'xh'=2,'z'=16,'xl'=2,'core'=2] {'xh','xl'}, dimensions={0} | all-to-all | bytes 2064384 | tf_op jit(solution)/shard_map/all_to_all | solution.py:412
  107.4 0.8 shard_map.61
  (27 shorter events, 0.4 us)
Async XLA Ops:
  0.6 14.2 %copy-start = (bf16[10368,2]{0,1:T(2,128)(2,1)S(1)}, bf16[10368,2]{0,1:T(2,128)(2,1)}, u32[]{:S(2)}) copy-start(bf16[10368,2]{0,1:T(2,128)(2,1)} %param.5) | copy-start | bytes 124420
  1.5 13.6 %collective-permute-start = (bf16[54,2,128]{2,0,1:T(8,128)(2,1)S(1)}, bf16[54,2,128]{2,0,1:T(8,128)(2,1)S(1)}, u32[]{:S(2)}, u32[]{:S(2)}) collective-permute-start(bf16[54,2,128]{2,0,1:T(8,128)(2,1)S(1)} %bitcast.62), channel_id=1, source_target_pairs={{0,66},{66,0},{2,64},{64,2},{1,67},{67,1},{3,65},{65,3},{4,70},{70... | collective-permute-start | bytes 82952 | tf_op jit(solution)/shard_map/ppermute | solution.py:348
  8.1 11.0 %collective-permute-start.1 = (bf16[432,128]{1,0:T(8,128)(2,1)S(1)}, bf16[432,128]{1,0:T(8,128)(2,1)S(1)}, u32[]{:S(2)}, u32[]{:S(2)}) collective-permute-start(bf16[432,128]{1,0:T(8,128)(2,1)S(1)} %get-tuple-element.16), channel_id=1, source_target_pairs={{4,0},{8,4},{12,8},{16,12},{20,16},{24,20},{28,24},{32,28},{36,32}... | collective-permute-start | bytes 331784 | tf_op jit(solution)/shard_map/ppermute | solution.py:21
  12.8 6.2 %collective-permute-start.2 = (bf16[288,128]{1,0:T(8,128)(2,1)S(1)}, bf16[288,128]{1,0:T(8,128)(2,1)S(1)}, u32[]{:S(2)}, u32[]{:S(2)}) collective-permute-start(bf16[288,128]{1,0:T(8,128)(2,1)S(1)} %bitcast.63), channel_id=1, source_target_pairs={{0,4},{4,8},{8,12},{12,16},{16,20},{20,24},{24,28},{28,32},{32,36}... | collective-permute-start | bytes 221192 | tf_op jit(solution)/shard_map/ppermute | solution.py:21
  20.0 32.3 %all-to-all-start = ((bf16[16,39,2,128]{3,2,1,0:T(2,128)(2,1)}), bf16[16,39,2,128]{3,2,1,0:T(2,128)(2,1)S(1)}, u32[]{:S(2)}, u32[]{:S(2)}) async-start(bf16[16,39,2,128]{3,2,1,0:T(2,128)(2,1)} %broadcast_in_dim.6), calls=%async_computation | async-start | bytes 638976 | tf_op jit(solution)/shard_map/all_to_all | solution.py:30
  33.8 26.9 %collective-permute-start.5 = (bf16[1728,128]{1,0:T(8,128)(2,1)S(1)}, bf16[1728,128]{1,0:T(8,128)(2,1)S(1)}, u32[]{:S(2)}, u32[]{:S(2)}) collective-permute-start(bf16[1728,128]{1,0:T(8,128)(2,1)S(1)} %constant_dynamic-update-slice_fusion), channel_id=1, source_target_pairs={{0,64},{2,66},{64,0},{66,2},{1,65},{3,67},{65,1},{67,3},{4,68},{6,... | collective-permute-start | bytes 1327112 | tf_op jit(solution)/shard_map/ppermute | solution.py:328
  38.7 22.0 %collective-permute-start.4 = (bf16[1728,128]{1,0:T(8,128)(2,1)S(1)}, bf16[1728,128]{1,0:T(8,128)(2,1)S(1)}, u32[]{:S(2)}, u32[]{:S(2)}) collective-permute-start(bf16[1728,128]{1,0:T(8,128)(2,1)S(1)} %constant_dynamic-update-slice_fusion), channel_id=1, source_target_pairs={{0,66},{2,0},{64,2},{66,64},{1,67},{3,1},{65,3},{67,65},{4,70},{6,... | collective-permute-start | bytes 1327112 | tf_op jit(solution)/shard_map/ppermute | solution.py:328
  40.7 20.1 %collective-permute-start.3 = (bf16[1728,128]{1,0:T(8,128)(2,1)S(1)}, bf16[1728,128]{1,0:T(8,128)(2,1)S(1)}, u32[]{:S(2)}, u32[]{:S(2)}) collective-permute-start(bf16[1728,128]{1,0:T(8,128)(2,1)S(1)} %constant_dynamic-update-slice_fusion), channel_id=1, source_target_pairs={{0,2},{2,64},{64,66},{66,0},{1,3},{3,65},{65,67},{67,1},{4,6},{6,6... | collective-permute-start | bytes 1327112 | tf_op jit(solution)/shard_map/ppermute | solution.py:328
  53.9 20.8 %all-to-all-start.1 = ((bf16[4,1248,128]{2,1,0:T(8,128)(2,1)}), bf16[4,1248,128]{2,1,0:T(8,128)(2,1)S(1)}, u32[]{:S(2)}, u32[]{:S(2)}) async-start(bf16[4,1248,128]{2,1,0:T(8,128)(2,1)} %broadcast_in_dim.7), calls=%async_computation.1 | async-start | bytes 2555904 | tf_op jit(solution)/shard_map/all_to_all | solution.py:30
  60.7 0.8 copy-start.1
  60.7 0.9 copy-start.2
  60.8 1.1 copy-start.3
  63.3 13.3 %collective-permute-start.6 = (bf16[4,1728,128]{2,1,0:T(8,128)(2,1)S(1)}, bf16[4,1728,128]{2,1,0:T(8,128)(2,1)}, u32[]{:S(2)}, u32[]{:S(2)}) collective-permute-start(bf16[4,1728,128]{2,1,0:T(8,128)(2,1)S(1)} %pad_maximum_fusion.own), channel_id=1, source_target_pairs={{0,1},{1,0},{2,3},{3,2},{4,5},{5,4},{6,7},{7,6},{8,9},{9,8},{10,11... | collective-permute-start | bytes 5308424 | tf_op jit(solution)/shard_map/ppermute | solution.py:25
  74.6 5.7 %collective-permute-start.7 = (bf16[4,1248,128]{2,1,0:T(8,128)(2,1)S(1)}, bf16[4,1248,128]{2,1,0:T(8,128)(2,1)S(1)}, u32[]{:S(2)}, u32[]{:S(2)}) collective-permute-start(bf16[4,1248,128]{2,1,0:T(8,128)(2,1)S(1)} %all-to-all-done.1.own), channel_id=1, source_target_pairs={{0,1},{1,0},{2,3},{3,2},{4,5},{5,4},{6,7},{7,6},{8,9},{9,8},{10,11... | collective-permute-start | bytes 3833864 | tf_op jit(solution)/shard_map/ppermute | solution.py:25

commit v6 on v5

--- a/solution.py
+++ b/solution.py
@@ -90,9 +90,20 @@
             value = high((tile - (up_count - up_half)) * nz, nz)
         return value.reshape(-1, LANES)
 
+    def both(tile):
+        start = up_size + tile * 2 * nz
+        return jnp.stack((low(start, 2 * nz), high(start, 2 * nz)), axis=1).reshape(-1, LANES)
+
     def mix_tile(kt, kw, pair):
-        start = up_size + ((kt * 3 + kw) * 2 + pair) * 2 * nz
-        return jnp.stack((low(start, 2 * nz), high(start, 2 * nz)), axis=1).reshape(-1, LANES)
+        at = kt * 3 + kw
+        if pair == 1:
+            return both(at)
+        ahead = pltpu.roll(both(at).astype(jnp.float32), LANES // 2, 1)
+        last = both(9 + at // 2).astype(jnp.float32)
+        if at % 2 == 0:
+            last = pltpu.roll(last, LANES // 2, 1)
+        lane = lax.broadcasted_iota(jnp.int32, ahead.shape, 1)
+        return jnp.where(lane < LANES // 2, ahead, last).astype(jnp.bfloat16)
 
     return up_tile, mix_tile
 
@@ -195,9 +206,9 @@
 
 
 def backward_kernel(
-    layout, width, place, rows, own, other, out, base, slope, mix_w, partial, evens, odds, up_w, total
+    layout, width, place, rows, own, other, out, base, slope, forward_w, mix_w, partial, evens, odds, up_w, total
 ):
-    up_tile, mix_tile = readers(layout, place, own, other)
+    up_tile, _ = readers(layout, place, own, other)
     channels = rows.shape[1] // 6
     unit = evens.shape[0] - total.shape[0]
     splits = up_w.shape[1] // (2 * LANES)
@@ -206,9 +217,10 @@
         for row in range(2):
             for shift_w in range(3):
                 at = (row * 3 + shift_w) * channels
-                mix_w[at : at + channels, kt * LANES : (kt + 1) * LANES] = mix_tile(
-                    kt, 2 - shift_w, row
-                )
+                lane = (kt * 3 + 2 - shift_w) * LANES
+                mix_w[at : at + channels, kt * LANES : (kt + 1) * LANES] = forward_w[
+                    row * channels : (row + 1) * channels, lane : lane + LANES
+                ]
     step = 3 * unit
 
     def product(k, _):
@@ -258,7 +270,9 @@
     layout, width, base, place, frame_rows, cot_rows, own, other, out, slope, *scratch
 ):
     forward_kernel(layout, width, place, frame_rows, own, other, out, slope, *scratch[:6])
-    backward_kernel(layout, width, place, cot_rows, own, other, out, base, slope, *scratch[6:])
+    backward_kernel(
+        layout, width, place, cot_rows, own, other, out, base, slope, scratch[4], *scratch[6:]
+    )
 
 
 def call(kernel, outs, scratch, flops, megabytes, place, *operands):
@@ -334,7 +348,7 @@
 
 
 def tiles_of(kernel):
-    return kernel.T.reshape(2, -1, LANES).transpose(1, 0, 2)
+    return kernel.reshape(-1, LANES, 2).transpose(0, 2, 1)
 
 
 def shards(frames, up_kernel, mix_kernel, cotangent):
@@ -356,20 +370,23 @@
 
     mix_tiles = jnp.where(xh == core, raw_mix, mix_other)
     splits = out_channels // LANES
-    pick_shape = (3, out_channels, 4 * part)
-    tap = lax.broadcasted_iota(jnp.int32, pick_shape, 0)
+    pick_shape = (2, out_channels, 2 * part)
+    slot = lax.broadcasted_iota(jnp.int32, pick_shape, 0)
     source = lax.broadcasted_iota(jnp.int32, pick_shape, 1)
     target = lax.broadcasted_iota(jnp.int32, pick_shape, 2)
-    pair, side, place = target // (2 * part), target // part % 2, target % part
-    wanted = (place // nz) * (4 * nz) + xh * (2 * nz) + (place % nz) * 2 + xl
-    pick = (source == wanted) & (tap == side + 1 - pair)
+    side, spot = target // part, target % part
+    wanted = (spot // nz) * (4 * nz) + xh * (2 * nz) + (spot % nz) * 2 + xl
+    pick = ((source == wanted) & (slot == side)).astype(jnp.bfloat16)
+    pick = pick.reshape(2, splits, LANES, 2 * part)
+    taps = mix_tiles.reshape(3, 3, 3, splits, 2, LANES).transpose(0, 2, 1, 3, 4, 5)
+    taps = taps.reshape(9, 3, splits, 2, LANES)
+    last = jnp.pad(taps[:, 2], ((0, 1), (0, 0), (0, 0), (0, 0))).reshape(5, 2, splits, 2, LANES)
     mix_part = jnp.einsum(
-        "thwsjl,hslm->twjm",
-        mix_tiles.reshape(3, 3, 3, splits, 2, LANES),
-        pick.astype(jnp.bfloat16).reshape(3, splits, LANES, 4 * part),
+        "thsjl,hslm->tjm",
+        jnp.concatenate((taps[:, :2], last), axis=0),
+        pick,
         preferred_element_type=jnp.float32,
     ).astype(jnp.bfloat16)
-    mix_part = mix_part.reshape(9, 2, 2, 2 * part).transpose(0, 2, 1, 3).reshape(-1, 2, LANES)
 
     frame_size, cot_size = 2 * (in_channels // LANES) * width, 2 * splits * width
     count = 2 * frame_count

time: 109 us -> 105 us (0.963)
  the two profiles are of different devices: /device:TPU:32 before, /device:TPU:1 now
where the time goes in v6:
time: 105 us; the launch traced here: 104 us
  starting transfers between devices  57.3 us (55%)
  blocking collectives  17.4 us (17%)
  Pallas kernels  13.1 us (12%)
  waiting for transfers between devices  7.32 us (7%)
  local copies, waits for them, and re-layouts  6.29 us (6%)
  other arithmetic  1.68 us (2%)
    all_to_all x2, starting transfers between devices, spread(): lax.all_to_all(jnp.broadcast_to(array, (count, *array.shape)), axis, 0, 0...  21.9 us
    all_to_all x1, blocking collectives, shards(): parts = lax.all_to_all(parts, RING, 0, 0, tiled=True)  17.4 us
    ppermute x2, starting transfers between devices, swap(): return lax.ppermute(array, 'core', [(0, 1), (1, 0)])  14.6 us
    pallas_call x2, Pallas kernels, call(): pl.pallas_call(kernel, out_shape=outs, in_specs=[pl.BlockSpec(memory_spac...  12.3 us
    ppermute x3, starting transfers between devices, ring(): return lax.ppermute(array, RING, [(i, (i + by) % 4) for i in range(4)])  10.1 us
    ppermute x2, starting transfers between devices, shift(): return lax.ppermute(array, axis, pairs)  5.47 us
    ppermute x1, starting transfers between devices, shards(): mix_other = lax.ppermute(raw_mix, RING, [(0, 3), (3, 0), (1, 2), (2, 1)])  5.22 us
    ppermute x3, waiting for transfers between devices, ring(): return lax.ppermute(array, RING, [(i, (i + by) % 4) for i in range(4)])  3.82 us
  transfers between devices with their start and end apart: 10, of which 3 were waited for; matrix products, arithmetic and copies ran while one was open for 5% of the time, Pallas kernels for 3%

profile of v6, /device:TPU:1, one launch (start us, length us, event | category | flops | bytes accessed | tf_op | source)
XLA Modules:
  0.0 104.3 jit_solution(15373148011155670660)
XLA Ops:
  0.6 0.0 copy-start
  0.6 0.8 reshape.61
  1.5 5.2 %collective-permute-start = (bf16[54,2,128]{2,0,1:T(8,128)(2,1)S(1)}, bf16[54,2,128]{2,0,1:T(8,128)(2,1)S(1)}, u32[]{:S(2)}, u32[]{:S(2)}) collective-permute-start(bf16[54,2,128]{2,0,1:T(8,128)(2,1)S(1)} %bitcast.67), channel_id=1, source_target_pairs={{0,66},{66,0},{2,64},{64,2},{1,67},{67,1},{3,65},{65,3},{4,70},{70... | collective-permute-start | bytes 82952 | tf_op jit(solution)/shard_map/ppermute | solution.py:362
  6.7 0.9 reshape.57
  7.6 0.9 slice_bitcast_fusion.1
  8.7 1.3 %collective-permute-start.1 = (bf16[432,128]{1,0:T(8,128)(2,1)S(1)}, bf16[432,128]{1,0:T(8,128)(2,1)S(1)}, u32[]{:S(2)}, u32[]{:S(2)}) collective-permute-start(bf16[432,128]{1,0:T(8,128)(2,1)S(1)} %get-tuple-element.16), channel_id=1, source_target_pairs={{4,0},{8,4},{12,8},{16,12},{20,16},{24,20},{28,24},{32,28},{36,32}... | collective-permute-start | bytes 331784 | tf_op jit(solution)/shard_map/ppermute | solution.py:21
  10.0 4.2 %collective-permute-start.2 = (bf16[288,128]{1,0:T(8,128)(2,1)S(1)}, bf16[288,128]{1,0:T(8,128)(2,1)S(1)}, u32[]{:S(2)}, u32[]{:S(2)}) collective-permute-start(bf16[288,128]{1,0:T(8,128)(2,1)S(1)} %bitcast.71), channel_id=1, source_target_pairs={{0,4},{4,8},{8,12},{12,16},{16,20},{20,24},{24,28},{28,32},{32,36}... | collective-permute-start | bytes 221192 | tf_op jit(solution)/shard_map/ppermute | solution.py:21
  14.3 0.0 copy-done
  14.3 0.1 dynamic-slice_reduce_fusion
  14.5 0.0 collective-permute-done
  14.7 0.2 fusion
  15.0 0.7 collective-permute-done.2
  15.6 0.0 collective-permute-done.1
  15.6 0.9 broadcast_in_dim.6
  16.5 16.3 %all-to-all-start = ((bf16[16,35,2,128]{3,2,1,0:T(2,128)(2,1)}), bf16[16,35,2,128]{3,2,1,0:T(2,128)(2,1)S(1)}, u32[]{:S(2)}, u32[]{:S(2)}) async-start(bf16[16,35,2,128]{3,2,1,0:T(2,128)(2,1)} %broadcast_in_dim.6), calls=%async_computation | async-start | bytes 573440 | tf_op jit(solution)/shard_map/all_to_all | solution.py:30
  32.8 4.8 %collective-permute-start.5 = (bf16[1728,128]{1,0:T(8,128)(2,1)S(1)}, bf16[1728,128]{1,0:T(8,128)(2,1)S(1)}, u32[]{:S(2)}, u32[]{:S(2)}) collective-permute-start(bf16[1728,128]{1,0:T(8,128)(2,1)S(1)} %constant_dynamic-update-slice_fusion), channel_id=1, source_target_pairs={{0,64},{2,66},{64,0},{66,2},{1,65},{3,67},{65,1},{67,3},{4,68},{6,... | collective-permute-start | bytes 1327112 | tf_op jit(solution)/shard_map/ppermute | solution.py:342
  37.6 1.9 %collective-permute-start.4 = (bf16[1728,128]{1,0:T(8,128)(2,1)S(1)}, bf16[1728,128]{1,0:T(8,128)(2,1)S(1)}, u32[]{:S(2)}, u32[]{:S(2)}) collective-permute-start(bf16[1728,128]{1,0:T(8,128)(2,1)S(1)} %constant_dynamic-update-slice_fusion), channel_id=1, source_target_pairs={{0,66},{2,0},{64,2},{66,64},{1,67},{3,1},{65,3},{67,65},{4,70},{6,... | collective-permute-start | bytes 1327112 | tf_op jit(solution)/shard_map/ppermute | solution.py:342
  39.6 3.4 %collective-permute-start.3 = (bf16[1728,128]{1,0:T(8,128)(2,1)S(1)}, bf16[1728,128]{1,0:T(8,128)(2,1)S(1)}, u32[]{:S(2)}, u32[]{:S(2)}) collective-permute-start(bf16[1728,128]{1,0:T(8,128)(2,1)S(1)} %constant_dynamic-update-slice_fusion), channel_id=1, source_target_pairs={{0,2},{2,64},{64,66},{66,0},{1,3},{3,65},{65,67},{67,1},{4,6},{6,6... | collective-permute-start | bytes 1327112 | tf_op jit(solution)/shard_map/ppermute | solution.py:342
  42.9 2.8 %all-to-all-done = bf16[16,35,2,128]{3,2,1,0:T(2,128)(2,1)S(1)} async-done(((bf16[16,35,2,128]{3,2,1,0:T(2,128)(2,1)}), bf16[16,35,2,128]{3,2,1,0:T(2,128)(2,1)S(1)}, u32[]{:S(2)}, u32[]{:S(2)}) %all-to-all-start) | async-done | bytes 286752 | tf_op jit(solution)/shard_map/all_to_all | solution.py:30
  45.8 0.1 slice_bitcast_fusion
  45.9 0.1 copy.40
  46.0 1.2 %broadcast_in_dim.7 = bf16[4,1120,128]{2,1,0:T(8,128)(2,1)} broadcast(bf16[1120,128]{1,0:T(8,128)(2,1)S(1)} %pad_maximum_fusion.1), dimensions={1,2} | broadcast | bytes 1433600 | tf_op jit(solution)/shard_map/broadcast_in_dim | solution.py:31
  47.2 5.6 %all-to-all-start.1 = ((bf16[4,1120,128]{2,1,0:T(8,128)(2,1)}), bf16[4,1120,128]{2,1,0:T(8,128)(2,1)S(1)}, u32[]{:S(2)}, u32[]{:S(2)}) async-start(bf16[4,1120,128]{2,1,0:T(8,128)(2,1)} %broadcast_in_dim.7), calls=%async_computation.1 | async-start | bytes 2293760 | tf_op jit(solution)/shard_map/all_to_all | solution.py:30
  52.8 0.0 collective-permute-done.5
  52.8 0.0 copy-start.1
  52.8 3.8 %collective-permute-done.4 = bf16[1728,128]{1,0:T(8,128)(2,1)S(1)} collective-permute-done((bf16[1728,128]{1,0:T(8,128)(2,1)S(1)}, bf16[1728,128]{1,0:T(8,128)(2,1)S(1)}, u32[]{:S(2)}, u32[]{:S(2)}) %collective-permute-start.4) | collective-permute-done | bytes 442400 | tf_op jit(solution)/shard_map/ppermute | solution.py:342
  56.6 0.0 copy-start.2
  56.6 0.0 collective-permute-done.3
  56.6 0.0 copy-start.3
  56.6 0.0 copy-done.1
  56.7 0.7 copy-done.2
  57.4 0.2 copy-done.3
  57.6 1.5 %pad_maximum_fusion.own = bf16[4,1728,128]{2,1,0:T(8,128)(2,1)S(1)} fusion(bf16[1,1728,128]{2,1,0:T(8,128)(2,1)} %bitcast.62, bf16[1,1728,128]{2,1,0:T(8,128)(2,1)} %bitcast.63, bf16[1,1728,128]{2,1,0:T(8,128)(2,1)} %bitcast.64, bf16[1,1728,128]{2,1,0:T(8,128)(2,1)S(1)} %bitcast.60), kind=kLoop, calls=%fused_computation | loop fusion | flops 2654208 | bytes 3538944 | tf_op jit(solution)/shard_map/stack | solution.py:407
  59.1 5.8 %collective-permute-start.6 = (bf16[4,1728,128]{2,1,0:T(8,128)(2,1)S(1)}, bf16[4,1728,128]{2,1,0:T(8,128)(2,1)}, u32[]{:S(2)}, u32[]{:S(2)}) collective-permute-start(bf16[4,1728,128]{2,1,0:T(8,128)(2,1)S(1)} %pad_maximum_fusion.own), channel_id=1, source_target_pairs={{0,1},{1,0},{2,3},{3,2},{4,5},{5,4},{6,7},{7,6},{8,9},{9,8},{10,11... | collective-permute-start | bytes 5308424 | tf_op jit(solution)/shard_map/ppermute | solution.py:25
  64.9 0.0 all-to-all-done.1.own
  64.9 8.8 %collective-permute-start.7 = (bf16[4,1120,128]{2,1,0:T(8,128)(2,1)S(1)}, bf16[4,1120,128]{2,1,0:T(8,128)(2,1)S(1)}, u32[]{:S(2)}, u32[]{:S(2)}) collective-permute-start(bf16[4,1120,128]{2,1,0:T(8,128)(2,1)S(1)} %all-to-all-done.1.own), channel_id=1, source_target_pairs={{0,1},{1,0},{2,3},{3,2},{4,5},{5,4},{6,7},{7,6},{8,9},{9,8},{10,11... | collective-permute-start | bytes 3440648 | tf_op jit(solution)/shard_map/ppermute | solution.py:25
  73.7 0.1 pad_add_fusion.place
  73.8 0.0 collective-permute-done.6.other
  73.8 3.6 %shard_map.59 = (bf16[768,2304]{1,0:T(8,128)(2,1)S(1)}, bf16[1152,1536]{1,0:T(8,128)(2,1)S(1)}) custom-call(s32[3]{0:T(128)S(1)} %pad_add_fusion.place, bf16[4,1728,128]{2,1,0:T(8,128)(2,1)S(1)} %pad_maximum_fusion.own, bf16[4,1728,128]{2,1,0:T(8,128)(2,1)} %collective-permute-done.6.other), custom_call_target="tpu_custom_call" | custom-call | flops 1000000000 | bytes 8388608 | tf_op jit(solution)/shard_map/pallas_call | solution.py:280
  77.5 0.0 collective-permute-done.7.other
  77.5 8.7 %shard_map.60 = bf16[4,1008,128]{2,1,0:T(8,128)(2,1)S(1)} custom-call(s32[3]{0:T(128)S(1)} %pad_add_fusion.place, bf16[768,2304]{1,0:T(8,128)(2,1)S(1)} %get-tuple-element.10.frame_rows, bf16[1152,1536]{1,0:T(8,128)(2,1)S(1)} %get-tuple-element.11.cot_rows, bf16[4,1120,128]{2,1,0:T(8,128)(2,1)S(1)} %all-to-all-done.1.own, ...), custom_call_target="tpu_custom_call" | custom-call | flops 4000000000 | bytes 8388608 | tf_op jit(solution)/shard_map/pallas_call | solution.py:280
  86.2 17.4 %all_to_all.15.parts = bf16[4,1008,128]{2,1,0:T(8,128)(2,1)S(1)} all-to-all(bf16[4,1008,128]{2,1,0:T(8,128)(2,1)S(1)} %shard_map.60), channel_id=1, replica_groups=mesh['y'=4,'xh'=2,'z'=16,'xl'=2,'core'=2] {'xh','xl'}, dimensions={0} | all-to-all | bytes 2064384 | tf_op jit(solution)/shard_map/all_to_all | solution.py:429
  103.5 0.8 shard_map.61
  (29 shorter events, 0.5 us)
Async XLA Ops:
  0.6 13.6 %copy-start = (bf16[10368,2]{0,1:T(2,128)(2,1)S(1)}, bf16[10368,2]{0,1:T(2,128)(2,1)}, u32[]{:S(2)}) copy-start(bf16[10368,2]{0,1:T(2,128)(2,1)} %param.5) | copy-start | bytes 124420
  1.5 13.1 %collective-permute-start = (bf16[54,2,128]{2,0,1:T(8,128)(2,1)S(1)}, bf16[54,2,128]{2,0,1:T(8,128)(2,1)S(1)}, u32[]{:S(2)}, u32[]{:S(2)}) collective-permute-start(bf16[54,2,128]{2,0,1:T(8,128)(2,1)S(1)} %bitcast.67), channel_id=1, source_target_pairs={{0,66},{66,0},{2,64},{64,2},{1,67},{67,1},{3,65},{65,3},{4,70},{70... | collective-permute-start | bytes 82952 | tf_op jit(solution)/shard_map/ppermute | solution.py:362
  8.7 6.9 %collective-permute-start.1 = (bf16[432,128]{1,0:T(8,128)(2,1)S(1)}, bf16[432,128]{1,0:T(8,128)(2,1)S(1)}, u32[]{:S(2)}, u32[]{:S(2)}) collective-permute-start(bf16[432,128]{1,0:T(8,128)(2,1)S(1)} %get-tuple-element.16), channel_id=1, source_target_pairs={{4,0},{8,4},{12,8},{16,12},{20,16},{24,20},{28,24},{32,28},{36,32}... | collective-permute-start | bytes 331784 | tf_op jit(solution)/shard_map/ppermute | solution.py:21
  10.0 5.6 %collective-permute-start.2 = (bf16[288,128]{1,0:T(8,128)(2,1)S(1)}, bf16[288,128]{1,0:T(8,128)(2,1)S(1)}, u32[]{:S(2)}, u32[]{:S(2)}) collective-permute-start(bf16[288,128]{1,0:T(8,128)(2,1)S(1)} %bitcast.71), channel_id=1, source_target_pairs={{0,4},{4,8},{8,12},{12,16},{16,20},{20,24},{24,28},{28,32},{32,36}... | collective-permute-start | bytes 221192 | tf_op jit(solution)/shard_map/ppermute | solution.py:21
  16.5 29.3 %all-to-all-start = ((bf16[16,35,2,128]{3,2,1,0:T(2,128)(2,1)}), bf16[16,35,2,128]{3,2,1,0:T(2,128)(2,1)S(1)}, u32[]{:S(2)}, u32[]{:S(2)}) async-start(bf16[16,35,2,128]{3,2,1,0:T(2,128)(2,1)} %broadcast_in_dim.6), calls=%async_computation | async-start | bytes 573440 | tf_op jit(solution)/shard_map/all_to_all | solution.py:30
  32.8 20.0 %collective-permute-start.5 = (bf16[1728,128]{1,0:T(8,128)(2,1)S(1)}, bf16[1728,128]{1,0:T(8,128)(2,1)S(1)}, u32[]{:S(2)}, u32[]{:S(2)}) collective-permute-start(bf16[1728,128]{1,0:T(8,128)(2,1)S(1)} %constant_dynamic-update-slice_fusion), channel_id=1, source_target_pairs={{0,64},{2,66},{64,0},{66,2},{1,65},{3,67},{65,1},{67,3},{4,68},{6,... | collective-permute-start | bytes 1327112 | tf_op jit(solution)/shard_map/ppermute | solution.py:342
  37.6 19.0 %collective-permute-start.4 = (bf16[1728,128]{1,0:T(8,128)(2,1)S(1)}, bf16[1728,128]{1,0:T(8,128)(2,1)S(1)}, u32[]{:S(2)}, u32[]{:S(2)}) collective-permute-start(bf16[1728,128]{1,0:T(8,128)(2,1)S(1)} %constant_dynamic-update-slice_fusion), channel_id=1, source_target_pairs={{0,66},{2,0},{64,2},{66,64},{1,67},{3,1},{65,3},{67,65},{4,70},{6,... | collective-permute-start | bytes 1327112 | tf_op jit(solution)/shard_map/ppermute | solution.py:342
  39.6 17.1 %collective-permute-start.3 = (bf16[1728,128]{1,0:T(8,128)(2,1)S(1)}, bf16[1728,128]{1,0:T(8,128)(2,1)S(1)}, u32[]{:S(2)}, u32[]{:S(2)}) collective-permute-start(bf16[1728,128]{1,0:T(8,128)(2,1)S(1)} %constant_dynamic-update-slice_fusion), channel_id=1, source_target_pairs={{0,2},{2,64},{64,66},{66,0},{1,3},{3,65},{65,67},{67,1},{4,6},{6,6... | collective-permute-start | bytes 1327112 | tf_op jit(solution)/shard_map/ppermute | solution.py:342
  47.2 17.7 %all-to-all-start.1 = ((bf16[4,1120,128]{2,1,0:T(8,128)(2,1)}), bf16[4,1120,128]{2,1,0:T(8,128)(2,1)S(1)}, u32[]{:S(2)}, u32[]{:S(2)}) async-start(bf16[4,1120,128]{2,1,0:T(8,128)(2,1)} %broadcast_in_dim.7), calls=%async_computation.1 | async-start | bytes 2293760 | tf_op jit(solution)/shard_map/all_to_all | solution.py:30
  52.8 3.8 %copy-start.1 = (bf16[1728,128]{1,0:T(8,128)(2,1)}, bf16[1728,128]{1,0:T(8,128)(2,1)S(1)}, u32[]{:S(2)}) copy-start(bf16[1728,128]{1,0:T(8,128)(2,1)S(1)} %collective-permute-done.5) | copy-start | bytes 1327108
  56.6 0.7 copy-start.2
  56.6 0.9 copy-start.3
  59.1 14.7 %collective-permute-start.6 = (bf16[4,1728,128]{2,1,0:T(8,128)(2,1)S(1)}, bf16[4,1728,128]{2,1,0:T(8,128)(2,1)}, u32[]{:S(2)}, u32[]{:S(2)}) collective-permute-start(bf16[4,1728,128]{2,1,0:T(8,128)(2,1)S(1)} %pad_maximum_fusion.own), channel_id=1, source_target_pairs={{0,1},{1,0},{2,3},{3,2},{4,5},{5,4},{6,7},{7,6},{8,9},{9,8},{10,11... | collective-permute-start | bytes 5308424 | tf_op jit(solution)/shard_map/ppermute | solution.py:25
  64.9 12.5 %collective-permute-start.7 = (bf16[4,1120,128]{2,1,0:T(8,128)(2,1)S(1)}, bf16[4,1120,128]{2,1,0:T(8,128)(2,1)S(1)}, u32[]{:S(2)}, u32[]{:S(2)}) collective-permute-start(bf16[4,1120,128]{2,1,0:T(8,128)(2,1)S(1)} %all-to-all-done.1.own), channel_id=1, source_target_pairs={{0,1},{1,0},{2,3},{3,2},{4,5},{5,4},{6,7},{7,6},{8,9},{9,8},{10,11... | collective-permute-start | bytes 3440648 | tf_op jit(solution)/shard_map/ppermute | solution.py:25

commit v7 on v6

--- a/solution.py
+++ b/solution.py
@@ -12,7 +12,6 @@
 RING = ("xh", "xl")
 LANES = 128
 PAD = 32
-OFFSETS = (0, 3, 1, 2)
 
 
 def shift(array, axis, by):
@@ -109,13 +108,13 @@
 
 
 def forward_kernel(
-    layout, width, place, rows, own, other, out, slope, up_w, ups, mask, hidden, mix_w, total
+    layout, width, place, rows, own, other, outs, slope, up_w, ups, mask, hidden, mix_w, total
 ):
     up_tile, mix_tile = readers(layout, place, own, other)
     splits = rows.shape[1] // (6 * LANES)
     part, unit = up_w.shape[0] // 6, mask.shape[0]
     column = lax.broadcasted_iota(jnp.int32, (PAD, LANES), 0) - 1
-    for block in range(out.shape[0]):
+    for block in range(len(outs)):
         side = (place[1] + (block + 1) // 2) % 2
         at = (2 * side + place[2]) * width + column
         inside = (at >= 0) & (at < 4 * width)
@@ -175,38 +174,38 @@
             (((1,), (1,)), ((), ())),
             preferred_element_type=jnp.float32,
         )
-    store(place, out, total, 0, total.shape[0] // unit, channels, width)
-
-
-def store(place, out, total, base, times, channels, width):
+    store(outs, total, 0, total.shape[0] // unit, channels, width)
+
+
+def store(outs, total, base, times, channels, width):
     splits = channels // LANES
-    for block in range(out.shape[0]):
-        member = (2 * place[0] + place[1] + OFFSETS[block]) % 4
+    for block, out in enumerate(outs):
         for time in range(times):
-            at = (time * out.shape[0] + block) * PAD
+            at = (time * len(outs) + block) * PAD
             for tile in range(2 * splits):
                 first = base + (time * 2 * splits + tile) * width
                 value = total[at : at + width, tile * LANES : (tile + 1) * LANES]
-                out[member, first : first + width, :] = value.astype(jnp.bfloat16)
-
-
-def add_kernel(sizes, parts, *outs):
+                out[first : first + width, :] = value.astype(jnp.bfloat16)
+
+
+def add_kernel(sizes, *refs):
+    parts, outs = refs[:4], refs[4:]
     first = 0
     for out, (times, splits, width) in zip(outs, sizes, strict=True):
         for time in range(times):
             for row in range(2):
                 for split in range(splits):
                     rows = slice(first, first + width)
-                    total = parts[0, rows, :].astype(jnp.float32)
-                    for member in range(1, parts.shape[0]):
-                        total = total + parts[member, rows, :].astype(jnp.float32)
+                    total = parts[0][rows, :].astype(jnp.float32)
+                    for part in parts[1:]:
+                        total = total + part[rows, :].astype(jnp.float32)
                     lanes = slice(split * LANES, (split + 1) * LANES)
                     out[time, row, :, lanes] = total.astype(jnp.bfloat16)
                     first += width
 
 
 def backward_kernel(
-    layout, width, place, rows, own, other, out, base, slope, forward_w, mix_w, partial, evens, odds, up_w, total
+    layout, width, place, rows, own, other, outs, base, slope, forward_w, mix_w, partial, evens, odds, up_w, total
 ):
     up_tile, _ = readers(layout, place, own, other)
     channels = rows.shape[1] // 6
@@ -263,15 +262,14 @@
             up_w[kt * 3 * LANES : (kt + 1) * 3 * LANES, :],
             preferred_element_type=jnp.float32,
         )
-    store(place, out, total, base, count // unit, splits * LANES, width)
-
-
-def compute_kernel(
-    layout, width, base, place, frame_rows, cot_rows, own, other, out, slope, *scratch
-):
-    forward_kernel(layout, width, place, frame_rows, own, other, out, slope, *scratch[:6])
+    store(outs, total, base, count // unit, splits * LANES, width)
+
+
+def compute_kernel(layout, width, base, place, frame_rows, cot_rows, own, other, *refs):
+    outs, slope, scratch = refs[:4], refs[4], refs[5:]
+    forward_kernel(layout, width, place, frame_rows, own, other, outs, slope, *scratch[:6])
     backward_kernel(
-        layout, width, place, cot_rows, own, other, out, base, slope, scratch[4], *scratch[6:]
+        layout, width, place, cot_rows, own, other, outs, base, slope, scratch[4], *scratch[6:]
     )
 
 
@@ -320,7 +318,7 @@
         pltpu.VMEM((times // 2 * unit, 2 * in_channels), jnp.float32),
     ]
     kernel = functools.partial(compute_kernel, layout, width, base)
-    out = jax.ShapeDtypeStruct((blocks, rows, LANES), jnp.bfloat16)
+    out = (jax.ShapeDtypeStruct((rows, LANES), jnp.bfloat16),) * blocks
     return call(kernel, out, scratch, 4 * 10**9, 32, place, frame_rows, cot_rows, own, other)
 
 
@@ -332,10 +330,10 @@
             jax.ShapeDtypeStruct((times, 2, width, splits * LANES), jnp.bfloat16)
             for times, splits, width in sizes
         ),
-        in_specs=[space],
+        in_specs=[space] * len(parts),
         out_specs=(space, space),
         compiler_params=pltpu.CompilerParams(vmem_limit_bytes=8 * 2**20),
-    )(parts)
+    )(*parts)
 
 
 def ring(array, by):
@@ -426,7 +424,7 @@
     parts = compute(
         layout, place, frame_rows, cot_rows, own, other, width, out_channels, in_channels
     )
-    parts = lax.all_to_all(parts, RING, 0, 0, tiled=True)
+    parts = (parts[0], ring(parts[3], 2), ring(parts[1], -1), ring(parts[2], 1))
     outs = ((count, splits, width), (frame_count, in_channels // LANES, width))
     return add_parts(parts, outs)
 

time: 105 us -> 104 us (level)
  blocking collectives: 17.4 us -> 0 us
  starting transfers between devices: 57.3 us -> 66 us
  waiting for transfers between devices: 7.32 us -> 15.4 us
    all_to_all x1 -> x0, blocking collectives: 17.4 us -> none  [shards(): parts = lax.all_to_all(parts, RING, 0, 0, tiled=True)]
    ppermute x3 -> x6, starting transfers between devices: 10.1 us -> 18.8 us  [ring(): return lax.ppermute(array, RING, [(i, (i + by) % 4) for i in range(4)])]
    ppermute x3 -> x6, waiting for transfers between devices: 3.82 us -> 11.9 us  [ring(): return lax.ppermute(array, RING, [(i, (i + by) % 4) for i in range(4)])]
  transfers between devices with their start and end apart: 10 -> 13, of which waited for: 3 -> 6; matrix products, arithmetic and copies ran while one was open for 5% -> 5% of each run, Pallas kernels for 3% -> 4%
where the time goes in v7:
time: 104 us
  starting transfers between devices  66 us (63%)
  waiting for transfers between devices  15.4 us (15%)
  Pallas kernels  13 us (12%)
  local copies, waits for them, and re-layouts  6.32 us (6%)
  other arithmetic  1.68 us (2%)
  between operations  1.04 us (1%)
    all_to_all x2, starting transfers between devices, spread(): lax.all_to_all(jnp.broadcast_to(array, (count, *array.shape)), axis, 0, 0...  21.9 us
    ppermute x6, starting transfers between devices, ring(): return lax.ppermute(array, RING, [(i, (i + by) % 4) for i in range(4)])  18.8 us
    ppermute x2, starting transfers between devices, swap(): return lax.ppermute(array, 'core', [(0, 1), (1, 0)])  14.6 us
    pallas_call x2, Pallas kernels, call(): pl.pallas_call(kernel, out_shape=outs, in_specs=[pl.BlockSpec(memory_spac...  12.3 us
    ppermute x6, waiting for transfers between devices, ring(): return lax.ppermute(array, RING, [(i, (i + by) % 4) for i in range(4)])  11.9 us
    ppermute x2, starting transfers between devices, shift(): return lax.ppermute(array, axis, pairs)  5.47 us
    ppermute x1, starting transfers between devices, shards(): mix_other = lax.ppermute(raw_mix, RING, [(0, 3), (3, 0), (1, 2), (2, 1)])  5.22 us
    all_to_all x2, waiting for transfers between devices, spread(): lax.all_to_all(jnp.broadcast_to(array, (count, *array.shape)), axis, 0, 0...  2.84 us
  transfers between devices with their start and end apart: 13, of which 6 were waited for; matrix products, arithmetic and copies ran while one was open for 5% of the time, Pallas kernels for 4%

profile of v7, /device:TPU:1, one launch (start us, length us, event | category | flops | bytes accessed | tf_op | source)
XLA Modules:
  0.0 103.7 jit_solution(16320604580748811279)
XLA Ops:
  0.6 0.0 copy-start
  0.6 0.8 reshape.61
  1.5 5.2 %collective-permute-start = (bf16[54,2,128]{2,0,1:T(8,128)(2,1)S(1)}, bf16[54,2,128]{2,0,1:T(8,128)(2,1)S(1)}, u32[]{:S(2)}, u32[]{:S(2)}) collective-permute-start(bf16[54,2,128]{2,0,1:T(8,128)(2,1)S(1)} %bitcast.67), channel_id=1, source_target_pairs={{0,66},{66,0},{2,64},{64,2},{1,67},{67,1},{3,65},{65,3},{4,70},{70... | collective-permute-start | bytes 82952 | tf_op jit(solution)/shard_map/ppermute | solution.py:360
  6.7 0.9 reshape.57
  7.6 0.9 slice_bitcast_fusion.1
  8.7 1.3 %collective-permute-start.1 = (bf16[432,128]{1,0:T(8,128)(2,1)S(1)}, bf16[432,128]{1,0:T(8,128)(2,1)S(1)}, u32[]{:S(2)}, u32[]{:S(2)}) collective-permute-start(bf16[432,128]{1,0:T(8,128)(2,1)S(1)} %get-tuple-element.24), channel_id=1, source_target_pairs={{4,0},{8,4},{12,8},{16,12},{20,16},{24,20},{28,24},{32,28},{36,32}... | collective-permute-start | bytes 331784 | tf_op jit(solution)/shard_map/ppermute | solution.py:20
  10.0 4.2 %collective-permute-start.2 = (bf16[288,128]{1,0:T(8,128)(2,1)S(1)}, bf16[288,128]{1,0:T(8,128)(2,1)S(1)}, u32[]{:S(2)}, u32[]{:S(2)}) collective-permute-start(bf16[288,128]{1,0:T(8,128)(2,1)S(1)} %bitcast.71), channel_id=1, source_target_pairs={{0,4},{4,8},{8,12},{12,16},{16,20},{20,24},{24,28},{28,32},{32,36}... | collective-permute-start | bytes 221192 | tf_op jit(solution)/shard_map/ppermute | solution.py:20
  14.3 0.0 copy-done
  14.3 0.1 dynamic-slice_reduce_fusion
  14.5 0.0 collective-permute-done
  14.7 0.2 fusion
  15.0 0.7 collective-permute-done.2
  15.6 0.0 collective-permute-done.1
  15.6 0.9 broadcast_in_dim.6
  16.5 16.3 %all-to-all-start = ((bf16[16,35,2,128]{3,2,1,0:T(2,128)(2,1)}), bf16[16,35,2,128]{3,2,1,0:T(2,128)(2,1)S(1)}, u32[]{:S(2)}, u32[]{:S(2)}) async-start(bf16[16,35,2,128]{3,2,1,0:T(2,128)(2,1)} %broadcast_in_dim.6), calls=%async_computation | async-start | bytes 573440 | tf_op jit(solution)/shard_map/all_to_all | solution.py:29
  32.8 4.8 %collective-permute-start.5 = (bf16[1728,128]{1,0:T(8,128)(2,1)S(1)}, bf16[1728,128]{1,0:T(8,128)(2,1)S(1)}, u32[]{:S(2)}, u32[]{:S(2)}) collective-permute-start(bf16[1728,128]{1,0:T(8,128)(2,1)S(1)} %constant_dynamic-update-slice_fusion), channel_id=1, source_target_pairs={{0,64},{2,66},{64,0},{66,2},{1,65},{3,67},{65,1},{67,3},{4,68},{6,... | collective-permute-start | bytes 1327112 | tf_op jit(solution)/shard_map/ppermute | solution.py:340
  37.6 1.9 %collective-permute-start.4 = (bf16[1728,128]{1,0:T(8,128)(2,1)S(1)}, bf16[1728,128]{1,0:T(8,128)(2,1)S(1)}, u32[]{:S(2)}, u32[]{:S(2)}) collective-permute-start(bf16[1728,128]{1,0:T(8,128)(2,1)S(1)} %constant_dynamic-update-slice_fusion), channel_id=1, source_target_pairs={{0,66},{2,0},{64,2},{66,64},{1,67},{3,1},{65,3},{67,65},{4,70},{6,... | collective-permute-start | bytes 1327112 | tf_op jit(solution)/shard_map/ppermute | solution.py:340
  39.6 3.4 %collective-permute-start.3 = (bf16[1728,128]{1,0:T(8,128)(2,1)S(1)}, bf16[1728,128]{1,0:T(8,128)(2,1)S(1)}, u32[]{:S(2)}, u32[]{:S(2)}) collective-permute-start(bf16[1728,128]{1,0:T(8,128)(2,1)S(1)} %constant_dynamic-update-slice_fusion), channel_id=1, source_target_pairs={{0,2},{2,64},{64,66},{66,0},{1,3},{3,65},{65,67},{67,1},{4,6},{6,6... | collective-permute-start | bytes 1327112 | tf_op jit(solution)/shard_map/ppermute | solution.py:340
  42.9 2.8 %all-to-all-done = bf16[16,35,2,128]{3,2,1,0:T(2,128)(2,1)S(1)} async-done(((bf16[16,35,2,128]{3,2,1,0:T(2,128)(2,1)}), bf16[16,35,2,128]{3,2,1,0:T(2,128)(2,1)S(1)}, u32[]{:S(2)}, u32[]{:S(2)}) %all-to-all-start) | async-done | bytes 286752 | tf_op jit(solution)/shard_map/all_to_all | solution.py:29
  45.8 0.1 slice_bitcast_fusion
  45.9 0.1 copy.40
  46.1 1.2 %broadcast_in_dim.7 = bf16[4,1120,128]{2,1,0:T(8,128)(2,1)} broadcast(bf16[1120,128]{1,0:T(8,128)(2,1)S(1)} %pad_maximum_fusion.1), dimensions={1,2} | broadcast | bytes 1433600 | tf_op jit(solution)/shard_map/broadcast_in_dim | solution.py:30
  47.2 5.6 %all-to-all-start.1 = ((bf16[4,1120,128]{2,1,0:T(8,128)(2,1)}), bf16[4,1120,128]{2,1,0:T(8,128)(2,1)S(1)}, u32[]{:S(2)}, u32[]{:S(2)}) async-start(bf16[4,1120,128]{2,1,0:T(8,128)(2,1)} %broadcast_in_dim.7), calls=%async_computation.1 | async-start | bytes 2293760 | tf_op jit(solution)/shard_map/all_to_all | solution.py:29
  52.8 0.0 collective-permute-done.5
  52.8 0.0 copy-start.1
  52.8 3.8 %collective-permute-done.4 = bf16[1728,128]{1,0:T(8,128)(2,1)S(1)} collective-permute-done((bf16[1728,128]{1,0:T(8,128)(2,1)S(1)}, bf16[1728,128]{1,0:T(8,128)(2,1)S(1)}, u32[]{:S(2)}, u32[]{:S(2)}) %collective-permute-start.4) | collective-permute-done | bytes 442400 | tf_op jit(solution)/shard_map/ppermute | solution.py:340
  56.7 0.0 copy-start.2
  56.7 0.0 collective-permute-done.3
  56.7 0.0 copy-start.3
  56.7 0.0 copy-done.1
  56.7 0.8 copy-done.2
  57.4 0.2 copy-done.3
  57.6 1.5 %pad_maximum_fusion.own = bf16[4,1728,128]{2,1,0:T(8,128)(2,1)S(1)} fusion(bf16[1,1728,128]{2,1,0:T(8,128)(2,1)} %bitcast.62, bf16[1,1728,128]{2,1,0:T(8,128)(2,1)} %bitcast.63, bf16[1,1728,128]{2,1,0:T(8,128)(2,1)} %bitcast.64, bf16[1,1728,128]{2,1,0:T(8,128)(2,1)S(1)} %bitcast.60), kind=kLoop, calls=%fused_computation | loop fusion | flops 2654208 | bytes 3538944 | tf_op jit(solution)/shard_map/stack | solution.py:405
  59.1 5.8 %collective-permute-start.6 = (bf16[4,1728,128]{2,1,0:T(8,128)(2,1)S(1)}, bf16[4,1728,128]{2,1,0:T(8,128)(2,1)}, u32[]{:S(2)}, u32[]{:S(2)}) collective-permute-start(bf16[4,1728,128]{2,1,0:T(8,128)(2,1)S(1)} %pad_maximum_fusion.own), channel_id=1, source_target_pairs={{0,1},{1,0},{2,3},{3,2},{4,5},{5,4},{6,7},{7,6},{8,9},{9,8},{10,11... | collective-permute-start | bytes 5308424 | tf_op jit(solution)/shard_map/ppermute | solution.py:24
  64.9 0.0 all-to-all-done.1.own
  64.9 8.8 %collective-permute-start.7 = (bf16[4,1120,128]{2,1,0:T(8,128)(2,1)S(1)}, bf16[4,1120,128]{2,1,0:T(8,128)(2,1)S(1)}, u32[]{:S(2)}, u32[]{:S(2)}) collective-permute-start(bf16[4,1120,128]{2,1,0:T(8,128)(2,1)S(1)} %all-to-all-done.1.own), channel_id=1, source_target_pairs={{0,1},{1,0},{2,3},{3,2},{4,5},{5,4},{6,7},{7,6},{8,9},{9,8},{10,11... | collective-permute-start | bytes 3440648 | tf_op jit(solution)/shard_map/ppermute | solution.py:24
  73.7 0.1 pad_add_fusion.place
  73.8 0.0 collective-permute-done.6.other
  73.8 3.6 %shard_map.59 = (bf16[768,2304]{1,0:T(8,128)(2,1)S(1)}, bf16[1152,1536]{1,0:T(8,128)(2,1)S(1)}) custom-call(s32[3]{0:T(128)S(1)} %pad_add_fusion.place, bf16[4,1728,128]{2,1,0:T(8,128)(2,1)S(1)} %pad_maximum_fusion.own, bf16[4,1728,128]{2,1,0:T(8,128)(2,1)} %collective-permute-done.6.other), custom_call_target="tpu_custom_call" | custom-call | flops 1000000000 | bytes 8388608 | tf_op jit(solution)/shard_map/pallas_call | solution.py:278
  77.5 0.0 collective-permute-done.7.other
  77.5 8.6 %shard_map.60 = (bf16[1008,128]{1,0:T(8,128)(2,1)S(1)}, bf16[1008,128]{1,0:T(8,128)(2,1)S(1)}, bf16[1008,128]{1,0:T(8,128)(2,1)S(1)}, bf16[1008,128]{1,0:T(8,128)(2,1)S(1)}) custom-call(s32[3]{0:T(128)S(1)} %pad_add_fusion.place, bf16[768,2304]{1,0:T(8,128)(2,1)S(1)} %get-tuple-element.14.frame_rows, bf16[1152,1536]{1,0:T(8,128)(2,1)S(1)} %get-tuple-element.15.cot_rows, ...), custom_call_target="tpu_custom_call" | custom-call | flops 4000000000 | bytes 8388608 | tf_op jit(solution)/shard_map/pallas_call | solution.py:278
  86.1 3.5 %collective-permute-start.8 = (bf16[1008,128]{1,0:T(8,128)(2,1)S(1)}, bf16[1008,128]{1,0:T(8,128)(2,1)S(1)}, u32[]{:S(2)}, u32[]{:S(2)}) collective-permute-start(bf16[1008,128]{1,0:T(8,128)(2,1)S(1)} %get-tuple-element.19), channel_id=1, source_target_pairs={{0,64},{2,66},{64,0},{66,2},{1,65},{3,67},{65,1},{67,3},{4,68},{6,... | collective-permute-start | bytes 774152 | tf_op jit(solution)/shard_map/ppermute | solution.py:340
  89.6 3.0 %collective-permute-start.9 = (bf16[1008,128]{1,0:T(8,128)(2,1)S(1)}, bf16[1008,128]{1,0:T(8,128)(2,1)S(1)}, u32[]{:S(2)}, u32[]{:S(2)}) collective-permute-start(bf16[1008,128]{1,0:T(8,128)(2,1)S(1)} %get-tuple-element.20), channel_id=1, source_target_pairs={{0,66},{2,0},{64,2},{66,64},{1,67},{3,1},{65,3},{67,65},{4,70},{6,... | collective-permute-start | bytes 774152 | tf_op jit(solution)/shard_map/ppermute | solution.py:340
  92.6 2.3 %collective-permute-start.10 = (bf16[1008,128]{1,0:T(8,128)(2,1)S(1)}, bf16[1008,128]{1,0:T(8,128)(2,1)S(1)}, u32[]{:S(2)}, u32[]{:S(2)}) collective-permute-start(bf16[1008,128]{1,0:T(8,128)(2,1)S(1)} %get-tuple-element.21), channel_id=1, source_target_pairs={{0,2},{2,64},{64,66},{66,0},{1,3},{3,65},{65,67},{67,1},{4,6},{6,6... | collective-permute-start | bytes 774152 | tf_op jit(solution)/shard_map/ppermute | solution.py:340
  94.9 2.5 %collective-permute-done.8.refs_1_ = bf16[1008,128]{1,0:T(8,128)(2,1)S(1)} collective-permute-done((bf16[1008,128]{1,0:T(8,128)(2,1)S(1)}, bf16[1008,128]{1,0:T(8,128)(2,1)S(1)}, u32[]{:S(2)}, u32[]{:S(2)}) %collective-permute-start.8) | collective-permute-done | bytes 258080 | tf_op jit(solution)/shard_map/ppermute | solution.py:340
  97.3 4.1 %collective-permute-done.9.refs_2_ = bf16[1008,128]{1,0:T(8,128)(2,1)S(1)} collective-permute-done((bf16[1008,128]{1,0:T(8,128)(2,1)S(1)}, bf16[1008,128]{1,0:T(8,128)(2,1)S(1)}, u32[]{:S(2)}, u32[]{:S(2)}) %collective-permute-start.9) | collective-permute-done | bytes 258080 | tf_op jit(solution)/shard_map/ppermute | solution.py:340
  101.4 1.5 %collective-permute-done.10.refs_3_ = bf16[1008,128]{1,0:T(8,128)(2,1)S(1)} collective-permute-done((bf16[1008,128]{1,0:T(8,128)(2,1)S(1)}, bf16[1008,128]{1,0:T(8,128)(2,1)S(1)}, u32[]{:S(2)}, u32[]{:S(2)}) %collective-permute-start.10) | collective-permute-done | bytes 258080 | tf_op jit(solution)/shard_map/ppermute | solution.py:340
  102.9 0.8 shard_map.61
  (29 shorter events, 0.5 us)
Async XLA Ops:
  0.6 13.6 %copy-start = (bf16[10368,2]{0,1:T(2,128)(2,1)S(1)}, bf16[10368,2]{0,1:T(2,128)(2,1)}, u32[]{:S(2)}) copy-start(bf16[10368,2]{0,1:T(2,128)(2,1)} %param.5) | copy-start | bytes 124420
  1.5 13.1 %collective-permute-start = (bf16[54,2,128]{2,0,1:T(8,128)(2,1)S(1)}, bf16[54,2,128]{2,0,1:T(8,128)(2,1)S(1)}, u32[]{:S(2)}, u32[]{:S(2)}) collective-permute-start(bf16[54,2,128]{2,0,1:T(8,128)(2,1)S(1)} %bitcast.67), channel_id=1, source_target_pairs={{0,66},{66,0},{2,64},{64,2},{1,67},{67,1},{3,65},{65,3},{4,70},{70... | collective-permute-start | bytes 82952 | tf_op jit(solution)/shard_map/ppermute | solution.py:360
  8.7 6.9 %collective-permute-start.1 = (bf16[432,128]{1,0:T(8,128)(2,1)S(1)}, bf16[432,128]{1,0:T(8,128)(2,1)S(1)}, u32[]{:S(2)}, u32[]{:S(2)}) collective-permute-start(bf16[432,128]{1,0:T(8,128)(2,1)S(1)} %get-tuple-element.24), channel_id=1, source_target_pairs={{4,0},{8,4},{12,8},{16,12},{20,16},{24,20},{28,24},{32,28},{36,32}... | collective-permute-start | bytes 331784 | tf_op jit(solution)/shard_map/ppermute | solution.py:20
  10.0 5.6 %collective-permute-start.2 = (bf16[288,128]{1,0:T(8,128)(2,1)S(1)}, bf16[288,128]{1,0:T(8,128)(2,1)S(1)}, u32[]{:S(2)}, u32[]{:S(2)}) collective-permute-start(bf16[288,128]{1,0:T(8,128)(2,1)S(1)} %bitcast.71), channel_id=1, source_target_pairs={{0,4},{4,8},{8,12},{12,16},{16,20},{20,24},{24,28},{28,32},{32,36}... | collective-permute-start | bytes 221192 | tf_op jit(solution)/shard_map/ppermute | solution.py:20
  16.5 29.3 %all-to-all-start = ((bf16[16,35,2,128]{3,2,1,0:T(2,128)(2,1)}), bf16[16,35,2,128]{3,2,1,0:T(2,128)(2,1)S(1)}, u32[]{:S(2)}, u32[]{:S(2)}) async-start(bf16[16,35,2,128]{3,2,1,0:T(2,128)(2,1)} %broadcast_in_dim.6), calls=%async_computation | async-start | bytes 573440 | tf_op jit(solution)/shard_map/all_to_all | solution.py:29
  32.8 20.0 %collective-permute-start.5 = (bf16[1728,128]{1,0:T(8,128)(2,1)S(1)}, bf16[1728,128]{1,0:T(8,128)(2,1)S(1)}, u32[]{:S(2)}, u32[]{:S(2)}) collective-permute-start(bf16[1728,128]{1,0:T(8,128)(2,1)S(1)} %constant_dynamic-update-slice_fusion), channel_id=1, source_target_pairs={{0,64},{2,66},{64,0},{66,2},{1,65},{3,67},{65,1},{67,3},{4,68},{6,... | collective-permute-start | bytes 1327112 | tf_op jit(solution)/shard_map/ppermute | solution.py:340
  37.6 19.0 %collective-permute-start.4 = (bf16[1728,128]{1,0:T(8,128)(2,1)S(1)}, bf16[1728,128]{1,0:T(8,128)(2,1)S(1)}, u32[]{:S(2)}, u32[]{:S(2)}) collective-permute-start(bf16[1728,128]{1,0:T(8,128)(2,1)S(1)} %constant_dynamic-update-slice_fusion), channel_id=1, source_target_pairs={{0,66},{2,0},{64,2},{66,64},{1,67},{3,1},{65,3},{67,65},{4,70},{6,... | collective-permute-start | bytes 1327112 | tf_op jit(solution)/shard_map/ppermute | solution.py:340
  39.6 17.1 %collective-permute-start.3 = (bf16[1728,128]{1,0:T(8,128)(2,1)S(1)}, bf16[1728,128]{1,0:T(8,128)(2,1)S(1)}, u32[]{:S(2)}, u32[]{:S(2)}) collective-permute-start(bf16[1728,128]{1,0:T(8,128)(2,1)S(1)} %constant_dynamic-update-slice_fusion), channel_id=1, source_target_pairs={{0,2},{2,64},{64,66},{66,0},{1,3},{3,65},{65,67},{67,1},{4,6},{6,6... | collective-permute-start | bytes 1327112 | tf_op jit(solution)/shard_map/ppermute | solution.py:340
  47.2 17.7 %all-to-all-start.1 = ((bf16[4,1120,128]{2,1,0:T(8,128)(2,1)}), bf16[4,1120,128]{2,1,0:T(8,128)(2,1)S(1)}, u32[]{:S(2)}, u32[]{:S(2)}) async-start(bf16[4,1120,128]{2,1,0:T(8,128)(2,1)} %broadcast_in_dim.7), calls=%async_computation.1 | async-start | bytes 2293760 | tf_op jit(solution)/shard_map/all_to_all | solution.py:29
  52.8 3.8 %copy-start.1 = (bf16[1728,128]{1,0:T(8,128)(2,1)}, bf16[1728,128]{1,0:T(8,128)(2,1)S(1)}, u32[]{:S(2)}) copy-start(bf16[1728,128]{1,0:T(8,128)(2,1)S(1)} %collective-permute-done.5) | copy-start | bytes 1327108
  56.7 0.8 copy-start.2
  56.7 0.9 copy-start.3
  59.1 14.7 %collective-permute-start.6 = (bf16[4,1728,128]{2,1,0:T(8,128)(2,1)S(1)}, bf16[4,1728,128]{2,1,0:T(8,128)(2,1)}, u32[]{:S(2)}, u32[]{:S(2)}) collective-permute-start(bf16[4,1728,128]{2,1,0:T(8,128)(2,1)S(1)} %pad_maximum_fusion.own), channel_id=1, source_target_pairs={{0,1},{1,0},{2,3},{3,2},{4,5},{5,4},{6,7},{7,6},{8,9},{9,8},{10,11... | collective-permute-start | bytes 5308424 | tf_op jit(solution)/shard_map/ppermute | solution.py:24
  64.9 12.6 %collective-permute-start.7 = (bf16[4,1120,128]{2,1,0:T(8,128)(2,1)S(1)}, bf16[4,1120,128]{2,1,0:T(8,128)(2,1)S(1)}, u32[]{:S(2)}, u32[]{:S(2)}) collective-permute-start(bf16[4,1120,128]{2,1,0:T(8,128)(2,1)S(1)} %all-to-all-done.1.own), channel_id=1, source_target_pairs={{0,1},{1,0},{2,3},{3,2},{4,5},{5,4},{6,7},{7,6},{8,9},{9,8},{10,11... | collective-permute-start | bytes 3440648 | tf_op jit(solution)/shard_map/ppermute | solution.py:24
  86.1 11.2 %collective-permute-start.8 = (bf16[1008,128]{1,0:T(8,128)(2,1)S(1)}, bf16[1008,128]{1,0:T(8,128)(2,1)S(1)}, u32[]{:S(2)}, u32[]{:S(2)}) collective-permute-start(bf16[1008,128]{1,0:T(8,128)(2,1)S(1)} %get-tuple-element.19), channel_id=1, source_target_pairs={{0,64},{2,66},{64,0},{66,2},{1,65},{3,67},{65,1},{67,3},{4,68},{6,... | collective-permute-start | bytes 774152 | tf_op jit(solution)/shard_map/ppermute | solution.py:340
  89.6 11.9 %collective-permute-start.9 = (bf16[1008,128]{1,0:T(8,128)(2,1)S(1)}, bf16[1008,128]{1,0:T(8,128)(2,1)S(1)}, u32[]{:S(2)}, u32[]{:S(2)}) collective-permute-start(bf16[1008,128]{1,0:T(8,128)(2,1)S(1)} %get-tuple-element.20), channel_id=1, source_target_pairs={{0,66},{2,0},{64,2},{66,64},{1,67},{3,1},{65,3},{67,65},{4,70},{6,... | collective-permute-start | bytes 774152 | tf_op jit(solution)/shard_map/ppermute | solution.py:340
  92.6 10.3 %collective-permute-start.10 = (bf16[1008,128]{1,0:T(8,128)(2,1)S(1)}, bf16[1008,128]{1,0:T(8,128)(2,1)S(1)}, u32[]{:S(2)}, u32[]{:S(2)}) collective-permute-start(bf16[1008,128]{1,0:T(8,128)(2,1)S(1)} %get-tuple-element.21), channel_id=1, source_target_pairs={{0,2},{2,64},{64,66},{66,0},{1,3},{3,65},{65,67},{67,1},{4,6},{6,6... | collective-permute-start | bytes 774152 | tf_op jit(solution)/shard_map/ppermute | solution.py:340

commit v8 on v7

--- a/solution.py
+++ b/solution.py
@@ -129,16 +129,17 @@
                         up_w[at : at + part, lane : lane + LANES] = up_tile(
                             kt, row - out_row + 1, kw, split, splits
                         )
-    step = 3 * unit
-
-    def product(k, _):
-        at = pl.ds(pl.multiple_of(k * step, step), step)
-        ups[at, :] = lax.dot_general(
-            rows[at, :], up_w[...], (((1,), (1,)), ((), ())), preferred_element_type=jnp.float32
-        )
-        return 0
-
-    lax.fori_loop(0, rows.shape[0] // step, product, 0)
+    last = rows.shape[0] - unit
+    pair, single = slice(0, 2 * LANES), slice(2 * LANES, 3 * LANES)
+    for first, count, lanes in ((unit, last, pair), (0, last, single)):
+        for start in range(first, first + count, count // 2):
+            at = slice(start, start + count // 2)
+            ups[at, lanes] = lax.dot_general(
+                rows[at, :],
+                up_w[lanes, :],
+                (((1,), (1,)), ((), ())),
+                preferred_element_type=jnp.float32,
+            )
     inside = mask[...] > 0
     times = 2 * (rows.shape[0] // unit - 1) - 1
     for time in range(times):
@@ -220,14 +221,14 @@
                 mix_w[at : at + channels, kt * LANES : (kt + 1) * LANES] = forward_w[
                     row * channels : (row + 1) * channels, lane : lane + LANES
                 ]
-    step = 3 * unit
-
-    def product(k, _):
-        at = pl.ds(pl.multiple_of(k * step, step), step)
-        partial[at, :] = jnp.dot(rows[at, :], mix_w[...], preferred_element_type=jnp.float32)
-        return 0
-
-    lax.fori_loop(0, rows.shape[0] // step, product, 0)
+    last = rows.shape[0] - unit
+    pair, single = slice(0, 2 * LANES), slice(2 * LANES, 3 * LANES)
+    for first, count, lanes in ((unit, last, pair), (0, last - unit, single)):
+        for start in range(first, first + count, count // 2):
+            at = slice(start, start + count // 2)
+            partial[at, lanes] = jnp.dot(
+                rows[at, :], mix_w[:, lanes], preferred_element_type=jnp.float32
+            )
     times = rows.shape[0] // unit - 2
     for time in range(times):
         at = time * unit
@@ -356,8 +357,7 @@
     ny, nz, nx = lax.axis_size("y"), lax.axis_size("z"), lax.axis_size(RING)
     part = out_channels // nx
 
-    raw_mix = tiles_of(mix_kernel)
-    mix_other = lax.ppermute(raw_mix, RING, [(0, 3), (3, 0), (1, 2), (2, 1)])
+    mix_other = lax.ppermute(mix_kernel, RING, [(0, 3), (3, 0), (1, 2), (2, 1)])
     up_column = lax.dynamic_index_in_dim(up_kernel.T, xl, 0, keepdims=False)
     up_tiles = up_column.reshape(-1, LANES)
     up_count = up_tiles.shape[0]
@@ -366,7 +366,7 @@
     up_pairs = (up_half + 1) // 2
     up_part = jnp.pad(up_part, ((0, 2 * up_pairs - up_half), (0, 0))).reshape(-1, 2, LANES)
 
-    mix_tiles = jnp.where(xh == core, raw_mix, mix_other)
+    mix_tiles = tiles_of(jnp.where(xh == core, mix_kernel, mix_other))
     splits = out_channels // LANES
     pick_shape = (2, out_channels, 2 * part)
     slot = lax.broadcasted_iota(jnp.int32, pick_shape, 0)

time: 104 us -> 102 us (0.981)
  Pallas kernels: 13 us -> 11.6 us
    pallas_call x2, Pallas kernels: 12.3 us -> 10.8 us  [call(): pl.pallas_call(kernel, out_shape=outs, in_specs=[pl.BlockSpec(memory_spac...]
  transfers between devices with their start and end apart: 13 -> 13, of which waited for: 6 -> 6; matrix products, arithmetic and copies ran while one was open for 5% -> 6% of each run, Pallas kernels for 4% -> 4%
where the time goes in v8:
time: 102 us
  starting transfers between devices  66.1 us (65%)
  waiting for transfers between devices  15.3 us (15%)
  Pallas kernels  11.6 us (11%)
  local copies, waits for them, and re-layouts  5.56 us (5%)
  other arithmetic  1.7 us (2%)
  between operations  1.06 us (1%)
    all_to_all x2, starting transfers between devices, spread(): lax.all_to_all(jnp.broadcast_to(array, (count, *array.shape)), axis, 0, 0...  21.9 us
    ppermute x6, starting transfers between devices, ring(): return lax.ppermute(array, RING, [(i, (i + by) % 4) for i in range(4)])  18.8 us
    ppermute x2, starting transfers between devices, swap(): return lax.ppermute(array, 'core', [(0, 1), (1, 0)])  14.6 us
    ppermute x6, waiting for transfers between devices, ring(): return lax.ppermute(array, RING, [(i, (i + by) % 4) for i in range(4)])  11.8 us
    pallas_call x2, Pallas kernels, call(): pl.pallas_call(kernel, out_shape=outs, in_specs=[pl.BlockSpec(memory_spac...  10.8 us
    ppermute x2, starting transfers between devices, shift(): return lax.ppermute(array, axis, pairs)  5.47 us
    ppermute x1, starting transfers between devices, shards(): mix_other = lax.ppermute(mix_kernel, RING, [(0, 3), (3, 0), (1, 2), (2, 1)])  5.35 us
    all_to_all x2, waiting for transfers between devices, spread(): lax.all_to_all(jnp.broadcast_to(array, (count, *array.shape)), axis, 0, 0...  2.84 us
  transfers between devices with their start and end apart: 13, of which 6 were waited for; matrix products, arithmetic and copies ran while one was open for 6% of the time, Pallas kernels for 4%

profile of v8, /device:TPU:1, one launch (start us, length us, event | category | flops | bytes accessed | tf_op | source)
XLA Modules:
  0.0 101.5 jit_solution(12987364608863317511)
XLA Ops:
  0.6 0.0 copy-start
  0.6 0.0 copy-start.4
  0.7 5.3 %collective-permute-start = (bf16[6912,2]{0,1:T(2,128)(2,1)}, bf16[6912,2]{0,1:T(2,128)(2,1)S(1)}, u32[]{:S(2)}, u32[]{:S(2)}) collective-permute-start(bf16[6912,2]{0,1:T(2,128)(2,1)} %param.6), channel_id=1, source_target_pairs={{0,66},{66,0},{2,64},{64,2},{1,67},{67,1},{3,65},{65,3},{4,70},{70... | collective-permute-start | bytes 82952 | tf_op jit(solution)/shard_map/ppermute | solution.py:360
  6.0 0.9 reshape.57
  7.0 0.9 slice_bitcast_fusion.1
  8.0 1.3 %collective-permute-start.1 = (bf16[432,128]{1,0:T(8,128)(2,1)S(1)}, bf16[432,128]{1,0:T(8,128)(2,1)S(1)}, u32[]{:S(2)}, u32[]{:S(2)}) collective-permute-start(bf16[432,128]{1,0:T(8,128)(2,1)S(1)} %get-tuple-element.24), channel_id=1, source_target_pairs={{4,0},{8,4},{12,8},{16,12},{20,16},{24,20},{28,24},{32,28},{36,32}... | collective-permute-start | bytes 331784 | tf_op jit(solution)/shard_map/ppermute | solution.py:20
  9.4 4.2 %collective-permute-start.2 = (bf16[288,128]{1,0:T(8,128)(2,1)S(1)}, bf16[288,128]{1,0:T(8,128)(2,1)S(1)}, u32[]{:S(2)}, u32[]{:S(2)}) collective-permute-start(bf16[288,128]{1,0:T(8,128)(2,1)S(1)} %bitcast.70), channel_id=1, source_target_pairs={{0,4},{4,8},{8,12},{12,16},{16,20},{20,24},{24,28},{28,32},{32,36}... | collective-permute-start | bytes 221192 | tf_op jit(solution)/shard_map/ppermute | solution.py:20
  13.6 0.0 copy-done
  13.6 0.1 dynamic-slice_reduce_fusion
  13.8 0.0 collective-permute-done
  13.8 0.0 copy-done.4
  13.9 0.1 reshape.61
  14.1 0.2 fusion
  14.4 0.6 collective-permute-done.2
  14.9 0.0 collective-permute-done.1
  14.9 0.9 broadcast_in_dim.6
  15.8 16.3 %all-to-all-start = ((bf16[16,35,2,128]{3,2,1,0:T(2,128)(2,1)}), bf16[16,35,2,128]{3,2,1,0:T(2,128)(2,1)S(1)}, u32[]{:S(2)}, u32[]{:S(2)}) async-start(bf16[16,35,2,128]{3,2,1,0:T(2,128)(2,1)} %broadcast_in_dim.6), calls=%async_computation | async-start | bytes 573440 | tf_op jit(solution)/shard_map/all_to_all | solution.py:29
  32.1 4.8 %collective-permute-start.5 = (bf16[1728,128]{1,0:T(8,128)(2,1)S(1)}, bf16[1728,128]{1,0:T(8,128)(2,1)S(1)}, u32[]{:S(2)}, u32[]{:S(2)}) collective-permute-start(bf16[1728,128]{1,0:T(8,128)(2,1)S(1)} %constant_dynamic-update-slice_fusion), channel_id=1, source_target_pairs={{0,64},{2,66},{64,0},{66,2},{1,65},{3,67},{65,1},{67,3},{4,68},{6,... | collective-permute-start | bytes 1327112 | tf_op jit(solution)/shard_map/ppermute | solution.py:341
  37.0 1.9 %collective-permute-start.4 = (bf16[1728,128]{1,0:T(8,128)(2,1)S(1)}, bf16[1728,128]{1,0:T(8,128)(2,1)S(1)}, u32[]{:S(2)}, u32[]{:S(2)}) collective-permute-start(bf16[1728,128]{1,0:T(8,128)(2,1)S(1)} %constant_dynamic-update-slice_fusion), channel_id=1, source_target_pairs={{0,66},{2,0},{64,2},{66,64},{1,67},{3,1},{65,3},{67,65},{4,70},{6,... | collective-permute-start | bytes 1327112 | tf_op jit(solution)/shard_map/ppermute | solution.py:341
  38.9 3.4 %collective-permute-start.3 = (bf16[1728,128]{1,0:T(8,128)(2,1)S(1)}, bf16[1728,128]{1,0:T(8,128)(2,1)S(1)}, u32[]{:S(2)}, u32[]{:S(2)}) collective-permute-start(bf16[1728,128]{1,0:T(8,128)(2,1)S(1)} %constant_dynamic-update-slice_fusion), channel_id=1, source_target_pairs={{0,2},{2,64},{64,66},{66,0},{1,3},{3,65},{65,67},{67,1},{4,6},{6,6... | collective-permute-start | bytes 1327112 | tf_op jit(solution)/shard_map/ppermute | solution.py:341
  42.3 2.8 %all-to-all-done = bf16[16,35,2,128]{3,2,1,0:T(2,128)(2,1)S(1)} async-done(((bf16[16,35,2,128]{3,2,1,0:T(2,128)(2,1)}), bf16[16,35,2,128]{3,2,1,0:T(2,128)(2,1)S(1)}, u32[]{:S(2)}, u32[]{:S(2)}) %all-to-all-start) | async-done | bytes 286752 | tf_op jit(solution)/shard_map/all_to_all | solution.py:29
  45.1 0.1 slice_bitcast_fusion
  45.2 0.1 copy.40
  45.4 1.2 %broadcast_in_dim.7 = bf16[4,1120,128]{2,1,0:T(8,128)(2,1)} broadcast(bf16[1120,128]{1,0:T(8,128)(2,1)S(1)} %pad_maximum_fusion.1), dimensions={1,2} | broadcast | bytes 1433600 | tf_op jit(solution)/shard_map/broadcast_in_dim | solution.py:30
  46.5 5.6 %all-to-all-start.1 = ((bf16[4,1120,128]{2,1,0:T(8,128)(2,1)}), bf16[4,1120,128]{2,1,0:T(8,128)(2,1)S(1)}, u32[]{:S(2)}, u32[]{:S(2)}) async-start(bf16[4,1120,128]{2,1,0:T(8,128)(2,1)} %broadcast_in_dim.7), calls=%async_computation.1 | async-start | bytes 2293760 | tf_op jit(solution)/shard_map/all_to_all | solution.py:29
  52.1 0.0 collective-permute-done.5
  52.1 0.0 copy-start.1
  52.1 3.8 %collective-permute-done.4 = bf16[1728,128]{1,0:T(8,128)(2,1)S(1)} collective-permute-done((bf16[1728,128]{1,0:T(8,128)(2,1)S(1)}, bf16[1728,128]{1,0:T(8,128)(2,1)S(1)}, u32[]{:S(2)}, u32[]{:S(2)}) %collective-permute-start.4) | collective-permute-done | bytes 442400 | tf_op jit(solution)/shard_map/ppermute | solution.py:341
  56.0 0.0 collective-permute-done.3
  56.0 0.0 copy-done.1
  56.0 0.8 copy-done.2
  56.8 0.2 copy-done.3
  56.9 1.5 %pad_maximum_fusion.own = bf16[4,1728,128]{2,1,0:T(8,128)(2,1)S(1)} fusion(bf16[1,1728,128]{2,1,0:T(8,128)(2,1)} %bitcast.61, bf16[1,1728,128]{2,1,0:T(8,128)(2,1)} %bitcast.62, bf16[1,1728,128]{2,1,0:T(8,128)(2,1)} %bitcast.63, bf16[1,1728,128]{2,1,0:T(8,128)(2,1)S(1)} %bitcast.59), kind=kLoop, calls=%fused_computation | loop fusion | flops 2654208 | bytes 3538944 | tf_op jit(solution)/shard_map/stack | solution.py:405
  58.4 5.8 %collective-permute-start.6 = (bf16[4,1728,128]{2,1,0:T(8,128)(2,1)S(1)}, bf16[4,1728,128]{2,1,0:T(8,128)(2,1)}, u32[]{:S(2)}, u32[]{:S(2)}) collective-permute-start(bf16[4,1728,128]{2,1,0:T(8,128)(2,1)S(1)} %pad_maximum_fusion.own), channel_id=1, source_target_pairs={{0,1},{1,0},{2,3},{3,2},{4,5},{5,4},{6,7},{7,6},{8,9},{9,8},{10,11... | collective-permute-start | bytes 5308424 | tf_op jit(solution)/shard_map/ppermute | solution.py:24
  64.2 0.0 all-to-all-done.1.own
  64.2 8.8 %collective-permute-start.7 = (bf16[4,1120,128]{2,1,0:T(8,128)(2,1)S(1)}, bf16[4,1120,128]{2,1,0:T(8,128)(2,1)S(1)}, u32[]{:S(2)}, u32[]{:S(2)}) collective-permute-start(bf16[4,1120,128]{2,1,0:T(8,128)(2,1)S(1)} %all-to-all-done.1.own), channel_id=1, source_target_pairs={{0,1},{1,0},{2,3},{3,2},{4,5},{5,4},{6,7},{7,6},{8,9},{9,8},{10,11... | collective-permute-start | bytes 3440648 | tf_op jit(solution)/shard_map/ppermute | solution.py:24
  73.1 0.1 pad_add_fusion.place
  73.1 0.0 collective-permute-done.6.other
  73.1 3.6 %shard_map.59 = (bf16[768,2304]{1,0:T(8,128)(2,1)S(1)}, bf16[1152,1536]{1,0:T(8,128)(2,1)S(1)}) custom-call(s32[3]{0:T(128)S(1)} %pad_add_fusion.place, bf16[4,1728,128]{2,1,0:T(8,128)(2,1)S(1)} %pad_maximum_fusion.own, bf16[4,1728,128]{2,1,0:T(8,128)(2,1)} %collective-permute-done.6.other), custom_call_target="tpu_custom_call" | custom-call | flops 1000000000 | bytes 8388608 | tf_op jit(solution)/shard_map/pallas_call | solution.py:279
  76.8 0.0 collective-permute-done.7.other
  76.8 7.1 %shard_map.60 = (bf16[1008,128]{1,0:T(8,128)(2,1)S(1)}, bf16[1008,128]{1,0:T(8,128)(2,1)S(1)}, bf16[1008,128]{1,0:T(8,128)(2,1)S(1)}, bf16[1008,128]{1,0:T(8,128)(2,1)S(1)}) custom-call(s32[3]{0:T(128)S(1)} %pad_add_fusion.place, bf16[768,2304]{1,0:T(8,128)(2,1)S(1)} %get-tuple-element.14.frame_rows, bf16[1152,1536]{1,0:T(8,128)(2,1)S(1)} %get-tuple-element.15.cot_rows, ...), custom_call_target="tpu_custom_call" | custom-call | flops 4000000000 | bytes 8388608 | tf_op jit(solution)/shard_map/pallas_call | solution.py:279
  83.9 3.5 %collective-permute-start.8 = (bf16[1008,128]{1,0:T(8,128)(2,1)S(1)}, bf16[1008,128]{1,0:T(8,128)(2,1)S(1)}, u32[]{:S(2)}, u32[]{:S(2)}) collective-permute-start(bf16[1008,128]{1,0:T(8,128)(2,1)S(1)} %get-tuple-element.19), channel_id=1, source_target_pairs={{0,64},{2,66},{64,0},{66,2},{1,65},{3,67},{65,1},{67,3},{4,68},{6,... | collective-permute-start | bytes 774152 | tf_op jit(solution)/shard_map/ppermute | solution.py:341
  87.4 3.0 %collective-permute-start.9 = (bf16[1008,128]{1,0:T(8,128)(2,1)S(1)}, bf16[1008,128]{1,0:T(8,128)(2,1)S(1)}, u32[]{:S(2)}, u32[]{:S(2)}) collective-permute-start(bf16[1008,128]{1,0:T(8,128)(2,1)S(1)} %get-tuple-element.20), channel_id=1, source_target_pairs={{0,66},{2,0},{64,2},{66,64},{1,67},{3,1},{65,3},{67,65},{4,70},{6,... | collective-permute-start | bytes 774152 | tf_op jit(solution)/shard_map/ppermute | solution.py:341
  90.4 2.3 %collective-permute-start.10 = (bf16[1008,128]{1,0:T(8,128)(2,1)S(1)}, bf16[1008,128]{1,0:T(8,128)(2,1)S(1)}, u32[]{:S(2)}, u32[]{:S(2)}) collective-permute-start(bf16[1008,128]{1,0:T(8,128)(2,1)S(1)} %get-tuple-element.21), channel_id=1, source_target_pairs={{0,2},{2,64},{64,66},{66,0},{1,3},{3,65},{65,67},{67,1},{4,6},{6,6... | collective-permute-start | bytes 774152 | tf_op jit(solution)/shard_map/ppermute | solution.py:341
  92.7 2.5 %collective-permute-done.8.refs_1_ = bf16[1008,128]{1,0:T(8,128)(2,1)S(1)} collective-permute-done((bf16[1008,128]{1,0:T(8,128)(2,1)S(1)}, bf16[1008,128]{1,0:T(8,128)(2,1)S(1)}, u32[]{:S(2)}, u32[]{:S(2)}) %collective-permute-start.8) | collective-permute-done | bytes 258080 | tf_op jit(solution)/shard_map/ppermute | solution.py:341
  95.2 4.1 %collective-permute-done.9.refs_2_ = bf16[1008,128]{1,0:T(8,128)(2,1)S(1)} collective-permute-done((bf16[1008,128]{1,0:T(8,128)(2,1)S(1)}, bf16[1008,128]{1,0:T(8,128)(2,1)S(1)}, u32[]{:S(2)}, u32[]{:S(2)}) %collective-permute-start.9) | collective-permute-done | bytes 258080 | tf_op jit(solution)/shard_map/ppermute | solution.py:341
  99.3 1.4 %collective-permute-done.10.refs_3_ = bf16[1008,128]{1,0:T(8,128)(2,1)S(1)} collective-permute-done((bf16[1008,128]{1,0:T(8,128)(2,1)S(1)}, bf16[1008,128]{1,0:T(8,128)(2,1)S(1)}, u32[]{:S(2)}, u32[]{:S(2)}) %collective-permute-start.10) | collective-permute-done | bytes 258080 | tf_op jit(solution)/shard_map/ppermute | solution.py:341
  100.7 0.8 shard_map.61
  (31 shorter events, 0.5 us)
Async XLA Ops:
  0.6 13.0 %copy-start = (bf16[10368,2]{0,1:T(2,128)(2,1)S(1)}, bf16[10368,2]{0,1:T(2,128)(2,1)}, u32[]{:S(2)}) copy-start(bf16[10368,2]{0,1:T(2,128)(2,1)} %param.5) | copy-start | bytes 124420
  0.6 13.2 %copy-start.4 = (bf16[6912,2]{0,1:T(2,128)(2,1)S(1)}, bf16[6912,2]{0,1:T(2,128)(2,1)}, u32[]{:S(2)}) copy-start(bf16[6912,2]{0,1:T(2,128)(2,1)} %param.6) | copy-start | bytes 82948
  0.7 13.2 %collective-permute-start = (bf16[6912,2]{0,1:T(2,128)(2,1)}, bf16[6912,2]{0,1:T(2,128)(2,1)S(1)}, u32[]{:S(2)}, u32[]{:S(2)}) collective-permute-start(bf16[6912,2]{0,1:T(2,128)(2,1)} %param.6), channel_id=1, source_target_pairs={{0,66},{66,0},{2,64},{64,2},{1,67},{67,1},{3,65},{65,3},{4,70},{70... | collective-permute-start | bytes 82952 | tf_op jit(solution)/shard_map/ppermute | solution.py:360
  8.0 6.9 %collective-permute-start.1 = (bf16[432,128]{1,0:T(8,128)(2,1)S(1)}, bf16[432,128]{1,0:T(8,128)(2,1)S(1)}, u32[]{:S(2)}, u32[]{:S(2)}) collective-permute-start(bf16[432,128]{1,0:T(8,128)(2,1)S(1)} %get-tuple-element.24), channel_id=1, source_target_pairs={{4,0},{8,4},{12,8},{16,12},{20,16},{24,20},{28,24},{32,28},{36,32}... | collective-permute-start | bytes 331784 | tf_op jit(solution)/shard_map/ppermute | solution.py:20
  9.4 5.6 %collective-permute-start.2 = (bf16[288,128]{1,0:T(8,128)(2,1)S(1)}, bf16[288,128]{1,0:T(8,128)(2,1)S(1)}, u32[]{:S(2)}, u32[]{:S(2)}) collective-permute-start(bf16[288,128]{1,0:T(8,128)(2,1)S(1)} %bitcast.70), channel_id=1, source_target_pairs={{0,4},{4,8},{8,12},{12,16},{16,20},{20,24},{24,28},{28,32},{32,36}... | collective-permute-start | bytes 221192 | tf_op jit(solution)/shard_map/ppermute | solution.py:20
  15.8 29.3 %all-to-all-start = ((bf16[16,35,2,128]{3,2,1,0:T(2,128)(2,1)}), bf16[16,35,2,128]{3,2,1,0:T(2,128)(2,1)S(1)}, u32[]{:S(2)}, u32[]{:S(2)}) async-start(bf16[16,35,2,128]{3,2,1,0:T(2,128)(2,1)} %broadcast_in_dim.6), calls=%async_computation | async-start | bytes 573440 | tf_op jit(solution)/shard_map/all_to_all | solution.py:29
  32.1 20.0 %collective-permute-start.5 = (bf16[1728,128]{1,0:T(8,128)(2,1)S(1)}, bf16[1728,128]{1,0:T(8,128)(2,1)S(1)}, u32[]{:S(2)}, u32[]{:S(2)}) collective-permute-start(bf16[1728,128]{1,0:T(8,128)(2,1)S(1)} %constant_dynamic-update-slice_fusion), channel_id=1, source_target_pairs={{0,64},{2,66},{64,0},{66,2},{1,65},{3,67},{65,1},{67,3},{4,68},{6,... | collective-permute-start | bytes 1327112 | tf_op jit(solution)/shard_map/ppermute | solution.py:341
  37.0 19.0 %collective-permute-start.4 = (bf16[1728,128]{1,0:T(8,128)(2,1)S(1)}, bf16[1728,128]{1,0:T(8,128)(2,1)S(1)}, u32[]{:S(2)}, u32[]{:S(2)}) collective-permute-start(bf16[1728,128]{1,0:T(8,128)(2,1)S(1)} %constant_dynamic-update-slice_fusion), channel_id=1, source_target_pairs={{0,66},{2,0},{64,2},{66,64},{1,67},{3,1},{65,3},{67,65},{4,70},{6,... | collective-permute-start | bytes 1327112 | tf_op jit(solution)/shard_map/ppermute | solution.py:341
  38.9 17.1 %collective-permute-start.3 = (bf16[1728,128]{1,0:T(8,128)(2,1)S(1)}, bf16[1728,128]{1,0:T(8,128)(2,1)S(1)}, u32[]{:S(2)}, u32[]{:S(2)}) collective-permute-start(bf16[1728,128]{1,0:T(8,128)(2,1)S(1)} %constant_dynamic-update-slice_fusion), channel_id=1, source_target_pairs={{0,2},{2,64},{64,66},{66,0},{1,3},{3,65},{65,67},{67,1},{4,6},{6,6... | collective-permute-start | bytes 1327112 | tf_op jit(solution)/shard_map/ppermute | solution.py:341
  46.5 17.7 %all-to-all-start.1 = ((bf16[4,1120,128]{2,1,0:T(8,128)(2,1)}), bf16[4,1120,128]{2,1,0:T(8,128)(2,1)S(1)}, u32[]{:S(2)}, u32[]{:S(2)}) async-start(bf16[4,1120,128]{2,1,0:T(8,128)(2,1)} %broadcast_in_dim.7), calls=%async_computation.1 | async-start | bytes 2293760 | tf_op jit(solution)/shard_map/all_to_all | solution.py:29
  52.1 3.8 %copy-start.1 = (bf16[1728,128]{1,0:T(8,128)(2,1)}, bf16[1728,128]{1,0:T(8,128)(2,1)S(1)}, u32[]{:S(2)}) copy-start(bf16[1728,128]{1,0:T(8,128)(2,1)S(1)} %collective-permute-done.5) | copy-start | bytes 1327108
  56.0 0.8 copy-start.2
  56.0 0.9 copy-start.3
  58.4 14.7 %collective-permute-start.6 = (bf16[4,1728,128]{2,1,0:T(8,128)(2,1)S(1)}, bf16[4,1728,128]{2,1,0:T(8,128)(2,1)}, u32[]{:S(2)}, u32[]{:S(2)}) collective-permute-start(bf16[4,1728,128]{2,1,0:T(8,128)(2,1)S(1)} %pad_maximum_fusion.own), channel_id=1, source_target_pairs={{0,1},{1,0},{2,3},{3,2},{4,5},{5,4},{6,7},{7,6},{8,9},{9,8},{10,11... | collective-permute-start | bytes 5308424 | tf_op jit(solution)/shard_map/ppermute | solution.py:24
  64.2 12.5 %collective-permute-start.7 = (bf16[4,1120,128]{2,1,0:T(8,128)(2,1)S(1)}, bf16[4,1120,128]{2,1,0:T(8,128)(2,1)S(1)}, u32[]{:S(2)}, u32[]{:S(2)}) collective-permute-start(bf16[4,1120,128]{2,1,0:T(8,128)(2,1)S(1)} %all-to-all-done.1.own), channel_id=1, source_target_pairs={{0,1},{1,0},{2,3},{3,2},{4,5},{5,4},{6,7},{7,6},{8,9},{9,8},{10,11... | collective-permute-start | bytes 3440648 | tf_op jit(solution)/shard_map/ppermute | solution.py:24
  83.9 11.2 %collective-permute-start.8 = (bf16[1008,128]{1,0:T(8,128)(2,1)S(1)}, bf16[1008,128]{1,0:T(8,128)(2,1)S(1)}, u32[]{:S(2)}, u32[]{:S(2)}) collective-permute-start(bf16[1008,128]{1,0:T(8,128)(2,1)S(1)} %get-tuple-element.19), channel_id=1, source_target_pairs={{0,64},{2,66},{64,0},{66,2},{1,65},{3,67},{65,1},{67,3},{4,68},{6,... | collective-permute-start | bytes 774152 | tf_op jit(solution)/shard_map/ppermute | solution.py:341
  87.4 11.9 %collective-permute-start.9 = (bf16[1008,128]{1,0:T(8,128)(2,1)S(1)}, bf16[1008,128]{1,0:T(8,128)(2,1)S(1)}, u32[]{:S(2)}, u32[]{:S(2)}) collective-permute-start(bf16[1008,128]{1,0:T(8,128)(2,1)S(1)} %get-tuple-element.20), channel_id=1, source_target_pairs={{0,66},{2,0},{64,2},{66,64},{1,67},{3,1},{65,3},{67,65},{4,70},{6,... | collective-permute-start | bytes 774152 | tf_op jit(solution)/shard_map/ppermute | solution.py:341
  90.4 10.3 %collective-permute-start.10 = (bf16[1008,128]{1,0:T(8,128)(2,1)S(1)}, bf16[1008,128]{1,0:T(8,128)(2,1)S(1)}, u32[]{:S(2)}, u32[]{:S(2)}) collective-permute-start(bf16[1008,128]{1,0:T(8,128)(2,1)S(1)} %get-tuple-element.21), channel_id=1, source_target_pairs={{0,2},{2,64},{64,66},{66,0},{1,3},{3,65},{65,67},{67,1},{4,6},{6,6... | collective-permute-start | bytes 774152 | tf_op jit(solution)/shard_map/ppermute | solution.py:341

commit v9 on v8

--- a/solution.py
+++ b/solution.py
@@ -391,10 +391,10 @@
     block = jnp.concatenate((flat(cotangent[3:]), flat(cotangent[:3]), flat(frames)), axis=0)
     early = (count - 3) * cot_size
     first = block.shape[0]
-    payload, following, previous = lax.optimization_barrier(
+    following = shift(block[early : count * cot_size + frame_size], PLANES, -1)
+    payload, previous = lax.optimization_barrier(
         (
             jnp.concatenate((up_part, mix_part), axis=0),
-            shift(block[early : count * cot_size + frame_size], PLANES, -1),
             shift(block[first - 2 * frame_size :], PLANES, 1),
         )
     )

time: 102 us -> 110 us (1.078)
  waiting for transfers between devices: 15.3 us -> 30.4 us
  starting transfers between devices: 66.1 us -> 59.2 us
    ppermute x2, waiting for transfers between devices: 0.57 us -> 13.7 us  [shift(): return lax.ppermute(array, axis, pairs)]
    ppermute x2, starting transfers between devices: 14.6 us -> 9.94 us  [swap(): return lax.ppermute(array, 'core', [(0, 1), (1, 0)])]
    ppermute x6, waiting for transfers between devices: 11.8 us -> 15.7 us  [ring(): return lax.ppermute(array, RING, [(i, (i + by) % 4) for i in range(4)])]
    all_to_all x2, waiting for transfers between devices: 2.84 us -> 0.01 us  [spread(): lax.all_to_all(jnp.broadcast_to(array, (count, *array.shape)), axis, 0, 0...]
    all_to_all x2, starting transfers between devices: 21.9 us -> 20.5 us  [spread(): lax.all_to_all(jnp.broadcast_to(array, (count, *array.shape)), axis, 0, 0...]
  transfers between devices with their start and end apart: 13 -> 13, of which waited for: 6 -> 7; matrix products, arithmetic and copies ran while one was open for 6% -> 4% of each run, Pallas kernels for 4% -> 3%
where the time goes in v9:
time: 110 us; the launch traced here: 109 us
  starting transfers between devices  59.2 us (54%)
  waiting for transfers between devices  30.4 us (28%)
  Pallas kernels  11.6 us (11%)
  local copies, waits for them, and re-layouts  4.47 us (4%)
  other arithmetic  1.72 us (2%)
    all_to_all x2, starting transfers between devices, spread(): lax.all_to_all(jnp.broadcast_to(array, (count, *array.shape)), axis, 0, 0...  20.5 us
    ppermute x6, starting transfers between devices, ring(): return lax.ppermute(array, RING, [(i, (i + by) % 4) for i in range(4)])  18.7 us
    ppermute x6, waiting for transfers between devices, ring(): return lax.ppermute(array, RING, [(i, (i + by) % 4) for i in range(4)])  15.7 us
    ppermute x2, waiting for transfers between devices, shift(): return lax.ppermute(array, axis, pairs)  13.7 us
    pallas_call x2, Pallas kernels, call(): pl.pallas_call(kernel, out_shape=outs, in_specs=[pl.BlockSpec(memory_spac...  10.8 us
    ppermute x2, starting transfers between devices, swap(): return lax.ppermute(array, 'core', [(0, 1), (1, 0)])  9.94 us
    ppermute x1, starting transfers between devices, shards(): mix_other = lax.ppermute(mix_kernel, RING, [(0, 3), (3, 0), (1, 2), (2, 1)])  5.22 us
    ppermute x2, starting transfers between devices, shift(): return lax.ppermute(array, axis, pairs)  4.84 us
  transfers between devices with their start and end apart: 13, of which 7 were waited for; matrix products, arithmetic and copies ran while one was open for 4% of the time, Pallas kernels for 3%

profile of v9, /device:TPU:1, one launch (start us, length us, event | category | flops | bytes accessed | tf_op | source)
XLA Modules:
  0.0 108.7 jit_solution(4129530985960153881)
XLA Ops:
  0.6 0.0 copy-start
  0.6 5.2 %collective-permute-start.1 = (bf16[6912,2]{0,1:T(2,128)(2,1)}, bf16[6912,2]{0,1:T(2,128)(2,1)S(1)}, u32[]{:S(2)}, u32[]{:S(2)}) collective-permute-start(bf16[6912,2]{0,1:T(2,128)(2,1)} %param.6), channel_id=1, source_target_pairs={{0,66},{66,0},{2,64},{64,2},{1,67},{67,1},{3,65},{65,3},{4,70},{70... | collective-permute-start | bytes 82952 | tf_op jit(solution)/shard_map/ppermute | solution.py:360
  5.9 0.9 reshape.57
  6.9 3.5 %collective-permute-start.2 = (bf16[288,128]{1,0:T(8,128)(2,1)S(1)}, bf16[288,128]{1,0:T(8,128)(2,1)S(1)}, u32[]{:S(2)}, u32[]{:S(2)}) collective-permute-start(bf16[288,128]{1,0:T(8,128)(2,1)S(1)} %bitcast.70), channel_id=1, source_target_pairs={{0,4},{4,8},{8,12},{12,16},{16,20},{20,24},{24,28},{28,32},{32,36}... | collective-permute-start | bytes 221192 | tf_op jit(solution)/shard_map/ppermute | solution.py:20
  10.5 0.0 copy-done
  10.5 0.1 dynamic-slice_reduce_fusion
  10.7 0.0 collective-permute-done.1
  10.8 0.1 reshape.61
  10.9 0.0 copy-start.4
  11.0 0.2 fusion
  11.3 0.5 collective-permute-done.2
  11.8 0.9 broadcast_in_dim.6
  12.7 16.3 %all-to-all-start = ((bf16[16,35,2,128]{3,2,1,0:T(2,128)(2,1)}), bf16[16,35,2,128]{3,2,1,0:T(2,128)(2,1)S(1)}, u32[]{:S(2)}, u32[]{:S(2)}) async-start(bf16[16,35,2,128]{3,2,1,0:T(2,128)(2,1)} %broadcast_in_dim.6), calls=%async_computation | async-start | bytes 573440 | tf_op jit(solution)/shard_map/all_to_all | solution.py:29
  29.0 0.0 copy-done.4
  29.1 1.3 %collective-permute-start = (bf16[432,128]{1,0:T(8,128)(2,1)S(1)}, bf16[432,128]{1,0:T(8,128)(2,1)S(1)}, u32[]{:S(2)}, u32[]{:S(2)}) collective-permute-start(bf16[432,128]{1,0:T(8,128)(2,1)S(1)} %get-tuple-element.22), channel_id=1, source_target_pairs={{4,0},{8,4},{12,8},{16,12},{20,16},{24,20},{28,24},{32,28},{36,32}... | collective-permute-start | bytes 331784 | tf_op jit(solution)/shard_map/ppermute | solution.py:20
  30.4 13.2 %collective-permute-done = bf16[432,128]{1,0:T(8,128)(2,1)S(1)} collective-permute-done((bf16[432,128]{1,0:T(8,128)(2,1)S(1)}, bf16[432,128]{1,0:T(8,128)(2,1)S(1)}, u32[]{:S(2)}, u32[]{:S(2)}) %collective-permute-start) | collective-permute-done | bytes 110624 | tf_op jit(solution)/shard_map/ppermute | solution.py:20
  43.6 1.9 %collective-permute-start.3 = (bf16[1728,128]{1,0:T(8,128)(2,1)S(1)}, bf16[1728,128]{1,0:T(8,128)(2,1)S(1)}, u32[]{:S(2)}, u32[]{:S(2)}) collective-permute-start(bf16[1728,128]{1,0:T(8,128)(2,1)S(1)} %constant_dynamic-update-slice_fusion), channel_id=1, source_target_pairs={{0,2},{2,64},{64,66},{66,0},{1,3},{3,65},{65,67},{67,1},{4,6},{6,6... | collective-permute-start | bytes 1327112 | tf_op jit(solution)/shard_map/ppermute | solution.py:341
  45.6 4.6 %collective-permute-start.4 = (bf16[1728,128]{1,0:T(8,128)(2,1)S(1)}, bf16[1728,128]{1,0:T(8,128)(2,1)S(1)}, u32[]{:S(2)}, u32[]{:S(2)}) collective-permute-start(bf16[1728,128]{1,0:T(8,128)(2,1)S(1)} %constant_dynamic-update-slice_fusion), channel_id=1, source_target_pairs={{0,66},{2,0},{64,2},{66,64},{1,67},{3,1},{65,3},{67,65},{4,70},{6,... | collective-permute-start | bytes 1327112 | tf_op jit(solution)/shard_map/ppermute | solution.py:341
  50.1 1.9 %collective-permute-start.5 = (bf16[1728,128]{1,0:T(8,128)(2,1)S(1)}, bf16[1728,128]{1,0:T(8,128)(2,1)S(1)}, u32[]{:S(2)}, u32[]{:S(2)}) collective-permute-start(bf16[1728,128]{1,0:T(8,128)(2,1)S(1)} %constant_dynamic-update-slice_fusion), channel_id=1, source_target_pairs={{0,64},{2,66},{64,0},{66,2},{1,65},{3,67},{65,1},{67,3},{4,68},{6,... | collective-permute-start | bytes 1327112 | tf_op jit(solution)/shard_map/ppermute | solution.py:341
  52.1 0.0 all-to-all-done
  52.1 0.1 slice_bitcast_fusion
  52.2 0.1 copy.40
  52.4 1.2 %broadcast_in_dim.7 = bf16[4,1120,128]{2,1,0:T(8,128)(2,1)} broadcast(bf16[1120,128]{1,0:T(8,128)(2,1)S(1)} %pad_maximum_fusion.1), dimensions={1,2} | broadcast | bytes 1433600 | tf_op jit(solution)/shard_map/broadcast_in_dim | solution.py:30
  53.5 4.2 %all-to-all-start.1 = ((bf16[4,1120,128]{2,1,0:T(8,128)(2,1)}), bf16[4,1120,128]{2,1,0:T(8,128)(2,1)S(1)}, u32[]{:S(2)}, u32[]{:S(2)}) async-start(bf16[4,1120,128]{2,1,0:T(8,128)(2,1)} %broadcast_in_dim.7), calls=%async_computation.1 | async-start | bytes 2293760 | tf_op jit(solution)/shard_map/all_to_all | solution.py:29
  57.7 0.0 collective-permute-done.3
  57.7 0.0 copy-start.1
  57.7 0.0 collective-permute-done.4
  57.7 0.0 copy-start.2
  57.7 6.8 %collective-permute-done.5 = bf16[1728,128]{1,0:T(8,128)(2,1)S(1)} collective-permute-done((bf16[1728,128]{1,0:T(8,128)(2,1)S(1)}, bf16[1728,128]{1,0:T(8,128)(2,1)S(1)}, u32[]{:S(2)}, u32[]{:S(2)}) %collective-permute-start.5) | collective-permute-done | bytes 442400 | tf_op jit(solution)/shard_map/ppermute | solution.py:341
  64.5 0.0 copy-done.1
  64.5 0.0 copy-done.2
  64.5 0.8 copy-done.3
  65.3 1.5 %pad_maximum_fusion.own = bf16[4,1728,128]{2,1,0:T(8,128)(2,1)S(1)} fusion(bf16[1,1728,128]{2,1,0:T(8,128)(2,1)} %bitcast.63, bf16[1,1728,128]{2,1,0:T(8,128)(2,1)} %bitcast.62, bf16[1,1728,128]{2,1,0:T(8,128)(2,1)} %bitcast.61, bf16[1,1728,128]{2,1,0:T(8,128)(2,1)S(1)} %bitcast.59), kind=kLoop, calls=%fused_computation | loop fusion | flops 2654208 | bytes 3538944 | tf_op jit(solution)/shard_map/stack | solution.py:405
  66.8 7.5 %collective-permute-start.6 = (bf16[4,1728,128]{2,1,0:T(8,128)(2,1)S(1)}, bf16[4,1728,128]{2,1,0:T(8,128)(2,1)}, u32[]{:S(2)}, u32[]{:S(2)}) collective-permute-start(bf16[4,1728,128]{2,1,0:T(8,128)(2,1)S(1)} %pad_maximum_fusion.own), channel_id=1, source_target_pairs={{0,1},{1,0},{2,3},{3,2},{4,5},{5,4},{6,7},{7,6},{8,9},{9,8},{10,11... | collective-permute-start | bytes 5308424 | tf_op jit(solution)/shard_map/ppermute | solution.py:24
  74.3 0.0 all-to-all-done.1.own
  74.3 2.4 %collective-permute-start.7 = (bf16[4,1120,128]{2,1,0:T(8,128)(2,1)S(1)}, bf16[4,1120,128]{2,1,0:T(8,128)(2,1)S(1)}, u32[]{:S(2)}, u32[]{:S(2)}) collective-permute-start(bf16[4,1120,128]{2,1,0:T(8,128)(2,1)S(1)} %all-to-all-done.1.own), channel_id=1, source_target_pairs={{0,1},{1,0},{2,3},{3,2},{4,5},{5,4},{6,7},{7,6},{8,9},{9,8},{10,11... | collective-permute-start | bytes 3440648 | tf_op jit(solution)/shard_map/ppermute | solution.py:24
  76.7 0.1 pad_add_fusion.place
  76.8 0.9 collective-permute-done.6.other
  77.7 3.6 %shard_map.59 = (bf16[768,2304]{1,0:T(8,128)(2,1)S(1)}, bf16[1152,1536]{1,0:T(8,128)(2,1)S(1)}) custom-call(s32[3]{0:T(128)S(1)} %pad_add_fusion.place, bf16[4,1728,128]{2,1,0:T(8,128)(2,1)S(1)} %pad_maximum_fusion.own, bf16[4,1728,128]{2,1,0:T(8,128)(2,1)} %collective-permute-done.6.other), custom_call_target="tpu_custom_call" | custom-call | flops 1000000000 | bytes 8388608 | tf_op jit(solution)/shard_map/pallas_call | solution.py:279
  81.4 0.0 collective-permute-done.7.other
  81.4 7.2 %shard_map.60 = (bf16[1008,128]{1,0:T(8,128)(2,1)S(1)}, bf16[1008,128]{1,0:T(8,128)(2,1)S(1)}, bf16[1008,128]{1,0:T(8,128)(2,1)S(1)}, bf16[1008,128]{1,0:T(8,128)(2,1)S(1)}) custom-call(s32[3]{0:T(128)S(1)} %pad_add_fusion.place, bf16[768,2304]{1,0:T(8,128)(2,1)S(1)} %get-tuple-element.12.frame_rows, bf16[1152,1536]{1,0:T(8,128)(2,1)S(1)} %get-tuple-element.13.cot_rows, ...), custom_call_target="tpu_custom_call" | custom-call | flops 4000000000 | bytes 8388608 | tf_op jit(solution)/shard_map/pallas_call | solution.py:279
  88.6 3.1 %collective-permute-start.10 = (bf16[1008,128]{1,0:T(8,128)(2,1)S(1)}, bf16[1008,128]{1,0:T(8,128)(2,1)S(1)}, u32[]{:S(2)}, u32[]{:S(2)}) collective-permute-start(bf16[1008,128]{1,0:T(8,128)(2,1)S(1)} %get-tuple-element.19), channel_id=1, source_target_pairs={{0,2},{2,64},{64,66},{66,0},{1,3},{3,65},{65,67},{67,1},{4,6},{6,6... | collective-permute-start | bytes 774152 | tf_op jit(solution)/shard_map/ppermute | solution.py:341
  91.7 5.3 %collective-permute-start.8 = (bf16[1008,128]{1,0:T(8,128)(2,1)S(1)}, bf16[1008,128]{1,0:T(8,128)(2,1)S(1)}, u32[]{:S(2)}, u32[]{:S(2)}) collective-permute-start(bf16[1008,128]{1,0:T(8,128)(2,1)S(1)} %get-tuple-element.17), channel_id=1, source_target_pairs={{0,64},{2,66},{64,0},{66,2},{1,65},{3,67},{65,1},{67,3},{4,68},{6,... | collective-permute-start | bytes 774152 | tf_op jit(solution)/shard_map/ppermute | solution.py:341
  97.0 1.9 %collective-permute-start.9 = (bf16[1008,128]{1,0:T(8,128)(2,1)S(1)}, bf16[1008,128]{1,0:T(8,128)(2,1)S(1)}, u32[]{:S(2)}, u32[]{:S(2)}) collective-permute-start(bf16[1008,128]{1,0:T(8,128)(2,1)S(1)} %get-tuple-element.18), channel_id=1, source_target_pairs={{0,66},{2,0},{64,2},{66,64},{1,67},{3,1},{65,3},{67,65},{4,70},{6,... | collective-permute-start | bytes 774152 | tf_op jit(solution)/shard_map/ppermute | solution.py:341
  99.0 1.2 %collective-permute-done.10.refs_3_ = bf16[1008,128]{1,0:T(8,128)(2,1)S(1)} collective-permute-done((bf16[1008,128]{1,0:T(8,128)(2,1)S(1)}, bf16[1008,128]{1,0:T(8,128)(2,1)S(1)}, u32[]{:S(2)}, u32[]{:S(2)}) %collective-permute-start.10) | collective-permute-done | bytes 258080 | tf_op jit(solution)/shard_map/ppermute | solution.py:341
  100.2 6.4 %collective-permute-done.8.refs_1_ = bf16[1008,128]{1,0:T(8,128)(2,1)S(1)} collective-permute-done((bf16[1008,128]{1,0:T(8,128)(2,1)S(1)}, bf16[1008,128]{1,0:T(8,128)(2,1)S(1)}, u32[]{:S(2)}, u32[]{:S(2)}) %collective-permute-start.8) | collective-permute-done | bytes 258080 | tf_op jit(solution)/shard_map/ppermute | solution.py:341
  106.6 1.4 %collective-permute-done.9.refs_2_ = bf16[1008,128]{1,0:T(8,128)(2,1)S(1)} collective-permute-done((bf16[1008,128]{1,0:T(8,128)(2,1)S(1)}, bf16[1008,128]{1,0:T(8,128)(2,1)S(1)}, u32[]{:S(2)}, u32[]{:S(2)}) %collective-permute-start.9) | collective-permute-done | bytes 258080 | tf_op jit(solution)/shard_map/ppermute | solution.py:341
  108.0 0.8 shard_map.61
  (31 shorter events, 0.5 us)
Async XLA Ops:
  0.6 9.8 %copy-start = (bf16[10368,2]{0,1:T(2,128)(2,1)S(1)}, bf16[10368,2]{0,1:T(2,128)(2,1)}, u32[]{:S(2)}) copy-start(bf16[10368,2]{0,1:T(2,128)(2,1)} %param.5) | copy-start | bytes 124420
  0.6 10.1 %collective-permute-start.1 = (bf16[6912,2]{0,1:T(2,128)(2,1)}, bf16[6912,2]{0,1:T(2,128)(2,1)S(1)}, u32[]{:S(2)}, u32[]{:S(2)}) collective-permute-start(bf16[6912,2]{0,1:T(2,128)(2,1)} %param.6), channel_id=1, source_target_pairs={{0,66},{66,0},{2,64},{64,2},{1,67},{67,1},{3,65},{65,3},{4,70},{70... | collective-permute-start | bytes 82952 | tf_op jit(solution)/shard_map/ppermute | solution.py:360
  6.9 4.9 %collective-permute-start.2 = (bf16[288,128]{1,0:T(8,128)(2,1)S(1)}, bf16[288,128]{1,0:T(8,128)(2,1)S(1)}, u32[]{:S(2)}, u32[]{:S(2)}) collective-permute-start(bf16[288,128]{1,0:T(8,128)(2,1)S(1)} %bitcast.70), channel_id=1, source_target_pairs={{0,4},{4,8},{8,12},{12,16},{16,20},{20,24},{24,28},{28,32},{32,36}... | collective-permute-start | bytes 221192 | tf_op jit(solution)/shard_map/ppermute | solution.py:20
  10.9 18.1 %copy-start.4 = (bf16[6,2,24,256]{3,2,1,0:T(8,128)(2,1)S(1)}, bf16[6,2,24,256]{3,2,1,0:T(8,128)(2,1)}, u32[]{:S(2)}) copy-start(bf16[6,2,24,256]{3,2,1,0:T(8,128)(2,1)} %param.7) | copy-start | bytes 442372
  12.7 39.4 %all-to-all-start = ((bf16[16,35,2,128]{3,2,1,0:T(2,128)(2,1)}), bf16[16,35,2,128]{3,2,1,0:T(2,128)(2,1)S(1)}, u32[]{:S(2)}, u32[]{:S(2)}) async-start(bf16[16,35,2,128]{3,2,1,0:T(2,128)(2,1)} %broadcast_in_dim.6), calls=%async_computation | async-start | bytes 573440 | tf_op jit(solution)/shard_map/all_to_all | solution.py:29
  29.1 14.5 %collective-permute-start = (bf16[432,128]{1,0:T(8,128)(2,1)S(1)}, bf16[432,128]{1,0:T(8,128)(2,1)S(1)}, u32[]{:S(2)}, u32[]{:S(2)}) collective-permute-start(bf16[432,128]{1,0:T(8,128)(2,1)S(1)} %get-tuple-element.22), channel_id=1, source_target_pairs={{4,0},{8,4},{12,8},{16,12},{20,16},{24,20},{28,24},{32,28},{36,32}... | collective-permute-start | bytes 331784 | tf_op jit(solution)/shard_map/ppermute | solution.py:20
  43.6 14.1 %collective-permute-start.3 = (bf16[1728,128]{1,0:T(8,128)(2,1)S(1)}, bf16[1728,128]{1,0:T(8,128)(2,1)S(1)}, u32[]{:S(2)}, u32[]{:S(2)}) collective-permute-start(bf16[1728,128]{1,0:T(8,128)(2,1)S(1)} %constant_dynamic-update-slice_fusion), channel_id=1, source_target_pairs={{0,2},{2,64},{64,66},{66,0},{1,3},{3,65},{65,67},{67,1},{4,6},{6,6... | collective-permute-start | bytes 1327112 | tf_op jit(solution)/shard_map/ppermute | solution.py:341
  45.6 12.2 %collective-permute-start.4 = (bf16[1728,128]{1,0:T(8,128)(2,1)S(1)}, bf16[1728,128]{1,0:T(8,128)(2,1)S(1)}, u32[]{:S(2)}, u32[]{:S(2)}) collective-permute-start(bf16[1728,128]{1,0:T(8,128)(2,1)S(1)} %constant_dynamic-update-slice_fusion), channel_id=1, source_target_pairs={{0,66},{2,0},{64,2},{66,64},{1,67},{3,1},{65,3},{67,65},{4,70},{6,... | collective-permute-start | bytes 1327112 | tf_op jit(solution)/shard_map/ppermute | solution.py:341
  50.1 14.4 %collective-permute-start.5 = (bf16[1728,128]{1,0:T(8,128)(2,1)S(1)}, bf16[1728,128]{1,0:T(8,128)(2,1)S(1)}, u32[]{:S(2)}, u32[]{:S(2)}) collective-permute-start(bf16[1728,128]{1,0:T(8,128)(2,1)S(1)} %constant_dynamic-update-slice_fusion), channel_id=1, source_target_pairs={{0,64},{2,66},{64,0},{66,2},{1,65},{3,67},{65,1},{67,3},{4,68},{6,... | collective-permute-start | bytes 1327112 | tf_op jit(solution)/shard_map/ppermute | solution.py:341
  53.5 20.8 %all-to-all-start.1 = ((bf16[4,1120,128]{2,1,0:T(8,128)(2,1)}), bf16[4,1120,128]{2,1,0:T(8,128)(2,1)S(1)}, u32[]{:S(2)}, u32[]{:S(2)}) async-start(bf16[4,1120,128]{2,1,0:T(8,128)(2,1)} %broadcast_in_dim.7), calls=%async_computation.1 | async-start | bytes 2293760 | tf_op jit(solution)/shard_map/all_to_all | solution.py:29
  57.7 6.8 %copy-start.1 = (bf16[1728,128]{1,0:T(8,128)(2,1)}, bf16[1728,128]{1,0:T(8,128)(2,1)S(1)}, u32[]{:S(2)}) copy-start(bf16[1728,128]{1,0:T(8,128)(2,1)S(1)} %collective-permute-done.3) | copy-start | bytes 1327108
  57.7 6.8 %copy-start.2 = (bf16[1728,128]{1,0:T(8,128)(2,1)}, bf16[1728,128]{1,0:T(8,128)(2,1)S(1)}, u32[]{:S(2)}) copy-start(bf16[1728,128]{1,0:T(8,128)(2,1)S(1)} %collective-permute-done.4) | copy-start | bytes 1327108
  64.5 0.8 copy-start.3
  66.8 11.0 %collective-permute-start.6 = (bf16[4,1728,128]{2,1,0:T(8,128)(2,1)S(1)}, bf16[4,1728,128]{2,1,0:T(8,128)(2,1)}, u32[]{:S(2)}, u32[]{:S(2)}) collective-permute-start(bf16[4,1728,128]{2,1,0:T(8,128)(2,1)S(1)} %pad_maximum_fusion.own), channel_id=1, source_target_pairs={{0,1},{1,0},{2,3},{3,2},{4,5},{5,4},{6,7},{7,6},{8,9},{9,8},{10,11... | collective-permute-start | bytes 5308424 | tf_op jit(solution)/shard_map/ppermute | solution.py:24
  74.3 7.1 %collective-permute-start.7 = (bf16[4,1120,128]{2,1,0:T(8,128)(2,1)S(1)}, bf16[4,1120,128]{2,1,0:T(8,128)(2,1)S(1)}, u32[]{:S(2)}, u32[]{:S(2)}) collective-permute-start(bf16[4,1120,128]{2,1,0:T(8,128)(2,1)S(1)} %all-to-all-done.1.own), channel_id=1, source_target_pairs={{0,1},{1,0},{2,3},{3,2},{4,5},{5,4},{6,7},{7,6},{8,9},{9,8},{10,11... | collective-permute-start | bytes 3440648 | tf_op jit(solution)/shard_map/ppermute | solution.py:24
  88.6 11.6 %collective-permute-start.10 = (bf16[1008,128]{1,0:T(8,128)(2,1)S(1)}, bf16[1008,128]{1,0:T(8,128)(2,1)S(1)}, u32[]{:S(2)}, u32[]{:S(2)}) collective-permute-start(bf16[1008,128]{1,0:T(8,128)(2,1)S(1)} %get-tuple-element.19), channel_id=1, source_target_pairs={{0,2},{2,64},{64,66},{66,0},{1,3},{3,65},{65,67},{67,1},{4,6},{6,6... | collective-permute-start | bytes 774152 | tf_op jit(solution)/shard_map/ppermute | solution.py:341
  91.7 14.9 %collective-permute-start.8 = (bf16[1008,128]{1,0:T(8,128)(2,1)S(1)}, bf16[1008,128]{1,0:T(8,128)(2,1)S(1)}, u32[]{:S(2)}, u32[]{:S(2)}) collective-permute-start(bf16[1008,128]{1,0:T(8,128)(2,1)S(1)} %get-tuple-element.17), channel_id=1, source_target_pairs={{0,64},{2,66},{64,0},{66,2},{1,65},{3,67},{65,1},{67,3},{4,68},{6,... | collective-permute-start | bytes 774152 | tf_op jit(solution)/shard_map/ppermute | solution.py:341
  97.0 10.9 %collective-permute-start.9 = (bf16[1008,128]{1,0:T(8,128)(2,1)S(1)}, bf16[1008,128]{1,0:T(8,128)(2,1)S(1)}, u32[]{:S(2)}, u32[]{:S(2)}) collective-permute-start(bf16[1008,128]{1,0:T(8,128)(2,1)S(1)} %get-tuple-element.18), channel_id=1, source_target_pairs={{0,66},{2,0},{64,2},{66,64},{1,67},{3,1},{65,3},{67,65},{4,70},{6,... | collective-permute-start | bytes 774152 | tf_op jit(solution)/shard_map/ppermute | solution.py:341

commit v10 on v9

--- a/solution.py
+++ b/solution.py
@@ -391,12 +391,10 @@
     block = jnp.concatenate((flat(cotangent[3:]), flat(cotangent[:3]), flat(frames)), axis=0)
     early = (count - 3) * cot_size
     first = block.shape[0]
+    previous = shift(block[first - 2 * frame_size :], PLANES, 1)
     following = shift(block[early : count * cot_size + frame_size], PLANES, -1)
-    payload, previous = lax.optimization_barrier(
-        (
-            jnp.concatenate((up_part, mix_part), axis=0),
-            shift(block[first - 2 * frame_size :], PLANES, 1),
-        )
+    payload, previous, following = lax.optimization_barrier(
+        (jnp.concatenate((up_part, mix_part), axis=0), previous, following)
     )
     planes = spread(payload, "z")
     block = jnp.concatenate((block, following, previous), axis=0)

time: 110 us -> 103 us (0.936); the launches traced: 109 us -> 101 us
  waiting for transfers between devices: 30.4 us -> 21.6 us
    ppermute x2, waiting for transfers between devices: 13.7 us -> 3.55 us  [shift(): return lax.ppermute(array, axis, pairs)]
    all_to_all x2, waiting for transfers between devices: 0.01 us -> 4.86 us  [spread(): lax.all_to_all(jnp.broadcast_to(array, (count, *array.shape)), axis, 0, 0...]
    ppermute x2, starting transfers between devices: 9.94 us -> 14 us  [swap(): return lax.ppermute(array, 'core', [(0, 1), (1, 0)])]
    ppermute x6, waiting for transfers between devices: 15.7 us -> 13.1 us  [ring(): return lax.ppermute(array, RING, [(i, (i + by) % 4) for i in range(4)])]
    ppermute x6, starting transfers between devices: 18.7 us -> 16.1 us  [ring(): return lax.ppermute(array, RING, [(i, (i + by) % 4) for i in range(4)])]
    all_to_all x2, starting transfers between devices: 20.5 us -> 18.8 us  [spread(): lax.all_to_all(jnp.broadcast_to(array, (count, *array.shape)), axis, 0, 0...]
  transfers between devices with their start and end apart: 13 -> 13, of which waited for: 7 -> 7; matrix products, arithmetic and copies ran while one was open for 4% -> 6% of each run, Pallas kernels for 3% -> 4%
where the time goes in v10:
time: 103 us; the launch traced here: 101 us
  starting transfers between devices  59.1 us (57%)
  waiting for transfers between devices  21.6 us (21%)
  Pallas kernels  11.6 us (11%)
  local copies, waits for them, and re-layouts  5.42 us (5%)
  other arithmetic  1.7 us (2%)
  between operations  1.06 us (1%)
    all_to_all x2, starting transfers between devices, spread(): lax.all_to_all(jnp.broadcast_to(array, (count, *array.shape)), axis, 0, 0...  18.8 us
    ppermute x6, starting transfers between devices, ring(): return lax.ppermute(array, RING, [(i, (i + by) % 4) for i in range(4)])  16.1 us
    ppermute x2, starting transfers between devices, swap(): return lax.ppermute(array, 'core', [(0, 1), (1, 0)])  14 us
    ppermute x6, waiting for transfers between devices, ring(): return lax.ppermute(array, RING, [(i, (i + by) % 4) for i in range(4)])  13.1 us
    pallas_call x2, Pallas kernels, call(): pl.pallas_call(kernel, out_shape=outs, in_specs=[pl.BlockSpec(memory_spac...  10.8 us
    ppermute x1, starting transfers between devices, shards(): mix_other = lax.ppermute(mix_kernel, RING, [(0, 3), (3, 0), (1, 2), (2, 1)])  5.35 us
    all_to_all x2, waiting for transfers between devices, spread(): lax.all_to_all(jnp.broadcast_to(array, (count, *array.shape)), axis, 0, 0...  4.86 us
    ppermute x2, starting transfers between devices, shift(): return lax.ppermute(array, axis, pairs)  4.84 us
  transfers between devices with their start and end apart: 13, of which 7 were waited for; matrix products, arithmetic and copies ran while one was open for 6% of the time, Pallas kernels for 4%

profile of v10, /device:TPU:1, one launch (start us, length us, event | category | flops | bytes accessed | tf_op | source)
XLA Modules:
  0.0 100.6 jit_solution(3209096728829181516)
XLA Ops:
  0.6 0.0 copy-start
  0.6 0.0 copy-start.4
  0.7 5.3 %collective-permute-start = (bf16[6912,2]{0,1:T(2,128)(2,1)}, bf16[6912,2]{0,1:T(2,128)(2,1)S(1)}, u32[]{:S(2)}, u32[]{:S(2)}) collective-permute-start(bf16[6912,2]{0,1:T(2,128)(2,1)} %param.6), channel_id=1, source_target_pairs={{0,66},{66,0},{2,64},{64,2},{1,67},{67,1},{3,65},{65,3},{4,70},{70... | collective-permute-start | bytes 82952 | tf_op jit(solution)/shard_map/ppermute | solution.py:360
  6.0 0.9 reshape.57
  7.0 3.5 %collective-permute-start.1 = (bf16[288,128]{1,0:T(8,128)(2,1)S(1)}, bf16[288,128]{1,0:T(8,128)(2,1)S(1)}, u32[]{:S(2)}, u32[]{:S(2)}) collective-permute-start(bf16[288,128]{1,0:T(8,128)(2,1)S(1)} %bitcast.70), channel_id=1, source_target_pairs={{0,4},{4,8},{8,12},{12,16},{16,20},{20,24},{24,28},{28,32},{32,36}... | collective-permute-start | bytes 221192 | tf_op jit(solution)/shard_map/ppermute | solution.py:20
  10.6 0.9 slice_bitcast_fusion.1
  11.6 1.3 %collective-permute-start.2 = (bf16[432,128]{1,0:T(8,128)(2,1)S(1)}, bf16[432,128]{1,0:T(8,128)(2,1)S(1)}, u32[]{:S(2)}, u32[]{:S(2)}) collective-permute-start(bf16[432,128]{1,0:T(8,128)(2,1)S(1)} %get-tuple-element.24), channel_id=1, source_target_pairs={{4,0},{8,4},{12,8},{16,12},{20,16},{24,20},{28,24},{32,28},{36,32}... | collective-permute-start | bytes 331784 | tf_op jit(solution)/shard_map/ppermute | solution.py:20
  13.0 0.0 copy-done
  13.0 0.1 dynamic-slice_reduce_fusion
  13.2 0.0 collective-permute-done
  13.2 0.0 copy-done.4
  13.3 0.1 reshape.61
  13.5 0.2 fusion
  13.7 0.0 collective-permute-done.1
  13.8 3.5 %collective-permute-done.2 = bf16[432,128]{1,0:T(8,128)(2,1)S(1)} collective-permute-done((bf16[432,128]{1,0:T(8,128)(2,1)S(1)}, bf16[432,128]{1,0:T(8,128)(2,1)S(1)}, u32[]{:S(2)}, u32[]{:S(2)}) %collective-permute-start.2) | collective-permute-done | bytes 110624 | tf_op jit(solution)/shard_map/ppermute | solution.py:20
  17.3 0.9 broadcast_in_dim.6
  18.2 14.6 %all-to-all-start = ((bf16[16,35,2,128]{3,2,1,0:T(2,128)(2,1)}), bf16[16,35,2,128]{3,2,1,0:T(2,128)(2,1)S(1)}, u32[]{:S(2)}, u32[]{:S(2)}) async-start(bf16[16,35,2,128]{3,2,1,0:T(2,128)(2,1)} %broadcast_in_dim.6), calls=%async_computation | async-start | bytes 573440 | tf_op jit(solution)/shard_map/all_to_all | solution.py:29
  32.8 2.4 %collective-permute-start.5 = (bf16[1728,128]{1,0:T(8,128)(2,1)S(1)}, bf16[1728,128]{1,0:T(8,128)(2,1)S(1)}, u32[]{:S(2)}, u32[]{:S(2)}) collective-permute-start(bf16[1728,128]{1,0:T(8,128)(2,1)S(1)} %constant_dynamic-update-slice_fusion), channel_id=1, source_target_pairs={{0,64},{2,66},{64,0},{66,2},{1,65},{3,67},{65,1},{67,3},{4,68},{6,... | collective-permute-start | bytes 1327112 | tf_op jit(solution)/shard_map/ppermute | solution.py:341
  35.2 3.7 %collective-permute-start.4 = (bf16[1728,128]{1,0:T(8,128)(2,1)S(1)}, bf16[1728,128]{1,0:T(8,128)(2,1)S(1)}, u32[]{:S(2)}, u32[]{:S(2)}) collective-permute-start(bf16[1728,128]{1,0:T(8,128)(2,1)S(1)} %constant_dynamic-update-slice_fusion), channel_id=1, source_target_pairs={{0,66},{2,0},{64,2},{66,64},{1,67},{3,1},{65,3},{67,65},{4,70},{6,... | collective-permute-start | bytes 1327112 | tf_op jit(solution)/shard_map/ppermute | solution.py:341
  39.0 1.9 %collective-permute-start.3 = (bf16[1728,128]{1,0:T(8,128)(2,1)S(1)}, bf16[1728,128]{1,0:T(8,128)(2,1)S(1)}, u32[]{:S(2)}, u32[]{:S(2)}) collective-permute-start(bf16[1728,128]{1,0:T(8,128)(2,1)S(1)} %constant_dynamic-update-slice_fusion), channel_id=1, source_target_pairs={{0,2},{2,64},{64,66},{66,0},{1,3},{3,65},{65,67},{67,1},{4,6},{6,6... | collective-permute-start | bytes 1327112 | tf_op jit(solution)/shard_map/ppermute | solution.py:341
  40.9 4.9 %all-to-all-done = bf16[16,35,2,128]{3,2,1,0:T(2,128)(2,1)S(1)} async-done(((bf16[16,35,2,128]{3,2,1,0:T(2,128)(2,1)}), bf16[16,35,2,128]{3,2,1,0:T(2,128)(2,1)S(1)}, u32[]{:S(2)}, u32[]{:S(2)}) %all-to-all-start) | async-done | bytes 286752 | tf_op jit(solution)/shard_map/all_to_all | solution.py:29
  45.8 0.1 slice_bitcast_fusion
  45.9 0.1 copy.40
  46.0 1.2 %broadcast_in_dim.7 = bf16[4,1120,128]{2,1,0:T(8,128)(2,1)} broadcast(bf16[1120,128]{1,0:T(8,128)(2,1)S(1)} %pad_maximum_fusion.1), dimensions={1,2} | broadcast | bytes 1433600 | tf_op jit(solution)/shard_map/broadcast_in_dim | solution.py:30
  47.2 4.2 %all-to-all-start.1 = ((bf16[4,1120,128]{2,1,0:T(8,128)(2,1)}), bf16[4,1120,128]{2,1,0:T(8,128)(2,1)S(1)}, u32[]{:S(2)}, u32[]{:S(2)}) async-start(bf16[4,1120,128]{2,1,0:T(8,128)(2,1)} %broadcast_in_dim.7), calls=%async_computation.1 | async-start | bytes 2293760 | tf_op jit(solution)/shard_map/all_to_all | solution.py:29
  51.4 0.0 collective-permute-done.5
  51.4 0.0 copy-start.1
  51.4 2.7 %collective-permute-done.4 = bf16[1728,128]{1,0:T(8,128)(2,1)S(1)} collective-permute-done((bf16[1728,128]{1,0:T(8,128)(2,1)S(1)}, bf16[1728,128]{1,0:T(8,128)(2,1)S(1)}, u32[]{:S(2)}, u32[]{:S(2)}) %collective-permute-start.4) | collective-permute-done | bytes 442400 | tf_op jit(solution)/shard_map/ppermute | solution.py:341
  54.1 2.0 %collective-permute-done.3 = bf16[1728,128]{1,0:T(8,128)(2,1)S(1)} collective-permute-done((bf16[1728,128]{1,0:T(8,128)(2,1)S(1)}, bf16[1728,128]{1,0:T(8,128)(2,1)S(1)}, u32[]{:S(2)}, u32[]{:S(2)}) %collective-permute-start.3) | collective-permute-done | bytes 442400 | tf_op jit(solution)/shard_map/ppermute | solution.py:341
  56.2 0.0 copy-done.1
  56.2 0.0 copy-done.2
  56.2 0.8 copy-done.3
  57.0 1.5 %pad_maximum_fusion.own = bf16[4,1728,128]{2,1,0:T(8,128)(2,1)S(1)} fusion(bf16[1,1728,128]{2,1,0:T(8,128)(2,1)} %bitcast.61, bf16[1,1728,128]{2,1,0:T(8,128)(2,1)} %bitcast.62, bf16[1,1728,128]{2,1,0:T(8,128)(2,1)} %bitcast.63, bf16[1,1728,128]{2,1,0:T(8,128)(2,1)S(1)} %bitcast.59), kind=kLoop, calls=%fused_computation | loop fusion | flops 2654208 | bytes 3538944 | tf_op jit(solution)/shard_map/stack | solution.py:403
  58.5 5.2 %collective-permute-start.6 = (bf16[4,1728,128]{2,1,0:T(8,128)(2,1)S(1)}, bf16[4,1728,128]{2,1,0:T(8,128)(2,1)}, u32[]{:S(2)}, u32[]{:S(2)}) collective-permute-start(bf16[4,1728,128]{2,1,0:T(8,128)(2,1)S(1)} %pad_maximum_fusion.own), channel_id=1, source_target_pairs={{0,1},{1,0},{2,3},{3,2},{4,5},{5,4},{6,7},{7,6},{8,9},{9,8},{10,11... | collective-permute-start | bytes 5308424 | tf_op jit(solution)/shard_map/ppermute | solution.py:24
  63.6 0.0 all-to-all-done.1.own
  63.6 8.8 %collective-permute-start.7 = (bf16[4,1120,128]{2,1,0:T(8,128)(2,1)S(1)}, bf16[4,1120,128]{2,1,0:T(8,128)(2,1)S(1)}, u32[]{:S(2)}, u32[]{:S(2)}) collective-permute-start(bf16[4,1120,128]{2,1,0:T(8,128)(2,1)S(1)} %all-to-all-done.1.own), channel_id=1, source_target_pairs={{0,1},{1,0},{2,3},{3,2},{4,5},{5,4},{6,7},{7,6},{8,9},{9,8},{10,11... | collective-permute-start | bytes 3440648 | tf_op jit(solution)/shard_map/ppermute | solution.py:24
  72.4 0.1 pad_add_fusion.place
  72.5 0.0 collective-permute-done.6.other
  72.5 3.6 %shard_map.59 = (bf16[768,2304]{1,0:T(8,128)(2,1)S(1)}, bf16[1152,1536]{1,0:T(8,128)(2,1)S(1)}) custom-call(s32[3]{0:T(128)S(1)} %pad_add_fusion.place, bf16[4,1728,128]{2,1,0:T(8,128)(2,1)S(1)} %pad_maximum_fusion.own, bf16[4,1728,128]{2,1,0:T(8,128)(2,1)} %collective-permute-done.6.other), custom_call_target="tpu_custom_call" | custom-call | flops 1000000000 | bytes 8388608 | tf_op jit(solution)/shard_map/pallas_call | solution.py:279
  76.2 0.0 collective-permute-done.7.other
  76.2 7.1 %shard_map.60 = (bf16[1008,128]{1,0:T(8,128)(2,1)S(1)}, bf16[1008,128]{1,0:T(8,128)(2,1)S(1)}, bf16[1008,128]{1,0:T(8,128)(2,1)S(1)}, bf16[1008,128]{1,0:T(8,128)(2,1)S(1)}) custom-call(s32[3]{0:T(128)S(1)} %pad_add_fusion.place, bf16[768,2304]{1,0:T(8,128)(2,1)S(1)} %get-tuple-element.14.frame_rows, bf16[1152,1536]{1,0:T(8,128)(2,1)S(1)} %get-tuple-element.15.cot_rows, ...), custom_call_target="tpu_custom_call" | custom-call | flops 4000000000 | bytes 8388608 | tf_op jit(solution)/shard_map/pallas_call | solution.py:279
  83.3 2.4 %collective-permute-start.8 = (bf16[1008,128]{1,0:T(8,128)(2,1)S(1)}, bf16[1008,128]{1,0:T(8,128)(2,1)S(1)}, u32[]{:S(2)}, u32[]{:S(2)}) collective-permute-start(bf16[1008,128]{1,0:T(8,128)(2,1)S(1)} %get-tuple-element.19), channel_id=1, source_target_pairs={{0,64},{2,66},{64,0},{66,2},{1,65},{3,67},{65,1},{67,3},{4,68},{6,... | collective-permute-start | bytes 774152 | tf_op jit(solution)/shard_map/ppermute | solution.py:341
  85.8 3.7 %collective-permute-start.9 = (bf16[1008,128]{1,0:T(8,128)(2,1)S(1)}, bf16[1008,128]{1,0:T(8,128)(2,1)S(1)}, u32[]{:S(2)}, u32[]{:S(2)}) collective-permute-start(bf16[1008,128]{1,0:T(8,128)(2,1)S(1)} %get-tuple-element.20), channel_id=1, source_target_pairs={{0,66},{2,0},{64,2},{66,64},{1,67},{3,1},{65,3},{67,65},{4,70},{6,... | collective-permute-start | bytes 774152 | tf_op jit(solution)/shard_map/ppermute | solution.py:341
  89.5 1.9 %collective-permute-start.10 = (bf16[1008,128]{1,0:T(8,128)(2,1)S(1)}, bf16[1008,128]{1,0:T(8,128)(2,1)S(1)}, u32[]{:S(2)}, u32[]{:S(2)}) collective-permute-start(bf16[1008,128]{1,0:T(8,128)(2,1)S(1)} %get-tuple-element.21), channel_id=1, source_target_pairs={{0,2},{2,64},{64,66},{66,0},{1,3},{3,65},{65,67},{67,1},{4,6},{6,6... | collective-permute-start | bytes 774152 | tf_op jit(solution)/shard_map/ppermute | solution.py:341
  91.4 3.1 %collective-permute-done.8.refs_1_ = bf16[1008,128]{1,0:T(8,128)(2,1)S(1)} collective-permute-done((bf16[1008,128]{1,0:T(8,128)(2,1)S(1)}, bf16[1008,128]{1,0:T(8,128)(2,1)S(1)}, u32[]{:S(2)}, u32[]{:S(2)}) %collective-permute-start.8) | collective-permute-done | bytes 258080 | tf_op jit(solution)/shard_map/ppermute | solution.py:341
  94.6 3.3 %collective-permute-done.9.refs_2_ = bf16[1008,128]{1,0:T(8,128)(2,1)S(1)} collective-permute-done((bf16[1008,128]{1,0:T(8,128)(2,1)S(1)}, bf16[1008,128]{1,0:T(8,128)(2,1)S(1)}, u32[]{:S(2)}, u32[]{:S(2)}) %collective-permute-start.9) | collective-permute-done | bytes 258080 | tf_op jit(solution)/shard_map/ppermute | solution.py:341
  97.9 1.9 %collective-permute-done.10.refs_3_ = bf16[1008,128]{1,0:T(8,128)(2,1)S(1)} collective-permute-done((bf16[1008,128]{1,0:T(8,128)(2,1)S(1)}, bf16[1008,128]{1,0:T(8,128)(2,1)S(1)}, u32[]{:S(2)}, u32[]{:S(2)}) %collective-permute-start.10) | collective-permute-done | bytes 258080 | tf_op jit(solution)/shard_map/ppermute | solution.py:341
  99.8 0.8 shard_map.61
  (31 shorter events, 0.5 us)
Async XLA Ops:
  0.6 12.3 %copy-start = (bf16[10368,2]{0,1:T(2,128)(2,1)S(1)}, bf16[10368,2]{0,1:T(2,128)(2,1)}, u32[]{:S(2)}) copy-start(bf16[10368,2]{0,1:T(2,128)(2,1)} %param.5) | copy-start | bytes 124420
  0.6 12.6 %copy-start.4 = (bf16[6912,2]{0,1:T(2,128)(2,1)S(1)}, bf16[6912,2]{0,1:T(2,128)(2,1)}, u32[]{:S(2)}) copy-start(bf16[6912,2]{0,1:T(2,128)(2,1)} %param.6) | copy-start | bytes 82948
  0.7 12.6 %collective-permute-start = (bf16[6912,2]{0,1:T(2,128)(2,1)}, bf16[6912,2]{0,1:T(2,128)(2,1)S(1)}, u32[]{:S(2)}, u32[]{:S(2)}) collective-permute-start(bf16[6912,2]{0,1:T(2,128)(2,1)} %param.6), channel_id=1, source_target_pairs={{0,66},{66,0},{2,64},{64,2},{1,67},{67,1},{3,65},{65,3},{4,70},{70... | collective-permute-start | bytes 82952 | tf_op jit(solution)/shard_map/ppermute | solution.py:360
  7.0 6.7 %collective-permute-start.1 = (bf16[288,128]{1,0:T(8,128)(2,1)S(1)}, bf16[288,128]{1,0:T(8,128)(2,1)S(1)}, u32[]{:S(2)}, u32[]{:S(2)}) collective-permute-start(bf16[288,128]{1,0:T(8,128)(2,1)S(1)} %bitcast.70), channel_id=1, source_target_pairs={{0,4},{4,8},{8,12},{12,16},{16,20},{20,24},{24,28},{28,32},{32,36}... | collective-permute-start | bytes 221192 | tf_op jit(solution)/shard_map/ppermute | solution.py:20
  11.6 5.7 %collective-permute-start.2 = (bf16[432,128]{1,0:T(8,128)(2,1)S(1)}, bf16[432,128]{1,0:T(8,128)(2,1)S(1)}, u32[]{:S(2)}, u32[]{:S(2)}) collective-permute-start(bf16[432,128]{1,0:T(8,128)(2,1)S(1)} %get-tuple-element.24), channel_id=1, source_target_pairs={{4,0},{8,4},{12,8},{16,12},{20,16},{24,20},{28,24},{32,28},{36,32}... | collective-permute-start | bytes 331784 | tf_op jit(solution)/shard_map/ppermute | solution.py:20
  18.2 27.6 %all-to-all-start = ((bf16[16,35,2,128]{3,2,1,0:T(2,128)(2,1)}), bf16[16,35,2,128]{3,2,1,0:T(2,128)(2,1)S(1)}, u32[]{:S(2)}, u32[]{:S(2)}) async-start(bf16[16,35,2,128]{3,2,1,0:T(2,128)(2,1)} %broadcast_in_dim.6), calls=%async_computation | async-start | bytes 573440 | tf_op jit(solution)/shard_map/all_to_all | solution.py:29
  32.8 18.6 %collective-permute-start.5 = (bf16[1728,128]{1,0:T(8,128)(2,1)S(1)}, bf16[1728,128]{1,0:T(8,128)(2,1)S(1)}, u32[]{:S(2)}, u32[]{:S(2)}) collective-permute-start(bf16[1728,128]{1,0:T(8,128)(2,1)S(1)} %constant_dynamic-update-slice_fusion), channel_id=1, source_target_pairs={{0,64},{2,66},{64,0},{66,2},{1,65},{3,67},{65,1},{67,3},{4,68},{6,... | collective-permute-start | bytes 1327112 | tf_op jit(solution)/shard_map/ppermute | solution.py:341
  35.2 18.9 %collective-permute-start.4 = (bf16[1728,128]{1,0:T(8,128)(2,1)S(1)}, bf16[1728,128]{1,0:T(8,128)(2,1)S(1)}, u32[]{:S(2)}, u32[]{:S(2)}) collective-permute-start(bf16[1728,128]{1,0:T(8,128)(2,1)S(1)} %constant_dynamic-update-slice_fusion), channel_id=1, source_target_pairs={{0,66},{2,0},{64,2},{66,64},{1,67},{3,1},{65,3},{67,65},{4,70},{6,... | collective-permute-start | bytes 1327112 | tf_op jit(solution)/shard_map/ppermute | solution.py:341
  39.0 17.2 %collective-permute-start.3 = (bf16[1728,128]{1,0:T(8,128)(2,1)S(1)}, bf16[1728,128]{1,0:T(8,128)(2,1)S(1)}, u32[]{:S(2)}, u32[]{:S(2)}) collective-permute-start(bf16[1728,128]{1,0:T(8,128)(2,1)S(1)} %constant_dynamic-update-slice_fusion), channel_id=1, source_target_pairs={{0,2},{2,64},{64,66},{66,0},{1,3},{3,65},{65,67},{67,1},{4,6},{6,6... | collective-permute-start | bytes 1327112 | tf_op jit(solution)/shard_map/ppermute | solution.py:341
  47.2 16.4 %all-to-all-start.1 = ((bf16[4,1120,128]{2,1,0:T(8,128)(2,1)}), bf16[4,1120,128]{2,1,0:T(8,128)(2,1)S(1)}, u32[]{:S(2)}, u32[]{:S(2)}) async-start(bf16[4,1120,128]{2,1,0:T(8,128)(2,1)} %broadcast_in_dim.7), calls=%async_computation.1 | async-start | bytes 2293760 | tf_op jit(solution)/shard_map/all_to_all | solution.py:29
  51.4 4.8 %copy-start.1 = (bf16[1728,128]{1,0:T(8,128)(2,1)}, bf16[1728,128]{1,0:T(8,128)(2,1)S(1)}, u32[]{:S(2)}) copy-start(bf16[1728,128]{1,0:T(8,128)(2,1)S(1)} %collective-permute-done.5) | copy-start | bytes 1327108
  54.1 2.0 %copy-start.2 = (bf16[1728,128]{1,0:T(8,128)(2,1)}, bf16[1728,128]{1,0:T(8,128)(2,1)S(1)}, u32[]{:S(2)}) copy-start(bf16[1728,128]{1,0:T(8,128)(2,1)S(1)} %collective-permute-done.4) | copy-start | bytes 1327108
  56.2 0.8 copy-start.3
  58.5 14.1 %collective-permute-start.6 = (bf16[4,1728,128]{2,1,0:T(8,128)(2,1)S(1)}, bf16[4,1728,128]{2,1,0:T(8,128)(2,1)}, u32[]{:S(2)}, u32[]{:S(2)}) collective-permute-start(bf16[4,1728,128]{2,1,0:T(8,128)(2,1)S(1)} %pad_maximum_fusion.own), channel_id=1, source_target_pairs={{0,1},{1,0},{2,3},{3,2},{4,5},{5,4},{6,7},{7,6},{8,9},{9,8},{10,11... | collective-permute-start | bytes 5308424 | tf_op jit(solution)/shard_map/ppermute | solution.py:24
  63.6 12.5 %collective-permute-start.7 = (bf16[4,1120,128]{2,1,0:T(8,128)(2,1)S(1)}, bf16[4,1120,128]{2,1,0:T(8,128)(2,1)S(1)}, u32[]{:S(2)}, u32[]{:S(2)}) collective-permute-start(bf16[4,1120,128]{2,1,0:T(8,128)(2,1)S(1)} %all-to-all-done.1.own), channel_id=1, source_target_pairs={{0,1},{1,0},{2,3},{3,2},{4,5},{5,4},{6,7},{7,6},{8,9},{9,8},{10,11... | collective-permute-start | bytes 3440648 | tf_op jit(solution)/shard_map/ppermute | solution.py:24
  83.3 11.2 %collective-permute-start.8 = (bf16[1008,128]{1,0:T(8,128)(2,1)S(1)}, bf16[1008,128]{1,0:T(8,128)(2,1)S(1)}, u32[]{:S(2)}, u32[]{:S(2)}) collective-permute-start(bf16[1008,128]{1,0:T(8,128)(2,1)S(1)} %get-tuple-element.19), channel_id=1, source_target_pairs={{0,64},{2,66},{64,0},{66,2},{1,65},{3,67},{65,1},{67,3},{4,68},{6,... | collective-permute-start | bytes 774152 | tf_op jit(solution)/shard_map/ppermute | solution.py:341
  85.8 12.1 %collective-permute-start.9 = (bf16[1008,128]{1,0:T(8,128)(2,1)S(1)}, bf16[1008,128]{1,0:T(8,128)(2,1)S(1)}, u32[]{:S(2)}, u32[]{:S(2)}) collective-permute-start(bf16[1008,128]{1,0:T(8,128)(2,1)S(1)} %get-tuple-element.20), channel_id=1, source_target_pairs={{0,66},{2,0},{64,2},{66,64},{1,67},{3,1},{65,3},{67,65},{4,70},{6,... | collective-permute-start | bytes 774152 | tf_op jit(solution)/shard_map/ppermute | solution.py:341
  89.5 10.3 %collective-permute-start.10 = (bf16[1008,128]{1,0:T(8,128)(2,1)S(1)}, bf16[1008,128]{1,0:T(8,128)(2,1)S(1)}, u32[]{:S(2)}, u32[]{:S(2)}) collective-permute-start(bf16[1008,128]{1,0:T(8,128)(2,1)S(1)} %get-tuple-element.21), channel_id=1, source_target_pairs={{0,2},{2,64},{64,66},{66,0},{1,3},{3,65},{65,67},{67,1},{4,6},{6,6... | collective-permute-start | bytes 774152 | tf_op jit(solution)/shard_map/ppermute | solution.py:341

commit v11 on v10

--- a/solution.py
+++ b/solution.py
@@ -323,6 +323,22 @@
     return call(kernel, out, scratch, 4 * 10**9, 32, place, frame_rows, cot_rows, own, other)
 
 
+def stack_kernel(*refs):
+    for member, ref in enumerate(refs[:-1]):
+        refs[-1][member] = ref[...]
+
+
+def gathered(*blocks):
+    space = pl.BlockSpec(memory_space=pltpu.VMEM)
+    return pl.pallas_call(
+        stack_kernel,
+        out_shape=jax.ShapeDtypeStruct((len(blocks), *blocks[0].shape), blocks[0].dtype),
+        in_specs=[space] * len(blocks),
+        out_specs=space,
+        compiler_params=pltpu.CompilerParams(vmem_limit_bytes=8 * 2**20),
+    )(*blocks)
+
+
 def add_parts(parts, sizes):
     space = pl.BlockSpec(memory_space=pltpu.VMEM)
     return pl.pallas_call(
@@ -400,7 +416,7 @@
     block = jnp.concatenate((block, following, previous), axis=0)
     blocks = (block, ring(block, 1), ring(block, -1), ring(block, 2))
     planes, block = lax.optimization_barrier((planes, block))
-    blocks = jnp.stack(blocks)
+    blocks = gathered(block, *blocks[1:])
     others = swap(blocks)
     last = first + 3 * cot_size + frame_size
     cot_starts = [early + time * cot_size for time in range(3)]

time: 103 us -> 104 us (level); the launches traced: 101 us -> 103 us
  waiting for transfers between devices: 21.6 us -> 13.8 us
  starting transfers between devices: 59.1 us -> 66.4 us
  local copies, waits for them, and re-layouts: 5.42 us -> 10 us
  other arithmetic: 1.7 us -> 0.2 us
    unnamed x15 -> x21, local copies, waits for them, and re-layouts: 1.79 us -> 6.38 us
    ppermute x6, starting transfers between devices: 16.1 us -> 19.5 us  [ring(): return lax.ppermute(array, RING, [(i, (i + by) % 4) for i in range(4)])]
    all_to_all x2, starting transfers between devices: 18.8 us -> 21.9 us  [spread(): lax.all_to_all(jnp.broadcast_to(array, (count, *array.shape)), axis, 0, 0...]
    ppermute x2, waiting for transfers between devices: 3.55 us -> 0.57 us  [shift(): return lax.ppermute(array, axis, pairs)]
    ppermute x6, waiting for transfers between devices: 13.1 us -> 10.4 us  [ring(): return lax.ppermute(array, RING, [(i, (i + by) % 4) for i in range(4)])]
    all_to_all x2, waiting for transfers between devices: 4.86 us -> 2.84 us  [spread(): lax.all_to_all(jnp.broadcast_to(array, (count, *array.shape)), axis, 0, 0...]
    another operation x1 -> x0, other arithmetic: 1.5 us -> none  [shards(): blocks = jnp.stack(blocks)]
  transfers between devices with their start and end apart: 13 -> 13, of which waited for: 7 -> 5; matrix products, arithmetic and copies ran while one was open for 6% -> 4% of each run, Pallas kernels for 4% -> 4%
where the time goes in v11:
time: 104 us; the launch traced here: 103 us
  starting transfers between devices  66.4 us (64%)
  waiting for transfers between devices  13.8 us (13%)
  Pallas kernels  11.7 us (11%)
  local copies, waits for them, and re-layouts  10 us (10%)
  between operations  1.06 us (1%)
    all_to_all x2, starting transfers between devices, spread(): lax.all_to_all(jnp.broadcast_to(array, (count, *array.shape)), axis, 0, 0...  21.9 us
    ppermute x6, starting transfers between devices, ring(): return lax.ppermute(array, RING, [(i, (i + by) % 4) for i in range(4)])  19.5 us
    ppermute x2, starting transfers between devices, swap(): return lax.ppermute(array, 'core', [(0, 1), (1, 0)])  14.3 us
    pallas_call x2, Pallas kernels, call(): pl.pallas_call(kernel, out_shape=outs, in_specs=[pl.BlockSpec(memory_spac...  10.8 us
    ppermute x6, waiting for transfers between devices, ring(): return lax.ppermute(array, RING, [(i, (i + by) % 4) for i in range(4)])  10.4 us
    unnamed x21, local copies, waits for them, and re-layouts  6.38 us
    ppermute x2, starting transfers between devices, shift(): return lax.ppermute(array, axis, pairs)  5.47 us
    ppermute x1, starting transfers between devices, shards(): mix_other = lax.ppermute(mix_kernel, RING, [(0, 3), (3, 0), (1, 2), (2, 1)])  5.35 us
  transfers between devices with their start and end apart: 13, of which 5 were waited for; matrix products, arithmetic and copies ran while one was open for 4% of the time, Pallas kernels for 4%

profile of v11, /device:TPU:1, one launch (start us, length us, event | category | flops | bytes accessed | tf_op | source)
XLA Modules:
  0.0 103.4 jit_solution(15236184263441637178)
XLA Ops:
  0.6 0.0 copy-start
  0.7 5.3 %collective-permute-start = (bf16[6912,2]{0,1:T(2,128)(2,1)}, bf16[6912,2]{0,1:T(2,128)(2,1)S(1)}, u32[]{:S(2)}, u32[]{:S(2)}) collective-permute-start(bf16[6912,2]{0,1:T(2,128)(2,1)} %param.6), channel_id=1, source_target_pairs={{0,66},{66,0},{2,64},{64,2},{1,67},{67,1},{3,65},{65,3},{4,70},{70... | collective-permute-start | bytes 82952 | tf_op jit(solution)/shard_map/ppermute | solution.py:376
  6.0 0.9 slice_bitcast_fusion.1
  7.0 0.9 reshape.59
  8.0 1.3 %collective-permute-start.2 = (bf16[432,128]{1,0:T(8,128)(2,1)S(1)}, bf16[432,128]{1,0:T(8,128)(2,1)S(1)}, u32[]{:S(2)}, u32[]{:S(2)}) collective-permute-start(bf16[432,128]{1,0:T(8,128)(2,1)S(1)} %get-tuple-element.27), channel_id=1, source_target_pairs={{4,0},{8,4},{12,8},{16,12},{20,16},{24,20},{28,24},{32,28},{36,32}... | collective-permute-start | bytes 331784 | tf_op jit(solution)/shard_map/ppermute | solution.py:20
  9.4 4.2 %collective-permute-start.1 = (bf16[288,128]{1,0:T(8,128)(2,1)S(1)}, bf16[288,128]{1,0:T(8,128)(2,1)S(1)}, u32[]{:S(2)}, u32[]{:S(2)}) collective-permute-start(bf16[288,128]{1,0:T(8,128)(2,1)S(1)} %bitcast.62), channel_id=1, source_target_pairs={{0,4},{4,8},{8,12},{12,16},{16,20},{20,24},{24,28},{28,32},{32,36}... | collective-permute-start | bytes 221192 | tf_op jit(solution)/shard_map/ppermute | solution.py:20
  13.6 0.1 dynamic-slice_reduce_fusion
  13.8 0.0 collective-permute-done
  13.8 0.0 copy-done.7
  13.9 0.1 reshape.55
  14.1 0.2 fusion
  14.4 0.6 collective-permute-done.1
  14.9 0.0 collective-permute-done.2
  14.9 0.9 broadcast_in_dim.6
  15.8 16.3 %all-to-all-start = ((bf16[16,35,2,128]{3,2,1,0:T(2,128)(2,1)}), bf16[16,35,2,128]{3,2,1,0:T(2,128)(2,1)S(1)}, u32[]{:S(2)}, u32[]{:S(2)}) async-start(bf16[16,35,2,128]{3,2,1,0:T(2,128)(2,1)} %broadcast_in_dim.6), calls=%async_computation | async-start | bytes 573440 | tf_op jit(solution)/shard_map/all_to_all | solution.py:29
  32.1 1.9 %collective-permute-start.3 = (bf16[1728,128]{1,0:T(8,128)(2,1)S(1)}, bf16[1728,128]{1,0:T(8,128)(2,1)S(1)}, u32[]{:S(2)}, u32[]{:S(2)}) collective-permute-start(bf16[1728,128]{1,0:T(8,128)(2,1)S(1)} %constant_dynamic-update-slice_fusion.refs_0_), channel_id=1, source_target_pairs={{0,2},{2,64},{64,66},{66,0},{1,3},{3,65},{65,67},{67,1},{4,6},{6,6... | collective-permute-start | bytes 1327112 | tf_op jit(solution)/shard_map/ppermute | solution.py:357
  34.1 4.6 %collective-permute-start.4 = (bf16[1728,128]{1,0:T(8,128)(2,1)S(1)}, bf16[1728,128]{1,0:T(8,128)(2,1)S(1)}, u32[]{:S(2)}, u32[]{:S(2)}) collective-permute-start(bf16[1728,128]{1,0:T(8,128)(2,1)S(1)} %constant_dynamic-update-slice_fusion.refs_0_), channel_id=1, source_target_pairs={{0,66},{2,0},{64,2},{66,64},{1,67},{3,1},{65,3},{67,65},{4,70},{6,... | collective-permute-start | bytes 1327112 | tf_op jit(solution)/shard_map/ppermute | solution.py:357
  38.7 3.6 %collective-permute-start.5 = (bf16[1728,128]{1,0:T(8,128)(2,1)S(1)}, bf16[1728,128]{1,0:T(8,128)(2,1)S(1)}, u32[]{:S(2)}, u32[]{:S(2)}) collective-permute-start(bf16[1728,128]{1,0:T(8,128)(2,1)S(1)} %constant_dynamic-update-slice_fusion.refs_0_), channel_id=1, source_target_pairs={{0,64},{2,66},{64,0},{66,2},{1,65},{3,67},{65,1},{67,3},{4,68},{6,... | collective-permute-start | bytes 1327112 | tf_op jit(solution)/shard_map/ppermute | solution.py:357
  42.3 2.8 %all-to-all-done = bf16[16,35,2,128]{3,2,1,0:T(2,128)(2,1)S(1)} async-done(((bf16[16,35,2,128]{3,2,1,0:T(2,128)(2,1)}), bf16[16,35,2,128]{3,2,1,0:T(2,128)(2,1)S(1)}, u32[]{:S(2)}, u32[]{:S(2)}) %all-to-all-start) | async-done | bytes 286752 | tf_op jit(solution)/shard_map/all_to_all | solution.py:29
  45.1 0.1 slice_bitcast_fusion
  45.3 0.1 copy.40
  45.4 1.2 %broadcast_in_dim.7 = bf16[4,1120,128]{2,1,0:T(8,128)(2,1)} broadcast(bf16[1120,128]{1,0:T(8,128)(2,1)S(1)} %pad_maximum_fusion), dimensions={1,2} | broadcast | bytes 1433600 | tf_op jit(solution)/shard_map/broadcast_in_dim | solution.py:30
  46.5 5.6 %all-to-all-start.1 = ((bf16[4,1120,128]{2,1,0:T(8,128)(2,1)}), bf16[4,1120,128]{2,1,0:T(8,128)(2,1)S(1)}, u32[]{:S(2)}, u32[]{:S(2)}) async-start(bf16[4,1120,128]{2,1,0:T(8,128)(2,1)} %broadcast_in_dim.7), calls=%async_computation.1 | async-start | bytes 2293760 | tf_op jit(solution)/shard_map/all_to_all | solution.py:29
  52.1 0.0 collective-permute-done.3.refs_1_
  52.1 0.8 copy-done.1
  52.9 0.0 collective-permute-done.4.refs_2_
  52.9 0.8 copy-done.3
  53.7 1.1 %collective-permute-done.5.refs_3_ = bf16[1728,128]{1,0:T(8,128)(2,1)S(1)} collective-permute-done((bf16[1728,128]{1,0:T(8,128)(2,1)S(1)}, bf16[1728,128]{1,0:T(8,128)(2,1)S(1)}, u32[]{:S(2)}, u32[]{:S(2)}) %collective-permute-start.5) | collective-permute-done | bytes 442400 | tf_op jit(solution)/shard_map/ppermute | solution.py:357
  54.8 0.8 copy-done.5
  55.6 1.0 copy-done.2
  56.6 1.0 copy-done.4
  57.6 1.0 copy-done.6
  58.6 0.1 shard_map.59.own
  58.8 8.4 %collective-permute-start.6 = (bf16[4,1728,128]{2,1,0:T(8,128)(2,1)S(1)}, bf16[4,1728,128]{2,1,0:T(8,128)(2,1)}, u32[]{:S(2)}, u32[]{:S(2)}) collective-permute-start(bf16[4,1728,128]{2,1,0:T(8,128)(2,1)S(1)} %shard_map.59.own), channel_id=1, source_target_pairs={{0,1},{1,0},{2,3},{3,2},{4,5},{5,4},{6,7},{7,6},{8,9},{9,8},{10,11... | collective-permute-start | bytes 5308424 | tf_op jit(solution)/shard_map/ppermute | solution.py:24
  67.2 0.0 all-to-all-done.1.own
  67.2 5.9 %collective-permute-start.7 = (bf16[4,1120,128]{2,1,0:T(8,128)(2,1)S(1)}, bf16[4,1120,128]{2,1,0:T(8,128)(2,1)S(1)}, u32[]{:S(2)}, u32[]{:S(2)}) collective-permute-start(bf16[4,1120,128]{2,1,0:T(8,128)(2,1)S(1)} %all-to-all-done.1.own), channel_id=1, source_target_pairs={{0,1},{1,0},{2,3},{3,2},{4,5},{5,4},{6,7},{7,6},{8,9},{9,8},{10,11... | collective-permute-start | bytes 3440648 | tf_op jit(solution)/shard_map/ppermute | solution.py:24
  73.0 0.1 pad_add_fusion.place
  73.1 0.0 collective-permute-done.6.other
  73.1 3.6 %shard_map.60 = (bf16[768,2304]{1,0:T(8,128)(2,1)S(1)}, bf16[1152,1536]{1,0:T(8,128)(2,1)S(1)}) custom-call(s32[3]{0:T(128)S(1)} %pad_add_fusion.place, bf16[4,1728,128]{2,1,0:T(8,128)(2,1)S(1)} %shard_map.59.own, bf16[4,1728,128]{2,1,0:T(8,128)(2,1)} %collective-permute-done.6.other), custom_call_target="tpu_custom_call" | custom-call | flops 1000000000 | bytes 8388608 | tf_op jit(solution)/shard_map/pallas_call | solution.py:279
  76.8 0.0 collective-permute-done.7.other
  76.8 7.1 %shard_map.61 = (bf16[1008,128]{1,0:T(8,128)(2,1)S(1)}, bf16[1008,128]{1,0:T(8,128)(2,1)S(1)}, bf16[1008,128]{1,0:T(8,128)(2,1)S(1)}, bf16[1008,128]{1,0:T(8,128)(2,1)S(1)}) custom-call(s32[3]{0:T(128)S(1)} %pad_add_fusion.place, bf16[768,2304]{1,0:T(8,128)(2,1)S(1)} %get-tuple-element.17.frame_rows, bf16[1152,1536]{1,0:T(8,128)(2,1)S(1)} %get-tuple-element.18.cot_rows, ...), custom_call_target="tpu_custom_call" | custom-call | flops 4000000000 | bytes 8388608 | tf_op jit(solution)/shard_map/pallas_call | solution.py:279
  83.9 2.2 %collective-permute-start.10 = (bf16[1008,128]{1,0:T(8,128)(2,1)S(1)}, bf16[1008,128]{1,0:T(8,128)(2,1)S(1)}, u32[]{:S(2)}, u32[]{:S(2)}) collective-permute-start(bf16[1008,128]{1,0:T(8,128)(2,1)S(1)} %get-tuple-element.23), channel_id=1, source_target_pairs={{0,2},{2,64},{64,66},{66,0},{1,3},{3,65},{65,67},{67,1},{4,6},{6,6... | collective-permute-start | bytes 774152 | tf_op jit(solution)/shard_map/ppermute | solution.py:357
  86.1 3.7 %collective-permute-start.8 = (bf16[1008,128]{1,0:T(8,128)(2,1)S(1)}, bf16[1008,128]{1,0:T(8,128)(2,1)S(1)}, u32[]{:S(2)}, u32[]{:S(2)}) collective-permute-start(bf16[1008,128]{1,0:T(8,128)(2,1)S(1)} %get-tuple-element.21), channel_id=1, source_target_pairs={{0,64},{2,66},{64,0},{66,2},{1,65},{3,67},{65,1},{67,3},{4,68},{6,... | collective-permute-start | bytes 774152 | tf_op jit(solution)/shard_map/ppermute | solution.py:357
  89.9 3.4 %collective-permute-start.9 = (bf16[1008,128]{1,0:T(8,128)(2,1)S(1)}, bf16[1008,128]{1,0:T(8,128)(2,1)S(1)}, u32[]{:S(2)}, u32[]{:S(2)}) collective-permute-start(bf16[1008,128]{1,0:T(8,128)(2,1)S(1)} %get-tuple-element.22), channel_id=1, source_target_pairs={{0,66},{2,0},{64,2},{66,64},{1,67},{3,1},{65,3},{67,65},{4,70},{6,... | collective-permute-start | bytes 774152 | tf_op jit(solution)/shard_map/ppermute | solution.py:357
  93.3 7.1 %collective-permute-done.10.refs_3_ = bf16[1008,128]{1,0:T(8,128)(2,1)S(1)} collective-permute-done((bf16[1008,128]{1,0:T(8,128)(2,1)S(1)}, bf16[1008,128]{1,0:T(8,128)(2,1)S(1)}, u32[]{:S(2)}, u32[]{:S(2)}) %collective-permute-start.10) | collective-permute-done | bytes 258080 | tf_op jit(solution)/shard_map/ppermute | solution.py:357
  100.4 0.0 collective-permute-done.8.refs_1_
  100.4 2.2 %collective-permute-done.9.refs_2_ = bf16[1008,128]{1,0:T(8,128)(2,1)S(1)} collective-permute-done((bf16[1008,128]{1,0:T(8,128)(2,1)S(1)}, bf16[1008,128]{1,0:T(8,128)(2,1)S(1)}, u32[]{:S(2)}, u32[]{:S(2)}) %collective-permute-start.9) | collective-permute-done | bytes 258080 | tf_op jit(solution)/shard_map/ppermute | solution.py:357
  102.6 0.8 shard_map.62
  (37 shorter events, 0.5 us)
Async XLA Ops:
  0.6 13.0 %copy-start = (bf16[10368,2]{0,1:T(2,128)(2,1)S(1)}, bf16[10368,2]{0,1:T(2,128)(2,1)}, u32[]{:S(2)}) copy-start(bf16[10368,2]{0,1:T(2,128)(2,1)} %param.5) | copy-start | bytes 124420
  0.6 13.2 %copy-start.7 = (bf16[6912,2]{0,1:T(2,128)(2,1)S(1)}, bf16[6912,2]{0,1:T(2,128)(2,1)}, u32[]{:S(2)}) copy-start(bf16[6912,2]{0,1:T(2,128)(2,1)} %param.6) | copy-start | bytes 82948
  0.7 13.2 %collective-permute-start = (bf16[6912,2]{0,1:T(2,128)(2,1)}, bf16[6912,2]{0,1:T(2,128)(2,1)S(1)}, u32[]{:S(2)}, u32[]{:S(2)}) collective-permute-start(bf16[6912,2]{0,1:T(2,128)(2,1)} %param.6), channel_id=1, source_target_pairs={{0,66},{66,0},{2,64},{64,2},{1,67},{67,1},{3,65},{65,3},{4,70},{70... | collective-permute-start | bytes 82952 | tf_op jit(solution)/shard_map/ppermute | solution.py:376
  8.0 6.9 %collective-permute-start.2 = (bf16[432,128]{1,0:T(8,128)(2,1)S(1)}, bf16[432,128]{1,0:T(8,128)(2,1)S(1)}, u32[]{:S(2)}, u32[]{:S(2)}) collective-permute-start(bf16[432,128]{1,0:T(8,128)(2,1)S(1)} %get-tuple-element.27), channel_id=1, source_target_pairs={{4,0},{8,4},{12,8},{16,12},{20,16},{24,20},{28,24},{32,28},{36,32}... | collective-permute-start | bytes 331784 | tf_op jit(solution)/shard_map/ppermute | solution.py:20
  9.4 5.6 %collective-permute-start.1 = (bf16[288,128]{1,0:T(8,128)(2,1)S(1)}, bf16[288,128]{1,0:T(8,128)(2,1)S(1)}, u32[]{:S(2)}, u32[]{:S(2)}) collective-permute-start(bf16[288,128]{1,0:T(8,128)(2,1)S(1)} %bitcast.62), channel_id=1, source_target_pairs={{0,4},{4,8},{8,12},{12,16},{16,20},{20,24},{24,28},{28,32},{32,36}... | collective-permute-start | bytes 221192 | tf_op jit(solution)/shard_map/ppermute | solution.py:20
  15.8 29.3 %all-to-all-start = ((bf16[16,35,2,128]{3,2,1,0:T(2,128)(2,1)}), bf16[16,35,2,128]{3,2,1,0:T(2,128)(2,1)S(1)}, u32[]{:S(2)}, u32[]{:S(2)}) async-start(bf16[16,35,2,128]{3,2,1,0:T(2,128)(2,1)} %broadcast_in_dim.6), calls=%async_computation | async-start | bytes 573440 | tf_op jit(solution)/shard_map/all_to_all | solution.py:29
  32.1 20.0 %collective-permute-start.3 = (bf16[1728,128]{1,0:T(8,128)(2,1)S(1)}, bf16[1728,128]{1,0:T(8,128)(2,1)S(1)}, u32[]{:S(2)}, u32[]{:S(2)}) collective-permute-start(bf16[1728,128]{1,0:T(8,128)(2,1)S(1)} %constant_dynamic-update-slice_fusion.refs_0_), channel_id=1, source_target_pairs={{0,2},{2,64},{64,66},{66,0},{1,3},{3,65},{65,67},{67,1},{4,6},{6,6... | collective-permute-start | bytes 1327112 | tf_op jit(solution)/shard_map/ppermute | solution.py:357
  34.1 18.8 %collective-permute-start.4 = (bf16[1728,128]{1,0:T(8,128)(2,1)S(1)}, bf16[1728,128]{1,0:T(8,128)(2,1)S(1)}, u32[]{:S(2)}, u32[]{:S(2)}) collective-permute-start(bf16[1728,128]{1,0:T(8,128)(2,1)S(1)} %constant_dynamic-update-slice_fusion.refs_0_), channel_id=1, source_target_pairs={{0,66},{2,0},{64,2},{66,64},{1,67},{3,1},{65,3},{67,65},{4,70},{6,... | collective-permute-start | bytes 1327112 | tf_op jit(solution)/shard_map/ppermute | solution.py:357
  38.7 16.1 %collective-permute-start.5 = (bf16[1728,128]{1,0:T(8,128)(2,1)S(1)}, bf16[1728,128]{1,0:T(8,128)(2,1)S(1)}, u32[]{:S(2)}, u32[]{:S(2)}) collective-permute-start(bf16[1728,128]{1,0:T(8,128)(2,1)S(1)} %constant_dynamic-update-slice_fusion.refs_0_), channel_id=1, source_target_pairs={{0,64},{2,66},{64,0},{66,2},{1,65},{3,67},{65,1},{67,3},{4,68},{6,... | collective-permute-start | bytes 1327112 | tf_op jit(solution)/shard_map/ppermute | solution.py:357
  46.5 20.6 %all-to-all-start.1 = ((bf16[4,1120,128]{2,1,0:T(8,128)(2,1)}), bf16[4,1120,128]{2,1,0:T(8,128)(2,1)S(1)}, u32[]{:S(2)}, u32[]{:S(2)}) async-start(bf16[4,1120,128]{2,1,0:T(8,128)(2,1)} %broadcast_in_dim.7), calls=%async_computation.1 | async-start | bytes 2293760 | tf_op jit(solution)/shard_map/all_to_all | solution.py:29
  52.1 0.8 copy-start.1
  52.9 0.8 copy-start.3
  54.8 0.8 copy-start.5
  55.6 1.0 copy-start.2
  56.6 1.0 copy-start.4
  57.6 1.0 copy-start.6
  58.8 14.4 %collective-permute-start.6 = (bf16[4,1728,128]{2,1,0:T(8,128)(2,1)S(1)}, bf16[4,1728,128]{2,1,0:T(8,128)(2,1)}, u32[]{:S(2)}, u32[]{:S(2)}) collective-permute-start(bf16[4,1728,128]{2,1,0:T(8,128)(2,1)S(1)} %shard_map.59.own), channel_id=1, source_target_pairs={{0,1},{1,0},{2,3},{3,2},{4,5},{5,4},{6,7},{7,6},{8,9},{9,8},{10,11... | collective-permute-start | bytes 5308424 | tf_op jit(solution)/shard_map/ppermute | solution.py:24
  67.2 9.6 %collective-permute-start.7 = (bf16[4,1120,128]{2,1,0:T(8,128)(2,1)S(1)}, bf16[4,1120,128]{2,1,0:T(8,128)(2,1)S(1)}, u32[]{:S(2)}, u32[]{:S(2)}) collective-permute-start(bf16[4,1120,128]{2,1,0:T(8,128)(2,1)S(1)} %all-to-all-done.1.own), channel_id=1, source_target_pairs={{0,1},{1,0},{2,3},{3,2},{4,5},{5,4},{6,7},{7,6},{8,9},{9,8},{10,11... | collective-permute-start | bytes 3440648 | tf_op jit(solution)/shard_map/ppermute | solution.py:24
  83.9 16.5 %collective-permute-start.10 = (bf16[1008,128]{1,0:T(8,128)(2,1)S(1)}, bf16[1008,128]{1,0:T(8,128)(2,1)S(1)}, u32[]{:S(2)}, u32[]{:S(2)}) collective-permute-start(bf16[1008,128]{1,0:T(8,128)(2,1)S(1)} %get-tuple-element.23), channel_id=1, source_target_pairs={{0,2},{2,64},{64,66},{66,0},{1,3},{3,65},{65,67},{67,1},{4,6},{6,6... | collective-permute-start | bytes 774152 | tf_op jit(solution)/shard_map/ppermute | solution.py:357
  86.1 14.3 %collective-permute-start.8 = (bf16[1008,128]{1,0:T(8,128)(2,1)S(1)}, bf16[1008,128]{1,0:T(8,128)(2,1)S(1)}, u32[]{:S(2)}, u32[]{:S(2)}) collective-permute-start(bf16[1008,128]{1,0:T(8,128)(2,1)S(1)} %get-tuple-element.21), channel_id=1, source_target_pairs={{0,64},{2,66},{64,0},{66,2},{1,65},{3,67},{65,1},{67,3},{4,68},{6,... | collective-permute-start | bytes 774152 | tf_op jit(solution)/shard_map/ppermute | solution.py:357
  89.9 12.8 %collective-permute-start.9 = (bf16[1008,128]{1,0:T(8,128)(2,1)S(1)}, bf16[1008,128]{1,0:T(8,128)(2,1)S(1)}, u32[]{:S(2)}, u32[]{:S(2)}) collective-permute-start(bf16[1008,128]{1,0:T(8,128)(2,1)S(1)} %get-tuple-element.22), channel_id=1, source_target_pairs={{0,66},{2,0},{64,2},{66,64},{1,67},{3,1},{65,3},{67,65},{4,70},{6,... | collective-permute-start | bytes 774152 | tf_op jit(solution)/shard_map/ppermute | solution.py:357
